TPU v7x, 256 devices: a whole 4x4x8 slice. The times are simulated.
256 devices in a mesh: seq: 64 (over x, z, core), head: 4 (over y).
Axes of the slice: x: 4, y: 4, z: 8, core: 2. Of those that a mesh axis runs over, the one named last changes fastest.
Arguments:
- tokens: bfloat16 [65536, 2048], P('seq', 'head'), may hold values from -6 to 6
- w_qkv: bfloat16 [2048, 6144], P(None, 'head'), may hold values from -1 to 1
- item_at: int32 [4, 2048], P('head'), may hold values from 0 to 2047, as said below
- rand_cols: int32 [16, 512, 4], P('head'), may hold values from 0 to 511, as said below
- rand_used: int32 [16, 512], P('head'), may hold values from 0 to 4, as said below
Outputs:
- attended: bfloat16 [4, 2048, 128, 128], P('head', 'seq')
Inputs may be any that keep to these rules, and one draw needn't show every extreme that they name: In head group g, item e * 512 + r stands for head g * 4 + e at block row r, and every item appears exactly once in item_at[g]. Positions j * 32 to (j + 1) * 32 - 1 hold the items placed at device j of seq. Of the items whose block rows lie on one device of seq, at most 1 of one group are placed at any one device, and exactly 1 at some. `rand_cols`: take all 128 candidates (used or not) of the items placed at one device in one head group, or of the items of one group whose block rows lie on one device: at most 2 of them lie in the block rows of any one device of seq, and exactly 2 in some. A candidate may equal a window block or block 0. `rand_used`: in each head group the counts of the 32 items placed at one device sum to exactly 64; the sums over the items whose block rows lie on one device vary.
All inputs are finite; a program needn't handle non-finite values.
Results may differ from a plain program's by a relative error of at most 0.019.
Values may be sent and summed in bfloat16 or wider, within the bound.
No kernel may reach another device: no remote copies, remote signals or barrier semaphores. Data moves between devices by JAX's collectives and lax.ppermute only.
A program may use at most 128 MiB of HBM per device.

v0:
```python
import math

import jax
import jax.numpy as jnp
from jax import lax
from jax.experimental import pallas as pl
from jax.experimental.pallas import tpu as pltpu
from jax.sharding import PartitionSpec as P

NEG = -1e30
BF = jnp.bfloat16
F32 = jnp.float32
VMEM_BYTES = 48 << 20


def dot(a, b):
    return jnp.dot(a, b, preferred_element_type=F32)


def dot_t(a, b):
    return lax.dot_general(a, b, (((1,), (1,)), ((), ())), preferred_element_type=F32)


def params():
    return pltpu.CompilerParams(vmem_limit_bytes=VMEM_BYTES)


def pack_tiles(table, dests, pair, shares, rows, heads, blk, hd, name):
    width = heads * hd
    ends = [(k, i) for k, share in enumerate(shares) for i in range(share)]

    def kernel(table_ref, dest_ref, pair_ref, *refs):
        outs = refs[: len(shares)]
        tiles, sems = refs[len(shares) :]

        def copy(n, t):
            k, i = ends[n]
            tile = table_ref[2 * dest_ref[n] + t]
            return pltpu.make_async_copy(tiles.at[tile], outs[k].at[i, t], sems.at[2 * n + t])

        for e in range(heads):
            for r in range(rows):
                at = slice(r * blk, (r + 1) * blk)
                tiles[e * rows + r, :, :hd] = pair_ref[at, e * hd : (e + 1) * hd]
                tiles[e * rows + r, :, hd:] = pair_ref[at, width + e * hd : width + (e + 1) * hd].T
        for n in range(len(ends)):
            for t in range(2):
                copy(n, t).start()
        for n in range(len(ends)):
            for t in range(2):
                copy(n, t).wait()

    anywhere = pl.BlockSpec(memory_space=pl.ANY)
    return pl.pallas_call(
        kernel,
        out_shape=[jax.ShapeDtypeStruct((share, 2, blk, 2 * hd), BF) for share in shares],
        grid_spec=pltpu.PrefetchScalarGridSpec(
            num_scalar_prefetch=2,
            grid=(1,),
            in_specs=[pl.BlockSpec(memory_space=pltpu.VMEM)],
            out_specs=[anywhere] * len(shares),
            scratch_shapes=[
                pltpu.VMEM((rows * heads, blk, 2 * hd), BF),
                pltpu.SemaphoreType.DMA((2 * len(ends),)),
            ],
        ),
        compiler_params=params(),
        name=name,
    )(table, dests, pair)


def merge_parts(parts, places, name):
    count = sum(len(at) for at in places)
    rest = parts[0].shape[1:]

    def kernel(*refs):
        out_ref, sems = refs[len(parts) :]
        copies = []
        for ref, at in zip(refs, places):
            for i, (g, a) in enumerate(at):
                copies.append(
                    pltpu.make_async_copy(ref.at[i], out_ref.at[g, a], sems.at[len(copies)])
                )
        for copy in copies:
            copy.start()
        for copy in copies:
            copy.wait()

    return pl.pallas_call(
        kernel,
        out_shape=jax.ShapeDtypeStruct((count // 4, 4, *rest), parts[0].dtype),
        in_specs=[pl.BlockSpec(memory_space=pltpu.VMEM)] * len(parts),
        out_specs=pl.BlockSpec(memory_space=pltpu.HBM),
        scratch_shapes=[pltpu.SemaphoreType.DMA((count,))],
        compiler_params=params(),
        name=name,
    )(*parts)


def take_tiles(index, tiles):
    count = index.shape[0]

    def kernel(index_ref, in_ref, out_ref, sems):
        def copy(i):
            return pltpu.make_async_copy(in_ref.at[index_ref[i]], out_ref.at[i], sems.at[i])

        for i in range(count):
            copy(i).start()
        for i in range(count):
            copy(i).wait()

    return pl.pallas_call(
        kernel,
        out_shape=jax.ShapeDtypeStruct((count, *tiles.shape[1:]), tiles.dtype),
        grid_spec=pltpu.PrefetchScalarGridSpec(
            num_scalar_prefetch=1,
            grid=(1,),
            in_specs=[pl.BlockSpec(memory_space=pltpu.VMEM)],
            out_specs=pl.BlockSpec(memory_space=pl.ANY),
            scratch_shapes=[pltpu.SemaphoreType.DMA((count,))],
        ),
        compiler_params=params(),
        name="take_tiles",
    )(index, tiles)


def near_attend(edges, query, around, first, rows, heads, blk, hd, factor):
    width = heads * hd

    def kernel(edge_ref, q_ref, kv_ref, first_ref, acc_ref, stat_ref):
        r = pl.program_id(0)
        window = pl.ds(pl.multiple_of(r * blk, blk), 3 * blk)
        key = lax.broadcasted_iota(jnp.int32, (3 * blk, blk), 0)
        low = jnp.where((r == 0) & (edge_ref[0] == 1), blk, 0)
        high = jnp.where((r == rows - 1) & (edge_ref[1] == 1), 2 * blk, 3 * blk)
        usable = (key >= low) & (key < high)
        row = lax.broadcasted_iota(jnp.int32, (8, blk), 0)
        for e in range(heads):
            keys = slice(e * hd, (e + 1) * hd)
            values = slice(width + e * hd, width + (e + 1) * hd)
            q = q_ref[:, keys]
            near = jnp.where(usable, dot_t(kv_ref[window, keys], q) * factor, NEG)
            glob = dot_t(first_ref[:, keys], q) * factor
            top = jnp.maximum(
                jnp.max(near, axis=0, keepdims=True), jnp.max(glob, axis=0, keepdims=True)
            )
            near = jnp.exp2(near - top)
            glob = jnp.exp2(glob - top)
            total = jnp.sum(near, axis=0, keepdims=True) + jnp.sum(glob, axis=0, keepdims=True)
            acc_ref[e] = dot(kv_ref[window, values].T, near.astype(BF)) + dot(
                first_ref[:, values].T, glob.astype(BF)
            )
            stat_ref[e] = jnp.where(row == 0, top, total)

    return pl.pallas_call(
        kernel,
        out_shape=(
            jax.ShapeDtypeStruct((rows * heads, hd, blk), F32),
            jax.ShapeDtypeStruct((rows * heads, 8, blk), F32),
        ),
        grid_spec=pltpu.PrefetchScalarGridSpec(
            num_scalar_prefetch=1,
            grid=(rows,),
            in_specs=[
                pl.BlockSpec((blk, width), lambda r, s: (r, 0)),
                pl.BlockSpec(around.shape, lambda r, s: (0, 0)),
                pl.BlockSpec(first.shape, lambda r, s: (0, 0)),
            ],
            out_specs=(
                pl.BlockSpec((heads, hd, blk), lambda r, s: (r, 0, 0)),
                pl.BlockSpec((heads, 8, blk), lambda r, s: (r, 0, 0)),
            ),
        ),
        compiler_params=params(),
        name="near_attend",
    )(edges, query, around, first)


def rand_attend(slot, count, target, query, tiles, acc, stat, rows, heads, blk, hd, rand, peers, factor):
    items = rows * heads
    slots = items * rand
    share = slots // len(tiles)

    def kernel(slot_ref, count_ref, target_ref, q_ref, acc_ref, stat_ref, *refs):
        out_ref, buffer, done, in_sems, out_sems = refs[len(tiles) :]
        copies = [
            pltpu.make_async_copy(refs[n], buffer.at[pl.ds(n * share, share)], in_sems.at[n])
            for n in range(len(tiles))
        ]

        def deliver(i):
            return pltpu.make_async_copy(done.at[i], out_ref.at[target_ref[i]], out_sems.at[i])

        for copy in copies:
            copy.start()
        key = lax.broadcasted_iota(jnp.int32, (rand * blk, blk), 0)

        def step(r, carry):
            first = r * heads
            at = pl.ds(pl.multiple_of(r * blk, blk), blk)
            each = range(heads)
            places = [[slot_ref[(first + e) * rand + j] for j in range(rand)] for e in each]
            keys = [jnp.concatenate([buffer[p, :, :hd] for p in places[e]], axis=0) for e in each]
            scores = [dot_t(keys[e], q_ref[at, e * hd : (e + 1) * hd]) for e in each]
            scores = [
                jnp.where(key < count_ref[first + e] * blk, scores[e] * factor, NEG) for e in each
            ]
            top0 = [stat_ref[first + e, 0:1] for e in each]
            total0 = [stat_ref[first + e, 1:2] for e in each]
            top = [jnp.maximum(jnp.max(scores[e], axis=0, keepdims=True), top0[e]) for e in each]
            keep = [jnp.exp2(top0[e] - top[e]) for e in each]
            expo = [jnp.exp2(scores[e] - top[e]) for e in each]
            total = [total0[e] * keep[e] + jnp.sum(expo[e], axis=0, keepdims=True) for e in each]
            values = [jnp.concatenate([buffer[p, :, hd:] for p in places[e]], axis=1) for e in each]
            summed = [acc_ref[first + e] * keep[e] + dot(values[e], expo[e].astype(BF)) for e in each]
            for e in each:
                done[first + e] = (summed[e] / total[e]).T.astype(BF)
            for e in each:
                deliver(first + e).start()
            return carry

        for copy in copies:
            copy.wait()
        lax.fori_loop(0, rows, step, 0)
        for i in range(items):
            deliver(i).wait()

    vmem = pl.BlockSpec(memory_space=pltpu.VMEM)
    anywhere = pl.BlockSpec(memory_space=pl.ANY)
    return pl.pallas_call(
        kernel,
        out_shape=jax.ShapeDtypeStruct((peers, blk, hd), BF),
        grid_spec=pltpu.PrefetchScalarGridSpec(
            num_scalar_prefetch=3,
            grid=(1,),
            in_specs=[vmem, vmem, vmem, *[anywhere] * len(tiles)],
            out_specs=pl.BlockSpec(memory_space=pltpu.HBM),
            scratch_shapes=[
                pltpu.VMEM((slots, blk, 2 * hd), BF),
                pltpu.VMEM((items, blk, hd), BF),
                pltpu.SemaphoreType.DMA((len(tiles),)),
                pltpu.SemaphoreType.DMA((items,)),
            ],
        ),
        compiler_params=params(),
        name="rand_attend",
    )(slot, count, target, query, acc, stat, *tiles)


NX, NZ, NC = 4, 8, 2
def device(x, z, core):
    return (x % NX * NZ + z % NZ) * NC + core


def seq_pairs(goal):
    return [
        (device(x, z, c), device(*goal(x, z, c)))
        for x in range(NX)
        for z in range(NZ)
        for c in range(NC)
    ]


def local(tokens, w_qkv, item_at, rand_cols, rand_used):
    peers = lax.axis_size("seq")
    assert peers == NX * NZ * NC
    me = lax.axis_index("seq")
    my_x, my_z, my_core = me // (NZ * NC), me // NC % NZ, me % NC
    groups = lax.axis_size("head")
    mine_y = lax.axis_index("head")
    heads, nblocks, rand = rand_cols.shape
    rows = nblocks // peers
    count, depth = tokens.shape
    blk = count // rows
    hd = w_qkv.shape[1] // (3 * heads)
    width = heads * hd
    items = heads * rows
    factor = math.log2(math.e) / math.sqrt(hd)

    asked = rand_cols.reshape(heads, peers, rows, rand).transpose(1, 2, 0, 3)
    asked = asked.reshape(peers, items * rand)
    order = jnp.arange(items * rand, dtype=jnp.int32)
    code = order * items + (order // rand) % heads * rows + asked % rows

    def held_for(holder):
        held = asked // rows == holder
        low = jnp.min(jnp.where(held, code, jnp.int32(1 << 30)), axis=1) % items
        high = jnp.max(jnp.where(held, code, 0), axis=1) % items
        return jnp.stack([low, high], axis=1).reshape(-1)

    far_z = device(my_x, my_z + NZ // 2, my_core)
    tables = (held_for(me), held_for(far_z))
    plane = NX * NC
    spot = jnp.arange(plane, dtype=jnp.int32)
    even = jnp.concatenate([spot[0:2], spot[4:6]])
    odd = jnp.concatenate([spot[2:4], spot[6:8]])
    moves = [(0, spot), (1, spot), (-1, spot), (2, even), (-2, odd)]
    dests = jnp.concatenate(
        [device(at // NC, my_z + move, at % NC) for move, at in moves]
    ).astype(jnp.int32)

    wanted = lax.dynamic_index_in_dim(asked, me, 0, keepdims=False)
    source = wanted // rows
    rank = jnp.sum(
        ((source[:, None] == source[None, :]) & (order[None, :] < order[:, None])).astype(jnp.int32),
        axis=1,
    )
    step = (my_z - source // NC) % NZ
    source_spot = source // (NZ * NC) * NC + source % NC
    my_two = (2 - 4 * (my_x % 2)) % NZ

    def route_kind(step):
        return jnp.where(
            step == 0, 0, jnp.where(step == 1, 1, jnp.where(step == NZ - 1, 2, jnp.where(step == my_two, 3, -1)))
        )

    near_kind = route_kind(step)
    other_kind = route_kind((step + NZ // 2) % NZ)
    half = (near_kind < 0).astype(jnp.int32)
    slot = source_spot * 4 + jnp.where(half == 1, other_kind, near_kind)
    slot = half * (items * rand // 2) + slot * 2 + rank

    my_used = lax.dynamic_slice_in_dim(rand_used, me * rows, rows, axis=1).T.reshape(-1)
    number = jnp.arange(items, dtype=jnp.int32)
    my_item = (number % heads) * nblocks + me * rows + number // heads
    place = jnp.arange(peers * items, dtype=jnp.int32)
    target = jnp.sum(
        jnp.where(item_at[0][None, :] == my_item[:, None], place[None, :] // items, 0), axis=1
    )
    home = (lax.dynamic_slice_in_dim(item_at[0], me * items, items) % nblocks) // rows
    edges = jnp.stack([me == 0, me == peers - 1]).astype(jnp.int32)

    def weight(shift, first, size):
        row = (mine_y + shift) % groups * depth
        return lax.dynamic_slice(w_qkv, (row, jnp.int32(first)), (depth, size))

    def w_pair(shift):
        return weight(shift, width, 2 * width)

    def w_query(shift):
        return weight(shift, 0, width)

    def spread(block, stride):
        holders = range(0, peers, 4 * stride)
        got = [
            lax.ppermute(block, "seq", [(h, h + k * stride) for h in holders]) for k in (1, 2, 3)
        ]
        return block + got[0] + got[1] + got[2]

    onward = [(i, (i + 1) % groups) for i in range(groups)]
    backward = [(b, a) for a, b in onward]

    def ring(part):
        middle = part.shape[0] // 2
        low = lax.ppermute(part, "head", onward)
        high = lax.ppermute(part, "head", backward)
        top = lax.ppermute(low[:middle], "head", onward)
        bottom = lax.ppermute(high[middle:], "head", backward)
        return low, high, top, bottom

    def keys_values(part, low, high, top, bottom):
        middle = part.shape[0] // 2
        total = dot(part, w_pair(0)) + dot(low, w_pair(3)) + dot(high, w_pair(1))
        return jnp.concatenate(
            [
                (total[:middle] + dot(top, w_pair(2))).astype(BF),
                (total[middle:] + dot(bottom, w_pair(2))).astype(BF),
            ],
            axis=0,
        )

    copied = lax.ppermute(tokens, "seq", seq_pairs(lambda x, z, c: (x, z + NZ // 2, c)))
    from_low, from_high, far_top, far_bottom = ring(tokens)
    zero = tokens[:blk]
    zero = jnp.where(me == 0, zero, jnp.zeros_like(zero))
    zero, own_table = lax.optimization_barrier((zero, tables[0]))
    zero = spread(spread(zero, peers // 4), peers // 16)
    zero, _ = lax.optimization_barrier((zero, (from_low, from_high)))
    zero = spread(zero, peers // 64)
    copied = jnp.concatenate([copied, zero], axis=0)
    copied_ring = ring(copied)

    pair = keys_values(tokens, from_low, from_high, far_top, far_bottom)
    up = [(i, i + 1) for i in range(peers - 1)]
    down = [(b, a) for a, b in up]
    before = lax.ppermute(pair[-blk:], "seq", up)
    after = lax.ppermute(pair[:blk], "seq", down)

    planes = [[device(x, z, c) for x in range(NX) for c in range(NC)] for z in range(NZ)]

    def along_z(part, move):
        return lax.ppermute(part, "seq", seq_pairs(lambda x, z, c: (x, z + move, c))) if move else part

    shares = [at.shape[0] for _, at in moves]
    steps = [move for move, _ in moves]
    whole = list(range(NX * NC))
    spots = [whole, whole, whole, [0, 1, 4, 5], [2, 3, 6, 7]]
    places = [[(g, min(k, 3)) for g in at] for k, at in enumerate(spots)]

    def pack(table, pair, name):
        return pack_tiles(table, dests, pair, shares, rows, heads, blk, hd, name)

    def shifted(parts):
        return [along_z(part, move) for part, move in zip(parts, steps)]

    def in_plane(block):
        got = lax.all_to_all(
            block, "seq", split_axis=0, concat_axis=0, axis_index_groups=planes, tiled=True
        )
        return got.reshape(-1, blk, 2 * hd)

    own_parts = shifted(pack(own_table, pair, "pack_own"))
    copied_pair = keys_values(copied, *copied_ring)
    copied_parts = pack(tables[1], copied_pair, "pack_copied")
    own_parts, copied_parts = lax.optimization_barrier((own_parts, copied_parts))
    copied_parts = shifted(copied_parts)
    own_tiles = in_plane(merge_parts(own_parts, places, "merge_own"))

    around = jnp.concatenate([before, pair, after], axis=0)
    far = jnp.concatenate([far_top, far_bottom], axis=0)
    query = dot(far, w_query(2)) + dot(tokens, w_query(0))
    query = (query + dot(from_low, w_query(3)) + dot(from_high, w_query(1))).astype(BF)
    first = copied_pair[count:]
    acc, stat = near_attend(edges, query, around, first, rows, heads, blk, hd, factor)
    copied_parts, acc, stat = lax.optimization_barrier((copied_parts, acc, stat))
    copied_tiles = in_plane(merge_parts(copied_parts, places, "merge_copied"))
    done = rand_attend(
        slot, my_used, target, query, (own_tiles, copied_tiles), acc, stat,
        rows, heads, blk, hd, rand, peers, factor,
    )
    back = lax.all_to_all(done, "seq", split_axis=0, concat_axis=0, tiled=True)
    return take_tiles(home, back)[None]


def solution(mesh):
    return jax.shard_map(
        local,
        mesh=mesh,
        in_specs=(
            P("seq", "head"),
            P(None, "head"),
            P("head", None),
            P("head", None, None),
            P("head", None),
        ),
        out_specs=P("head", "seq", None, None),
        check_vma=False,
    )
```

profile of v0, /device:TPU:1, one launch (start us, length us, event | category | flops | bytes accessed | tf_op | source)
XLA Modules:
  0.0 348.4 jit_solution(540799538764446439)
XLA Ops:
  0.1 1.2 reshape.309
  2.6 0.9 slice_select_fusion
  3.5 0.7 collective-permute-start.11
  4.2 1.3 collective-permute-start.10
  5.5 1.3 collective-permute-start.9
  6.9 3.6 %collective-permute-start.2 = (bf16[1024,512]{1,0:T(8,128)(2,1)S(1)}, bf16[1024,512]{1,0:T(8,128)(2,1)S(1)}, u32[]{:S(2)}, u32[]{:S(2)}) collective-permute-start(bf16[1024,512]{1,0:T(8,128)(2,1)S(1)} %copy-done.5), channel_id=1, source_target_pairs={{1,0},{2,1},{3,2},{0,3},{5,4},{6,5},{7,6},{4,7},{9,8},{10,9},{11,1... | collective-permute-start | bytes 3145736 | tf_op jit(solution)/shard_map/ppermute | solution.py:356
  10.4 4.5 %fusion.18 = f32[1024,1024]{0,1:T(8,128)} fusion(bf16[1024,512]{1,0:T(8,128)(2,1)S(1)} %copy-done.5, bf16[2048,1536]{1,0:T(8,128)(2,1)} %param.6, s32[]{:T(128)S(6)} %select_n.427), kind=kOutput, calls=%fused_computation.31 | convolution fusion | flops 1073741824 | bytes 6291460 | tf_op jit(solution)/shard_map/dot_general | solution.py:17
  14.9 7.0 %collective-permute-start.8 = (bf16[1024,512]{1,0:T(8,128)(2,1)S(1)}, bf16[1024,512]{1,0:T(8,128)(2,1)}, u32[]{:S(2)}, u32[]{:S(2)}) collective-permute-start(bf16[1024,512]{1,0:T(8,128)(2,1)S(1)} %copy-done.5), channel_id=1, source_target_pairs={{0,32},{4,36},{8,40},{12,44},{16,48},{20,52},{24,56},{28,60},{32,0... | collective-permute-start | bytes 3145736 | tf_op jit(solution)/shard_map/ppermute | solution.py:372
  21.9 1.1 add_add_fusion.2
  23.7 1.3 collective-permute-start.13
  25.1 1.3 collective-permute-start.12
  27.1 1.0 add_add_fusion.1
  28.1 2.1 collective-permute-done
  30.8 0.7 collective-permute-start.16
  31.5 1.3 collective-permute-start.15
  32.9 0.7 collective-permute-start.3
  33.6 2.9 fusion.15
  36.5 0.7 collective-permute-start.1
  37.2 42.0 %collective-permute-done.15 = bf16[128,512]{1,0:T(8,128)(2,1)S(1)} collective-permute-done((bf16[128,512]{1,0:T(8,128)(2,1)S(1)}, bf16[128,512]{1,0:T(8,128)(2,1)S(1)}, u32[]{:S(2)}, u32[]{:S(2)}) %collective-permute-start.15) | collective-permute-done | bytes 131104 | tf_op jit(solution)/shard_map/ppermute | solution.py:346
  79.3 2.4 pad_maximum_fusion.3
  81.6 2.7 collective-permute-start.19
  84.3 1.3 add_bitcast_fusion
  85.7 0.7 fusion.3
  86.4 0.7 fusion.4
  87.2 1.5 pad_maximum_fusion.2.pair_ref
  88.7 9.2 %pack_own.1 = (bf16[8,2,128,256]{3,2,1,0:T(8,128)(2,1)S(1)}, bf16[8,2,128,256]{3,2,1,0:T(8,128)(2,1)S(1)}, bf16[8,2,128,256]{3,2,1,0:T(8,128)(2,1)S(1)}, bf16[4,...) custom-call(s32[128]{0:T(128)S(1)} %reshape.312.table_ref, s32[32]{0:T(128)S(1)} %concatenate.28.dest_ref, ...), custom_call_target="tpu_custom_call" | custom-call | tf_op jit(solution)/shard_map/pack_own/pallas_call | solution.py:54
  97.9 3.2 collective-permute-start.6
  101.2 3.4 collective-permute-start.4
  104.5 3.7 %collective-permute-done.18 = bf16[1152,512]{1,0:T(8,128)(2,1)} collective-permute-done((bf16[1152,512]{1,0:T(8,128)(2,1)}, bf16[1152,512]{1,0:T(8,128)(2,1)}, u32[]{:S(2)}, u32[]{:S(2)}) %collective-permute-start.18) | collective-permute-done | bytes 1179680 | tf_op jit(solution)/shard_map/ppermute | solution.py:355
  108.2 1.1 slice.69
  110.0 1.1 slice.71
  111.2 3.8 %collective-permute-start.21 = (bf16[576,512]{1,0:T(8,128)(2,1)S(1)}, bf16[576,512]{1,0:T(8,128)(2,1)S(1)}, u32[]{:S(2)}, u32[]{:S(2)}) collective-permute-start(bf16[576,512]{1,0:T(8,128)(2,1)S(1)} %slice.71), channel_id=1, source_target_pairs={{1,0},{2,1},{3,2},{0,3},{5,4},{6,5},{7,6},{4,7},{9,8},{10,9},{11,1... | collective-permute-start | bytes 1769480 | tf_op jit(solution)/shard_map/ppermute | solution.py:358
  115.0 2.7 fusion.13
  117.6 2.7 fusion.10
  120.3 2.7 fusion
  123.0 2.8 collective-permute-start.7
  125.8 2.0 fusion.1
  127.9 2.5 fusion.2
  130.4 1.6 pad_maximum_fusion.1.pair_ref
  132.0 6.4 %pack_copied.1 = (bf16[8,2,128,256]{3,2,1,0:T(8,128)(2,1)S(1)}, bf16[8,2,128,256]{3,2,1,0:T(8,128)(2,1)}, bf16[8,2,128,256]{3,2,1,0:T(8,128)(2,1)}, bf16[4,2,128...) custom-call(s32[128]{0:T(128)S(1)} %reshape.313.table_ref, s32[32]{0:T(128)S(1)} %concatenate.28.dest_ref, ...), custom_call_target="tpu_custom_call" | custom-call | tf_op jit(solution)/shard_map/pack_copied/pallas_call | solution.py:54
  138.4 1.0 copy-done.2
  139.5 7.7 %collective-permute-done.7.refs_4_ = bf16[4,2,128,256]{3,2,1,0:T(8,128)(2,1)S(1)} collective-permute-done((bf16[4,2,128,256]{3,2,1,0:T(8,128)(2,1)S(1)}, bf16[4,2,128,256]{3,2,1,0:T(8,128)(2,1)S(1)}, u32[]{:S(2)}, u32[]{:S(2)}) %collective-permute-start.7) | collective-permute-done | bytes 524320 | tf_op jit(solution)/shard_map/ppermute | solution.py:392
  147.8 2.3 merge_own.1
  150.1 10.7 %all-to-all-start = ((bf16[8,4,2,128,256]{4,3,2,1,0:T(8,128)(2,1)}), bf16[8,4,2,128,256]{4,3,2,1,0:T(8,128)(2,1)}, u32[]{:S(2)}, u32[]{:S(2)}) async-start(bf16[8,4,2,128,256]{4,3,2,1,0:T(8,128)(2,1)} %merge_own.1), calls=%async_computation | async-start | bytes 8388608 | tf_op jit(solution)/shard_map/all_to_all | solution.py:407
  160.9 2.1 fusion.34
  163.0 4.0 %collective-permute-start.26 = (bf16[128,1024]{1,0:T(8,128)(2,1)S(1)}, bf16[128,1024]{1,0:T(8,128)(2,1)S(1)}, u32[]{:S(2)}, u32[]{:S(2)}) collective-permute-start(bf16[128,1024]{1,0:T(8,128)(2,1)S(1)} %slice.72), channel_id=1, source_target_pairs={{0,4},{4,8},{8,12},{12,16},{16,20},{20,24},{24,28},{28,32},{32,36}... | collective-permute-start | bytes 786440 | tf_op jit(solution)/shard_map/ppermute | solution.py:386
  167.1 2.7 collective-permute-start.23
  169.7 1.7 fusion.32
  171.5 2.1 collective-permute-start.27
  173.6 1.8 fusion.6
  176.0 3.0 collective-permute-start.25
  179.0 1.8 fusion.5.q_ref
  180.8 20.7 %collective-permute-done.27 = bf16[128,1024]{1,0:T(8,128)(2,1)S(1)} collective-permute-done((bf16[128,1024]{1,0:T(8,128)(2,1)S(1)}, bf16[128,1024]{1,0:T(8,128)(2,1)S(1)}, u32[]{:S(2)}, u32[]{:S(2)}) %collective-permute-start.27) | collective-permute-done | bytes 262176 | tf_op jit(solution)/shard_map/ppermute | solution.py:387
  201.8 1.1 slice.74.first_ref
  202.8 9.4 %near_attend.1 = (f32[32,128,128]{2,1,0:T(8,128)S(1)}, f32[32,8,128]{2,1,0:T(8,128)S(1)}) custom-call(s32[2]{0:T(128)S(1)} %add_convert_fusion.edge_ref, bf16[1024,512]{1,0:T(8,128)(2,1)S(1)} %fusion.5.q_ref, bf16[1280,1024]{1,0:T(8,128)(2,1)S(1)} %pad_maximum_fusion.kv_ref, bf16[128,1024]{1,0:T(8,128)(2,1)S(1)} %slice.74.first_ref), custom_call_target="tpu_custom_call" | custom-call | tf_op jit(solution)/shard_map/near_attend/pallas_call | solution.py:155
  212.3 2.3 merge_copied.1
  214.6 11.6 %all-to-all-start.1 = ((bf16[8,4,2,128,256]{4,3,2,1,0:T(8,128)(2,1)}), bf16[8,4,2,128,256]{4,3,2,1,0:T(8,128)(2,1)}, u32[]{:S(2)}, u32[]{:S(2)}) async-start(bf16[8,4,2,128,256]{4,3,2,1,0:T(8,128)(2,1)} %merge_copied.1), calls=%async_computation.1 | async-start | bytes 8388608 | tf_op jit(solution)/shard_map/all_to_all | solution.py:407
  226.4 1.2 copy.27
  228.4 46.8 %all-to-all-done.1 = bf16[8,4,2,128,256]{4,3,2,1,0:T(8,128)(2,1)} async-done(((bf16[8,4,2,128,256]{4,3,2,1,0:T(8,128)(2,1)}), bf16[8,4,2,128,256]{4,3,2,1,0:T(8,128)(2,1)}, u32[]{:S(2)}, u32[]{:S(2)}) %all-to-all-start.1) | async-done | bytes 4194336 | tf_op jit(solution)/shard_map/all_to_all | solution.py:407
  275.1 12.2 %rand_attend.1 = bf16[64,128,128]{2,1,0:T(8,128)(2,1)S(1)} custom-call(s32[128]{0:T(128)S(1)} %fusion.69.slot_ref, s32[32]{0:T(128)S(1)} %reshape.311.count_ref, s32[32]{0:T(128)S(1)} %select_reduce_fusion.4.target_ref, bf16[1024,512]{1,0:T(8,128)(2,1)S(1)} %fusion.5.q_ref, f32[32,128,128]{2,1,0:T(8,128)S(1)} %get-tuple-element.57.acc_ref, ...), custom_call_target="tpu_custom_call" | custom-call | tf_op jit(solution)/shard_map/rand_attend/pallas_call | solution.py:230
  287.3 1.3 copy-done.1
  288.7 6.5 %all-to-all-start.2 = ((bf16[64,128,128]{2,1,0:T(8,128)(2,1)}), bf16[64,128,128]{2,1,0:T(8,128)(2,1)S(1)}, u32[]{:S(2)}, u32[]{:S(2)}) async-start(bf16[64,128,128]{2,1,0:T(8,128)(2,1)} %copy-done.1), calls=%async_computation.2 | async-start | bytes 4194304 | tf_op jit(solution)/shard_map/all_to_all | solution.py:431
  295.3 51.2 %all-to-all-done.2.in_ref = bf16[64,128,128]{2,1,0:T(8,128)(2,1)S(1)} async-done(((bf16[64,128,128]{2,1,0:T(8,128)(2,1)}), bf16[64,128,128]{2,1,0:T(8,128)(2,1)S(1)}, u32[]{:S(2)}, u32[]{:S(2)}) %all-to-all-start.2) | async-done | bytes 2097184 | tf_op jit(solution)/shard_map/all_to_all | solution.py:431
  346.4 1.8 take_tiles.1
  (107 shorter events, 7.1 us)
Async XLA Ops:
  0.0 226.2 %copy-start = (s32[4,512]{1,0:T(4,128)S(1)}, s32[4,512]{1,0:T(4,128)}, u32[]{:S(2)}) copy-start(s32[4,512]{1,0:T(4,128)} %param.9) | copy-start | bytes 24580
  0.0 6.9 %copy-start.5 = (bf16[1024,512]{1,0:T(8,128)(2,1)S(1)}, bf16[1024,512]{1,0:T(8,128)(2,1)}, u32[]{:S(2)}) copy-start(bf16[1024,512]{1,0:T(8,128)(2,1)} %param.5) | copy-start | bytes 3145732
  1.2 1.2 copy-start.6
  3.5 11.4 %collective-permute-start.11 = (bf16[128,512]{1,0:T(8,128)(2,1)S(1)}, bf16[128,512]{1,0:T(8,128)(2,1)S(1)}, u32[]{:S(2)}, u32[]{:S(2)}) collective-permute-start(bf16[128,512]{1,0:T(8,128)(2,1)S(1)} %slice_select_fusion), channel_id=1, source_target_pairs={{0,192},{1,193},{2,194},{3,195}} | collective-permute-start | bytes 393224 | tf_op jit(solution)/shard_map/ppermute | solution.py:346
  4.2 17.7 %collective-permute-start.10 = (bf16[128,512]{1,0:T(8,128)(2,1)S(1)}, bf16[128,512]{1,0:T(8,128)(2,1)}, u32[]{:S(2)}, u32[]{:S(2)}) collective-permute-start(bf16[128,512]{1,0:T(8,128)(2,1)S(1)} %slice_select_fusion), channel_id=1, source_target_pairs={{0,128},{1,129},{2,130},{3,131}} | collective-permute-start | bytes 393224 | tf_op jit(solution)/shard_map/ppermute | solution.py:346
  5.5 16.4 %collective-permute-start.9 = (bf16[128,512]{1,0:T(8,128)(2,1)S(1)}, bf16[128,512]{1,0:T(8,128)(2,1)}, u32[]{:S(2)}, u32[]{:S(2)}) collective-permute-start(bf16[128,512]{1,0:T(8,128)(2,1)S(1)} %slice_select_fusion), channel_id=1, source_target_pairs={{0,64},{1,65},{2,66},{3,67}} | collective-permute-start | bytes 393224 | tf_op jit(solution)/shard_map/ppermute | solution.py:346
  6.9 21.2 %collective-permute-start.2 = (bf16[1024,512]{1,0:T(8,128)(2,1)S(1)}, bf16[1024,512]{1,0:T(8,128)(2,1)S(1)}, u32[]{:S(2)}, u32[]{:S(2)}) collective-permute-start(bf16[1024,512]{1,0:T(8,128)(2,1)S(1)} %copy-done.5), channel_id=1, source_target_pairs={{1,0},{2,1},{3,2},{0,3},{5,4},{6,5},{7,6},{4,7},{9,8},{10,9},{11,1... | collective-permute-start | bytes 3145736 | tf_op jit(solution)/shard_map/ppermute | solution.py:356
  10.4 19.8 %collective-permute-start = (bf16[1024,512]{1,0:T(8,128)(2,1)S(1)}, bf16[1024,512]{1,0:T(8,128)(2,1)S(1)}, u32[]{:S(2)}, u32[]{:S(2)}) collective-permute-start(bf16[1024,512]{1,0:T(8,128)(2,1)S(1)} %copy-done.5), channel_id=1, source_target_pairs={{0,1},{1,2},{2,3},{3,0},{4,5},{5,6},{6,7},{7,4},{8,9},{9,10},{10,1... | collective-permute-start | bytes 3145736 | tf_op jit(solution)/shard_map/ppermute | solution.py:355
  14.9 7.0 %copy-start.14 = (bf16[128,512]{1,0:T(8,128)(2,1)}, bf16[128,512]{1,0:T(8,128)(2,1)S(1)}, u32[]{:S(2)}) copy-start(bf16[128,512]{1,0:T(8,128)(2,1)S(1)} %collective-permute-done.11) | copy-start | bytes 393220
  14.9 64.3 %collective-permute-start.8 = (bf16[1024,512]{1,0:T(8,128)(2,1)S(1)}, bf16[1024,512]{1,0:T(8,128)(2,1)}, u32[]{:S(2)}, u32[]{:S(2)}) collective-permute-start(bf16[1024,512]{1,0:T(8,128)(2,1)S(1)} %copy-done.5), channel_id=1, source_target_pairs={{0,32},{4,36},{8,40},{12,44},{16,48},{20,52},{24,56},{28,60},{32,0... | collective-permute-start | bytes 3145736 | tf_op jit(solution)/shard_map/ppermute | solution.py:372
  23.0 2.1 collective-permute-start.14
  23.7 3.3 collective-permute-start.13
  25.1 2.0 collective-permute-start.12
  28.1 56.2 %copy-start.7 = (bf16[1024,512]{1,0:T(8,128)(2,1)}, bf16[1024,512]{1,0:T(8,128)(2,1)S(1)}, u32[]{:S(2)}) copy-start(bf16[1024,512]{1,0:T(8,128)(2,1)S(1)} %collective-permute-done.2) | copy-start | bytes 3145732
  30.2 6.3 %collective-permute-start.17 = (bf16[128,512]{1,0:T(8,128)(2,1)S(1)}, bf16[128,512]{1,0:T(8,128)(2,1)S(1)}, u32[]{:S(2)}, u32[]{:S(2)}) collective-permute-start(bf16[128,512]{1,0:T(8,128)(2,1)S(1)} %add_add_fusion.1), channel_id=1, source_target_pairs={{0,12},{16,28},{32,44},{48,60},{64,76},{80,92},{96,108},{112,124},... | collective-permute-start | bytes 393224 | tf_op jit(solution)/shard_map/ppermute | solution.py:346
  30.8 6.4 %collective-permute-start.16 = (bf16[128,512]{1,0:T(8,128)(2,1)S(1)}, bf16[128,512]{1,0:T(8,128)(2,1)S(1)}, u32[]{:S(2)}, u32[]{:S(2)}) collective-permute-start(bf16[128,512]{1,0:T(8,128)(2,1)S(1)} %add_add_fusion.1), channel_id=1, source_target_pairs={{0,8},{16,24},{32,40},{48,56},{64,72},{80,88},{96,104},{112,120},{... | collective-permute-start | bytes 393224 | tf_op jit(solution)/shard_map/ppermute | solution.py:346
  31.5 47.7 %collective-permute-start.15 = (bf16[128,512]{1,0:T(8,128)(2,1)S(1)}, bf16[128,512]{1,0:T(8,128)(2,1)S(1)}, u32[]{:S(2)}, u32[]{:S(2)}) collective-permute-start(bf16[128,512]{1,0:T(8,128)(2,1)S(1)} %add_add_fusion.1), channel_id=1, source_target_pairs={{0,4},{16,20},{32,36},{48,52},{64,68},{80,84},{96,100},{112,116},{... | collective-permute-start | bytes 393224 | tf_op jit(solution)/shard_map/ppermute | solution.py:346
  32.8 51.5 %slice-start = ((s8[6291456]{0:T(1024)(128)(4,1)}), s8[4194304]{0:T(1024)(128)(4,1)S(1)}, s32[]{:S(2)}) async-start(s8[6291456]{0:T(1024)(128)(4,1)} %bitcast.63), calls=%async_computation.3 | async-start | bytes 8388608
  32.9 51.4 %slice-start.1 = ((s8[6291456]{0:T(1024)(128)(4,1)}), s8[2097152]{0:T(1024)(128)(4,1)S(1)}, s32[]{:S(2)}) async-start(s8[6291456]{0:T(1024)(128)(4,1)} %bitcast.63), calls=%async_computation.4 | async-start | bytes 4194304
  32.9 52.8 %collective-permute-start.3 = (bf16[512,512]{1,0:T(8,128)(2,1)S(1)}, bf16[512,512]{1,0:T(8,128)(2,1)S(1)}, u32[]{:S(2)}, u32[]{:S(2)}) collective-permute-start(bf16[512,512]{1,0:T(8,128)(2,1)S(1)} %slice.65), channel_id=1, source_target_pairs={{1,0},{2,1},{3,2},{0,3},{5,4},{6,5},{7,6},{4,7},{9,8},{10,9},{11,1... | collective-permute-start | bytes 1572872 | tf_op jit(solution)/shard_map/ppermute | solution.py:358
  33.6 50.7 %copy-start.4 = (f32[1024,1024]{0,1:T(8,128)S(1)}, f32[1024,1024]{0,1:T(8,128)}, u32[]{:S(2)}) copy-start(f32[1024,1024]{0,1:T(8,128)} %fusion.18) | copy-start | bytes 12582916
  36.5 49.9 %collective-permute-start.1 = (bf16[512,512]{1,0:T(8,128)(2,1)S(1)}, bf16[512,512]{1,0:T(8,128)(2,1)S(1)}, u32[]{:S(2)}, u32[]{:S(2)}) collective-permute-start(bf16[512,512]{1,0:T(8,128)(2,1)S(1)} %slice.64), channel_id=1, source_target_pairs={{0,1},{1,2},{2,3},{3,0},{4,5},{5,6},{6,7},{7,4},{8,9},{9,10},{10,1... | collective-permute-start | bytes 1572872 | tf_op jit(solution)/shard_map/ppermute | solution.py:357
  81.6 26.6 %collective-permute-start.18 = (bf16[1152,512]{1,0:T(8,128)(2,1)}, bf16[1152,512]{1,0:T(8,128)(2,1)}, u32[]{:S(2)}, u32[]{:S(2)}) collective-permute-start(bf16[1152,512]{1,0:T(8,128)(2,1)} %pad_maximum_fusion.3), channel_id=1, source_target_pairs={{0,1},{1,2},{2,3},{3,0},{4,5},{5,6},{6,7},{7,4},{8,9},{9,10},{10,1... | collective-permute-start | bytes 3538952 | tf_op jit(solution)/shard_map/ppermute | solution.py:355
  81.6 28.4 %collective-permute-start.19 = (bf16[1152,512]{1,0:T(8,128)(2,1)}, bf16[1152,512]{1,0:T(8,128)(2,1)}, u32[]{:S(2)}, u32[]{:S(2)}) collective-permute-start(bf16[1152,512]{1,0:T(8,128)(2,1)} %pad_maximum_fusion.3), channel_id=1, source_target_pairs={{1,0},{2,1},{3,2},{0,3},{5,4},{6,5},{7,6},{4,7},{9,8},{10,9},{11,1... | collective-permute-start | bytes 3538952 | tf_op jit(solution)/shard_map/ppermute | solution.py:356
  85.7 1.5 copy-start.10
  86.4 0.8 copy-start.12
  97.9 41.5 %collective-permute-start.6 = (bf16[4,2,128,256]{3,2,1,0:T(8,128)(2,1)S(1)}, bf16[4,2,128,256]{3,2,1,0:T(8,128)(2,1)S(1)}, u32[]{:S(2)}, u32[]{:S(2)}) collective-permute-start(bf16[4,2,128,256]{3,2,1,0:T(8,128)(2,1)S(1)} %get-tuple-element.41), channel_id=1, source_target_pairs={{0,16},{4,20},{8,24},{12,28},{16,32},{20,36},{24,40},{28,44},{32,4... | collective-permute-start | bytes 1572872 | tf_op jit(solution)/shard_map/ppermute | solution.py:392
  101.2 46.6 %collective-permute-start.4 = (bf16[8,2,128,256]{3,2,1,0:T(8,128)(2,1)S(1)}, bf16[8,2,128,256]{3,2,1,0:T(8,128)(2,1)S(1)}, u32[]{:S(2)}, u32[]{:S(2)}) collective-permute-start(bf16[8,2,128,256]{3,2,1,0:T(8,128)(2,1)S(1)} %get-tuple-element.39), channel_id=1, source_target_pairs={{0,8},{4,12},{8,16},{12,20},{16,24},{20,28},{24,32},{28,36},{32,40... | collective-permute-start | bytes 3145736 | tf_op jit(solution)/shard_map/ppermute | solution.py:392
  104.5 43.2 %collective-permute-start.5 = (bf16[8,2,128,256]{3,2,1,0:T(8,128)(2,1)S(1)}, bf16[8,2,128,256]{3,2,1,0:T(8,128)(2,1)S(1)}, u32[]{:S(2)}, u32[]{:S(2)}) collective-permute-start(bf16[8,2,128,256]{3,2,1,0:T(8,128)(2,1)S(1)} %get-tuple-element.40), channel_id=1, source_target_pairs={{0,56},{4,60},{8,0},{12,4},{16,8},{20,12},{24,16},{28,20},{32,24},... | collective-permute-start | bytes 3145736 | tf_op jit(solution)/shard_map/ppermute | solution.py:392
  109.3 18.6 %collective-permute-start.20 = (bf16[576,512]{1,0:T(8,128)(2,1)S(1)}, bf16[576,512]{1,0:T(8,128)(2,1)S(1)}, u32[]{:S(2)}, u32[]{:S(2)}) collective-permute-start(bf16[576,512]{1,0:T(8,128)(2,1)S(1)} %slice.69), channel_id=1, source_target_pairs={{0,1},{1,2},{2,3},{3,0},{4,5},{5,6},{6,7},{7,4},{8,9},{9,10},{10,1... | collective-permute-start | bytes 1769480 | tf_op jit(solution)/shard_map/ppermute | solution.py:357
  111.2 11.8 %collective-permute-start.21 = (bf16[576,512]{1,0:T(8,128)(2,1)S(1)}, bf16[576,512]{1,0:T(8,128)(2,1)S(1)}, u32[]{:S(2)}, u32[]{:S(2)}) collective-permute-start(bf16[576,512]{1,0:T(8,128)(2,1)S(1)} %slice.71), channel_id=1, source_target_pairs={{1,0},{2,1},{3,2},{0,3},{5,4},{6,5},{7,6},{4,7},{9,8},{10,9},{11,1... | collective-permute-start | bytes 1769480 | tf_op jit(solution)/shard_map/ppermute | solution.py:358
  123.0 24.2 %collective-permute-start.7 = (bf16[4,2,128,256]{3,2,1,0:T(8,128)(2,1)S(1)}, bf16[4,2,128,256]{3,2,1,0:T(8,128)(2,1)S(1)}, u32[]{:S(2)}, u32[]{:S(2)}) collective-permute-start(bf16[4,2,128,256]{3,2,1,0:T(8,128)(2,1)S(1)} %get-tuple-element.42), channel_id=1, source_target_pairs={{0,48},{4,52},{8,56},{12,60},{16,0},{20,4},{24,8},{28,12},{32,16},... | collective-permute-start | bytes 1572872 | tf_op jit(solution)/shard_map/ppermute | solution.py:392
  127.9 2.5 copy-start.9
  138.4 1.0 copy-start.2
  150.1 64.5 %all-to-all-start = ((bf16[8,4,2,128,256]{4,3,2,1,0:T(8,128)(2,1)}), bf16[8,4,2,128,256]{4,3,2,1,0:T(8,128)(2,1)}, u32[]{:S(2)}, u32[]{:S(2)}) async-start(bf16[8,4,2,128,256]{4,3,2,1,0:T(8,128)(2,1)} %merge_own.1), calls=%async_computation | async-start | bytes 8388608 | tf_op jit(solution)/shard_map/all_to_all | solution.py:407
  163.0 10.6 %copy-start.11 = (bf16[512,512]{1,0:T(8,128)(2,1)S(1)}, bf16[512,512]{1,0:T(8,128)(2,1)}, u32[]{:S(2)}) copy-start(bf16[512,512]{1,0:T(8,128)(2,1)} %copy-done.10) | copy-start | bytes 1572868
  163.0 10.6 %copy-start.13 = (bf16[512,512]{1,0:T(8,128)(2,1)S(1)}, bf16[512,512]{1,0:T(8,128)(2,1)}, u32[]{:S(2)}) copy-start(bf16[512,512]{1,0:T(8,128)(2,1)} %copy-done.12) | copy-start | bytes 1572868
  163.0 13.0 %collective-permute-start.26 = (bf16[128,1024]{1,0:T(8,128)(2,1)S(1)}, bf16[128,1024]{1,0:T(8,128)(2,1)S(1)}, u32[]{:S(2)}, u32[]{:S(2)}) collective-permute-start(bf16[128,1024]{1,0:T(8,128)(2,1)S(1)} %slice.72), channel_id=1, source_target_pairs={{0,4},{4,8},{8,12},{12,16},{16,20},{20,24},{24,28},{28,32},{32,36}... | collective-permute-start | bytes 786440 | tf_op jit(solution)/shard_map/ppermute | solution.py:386
  167.0 45.3 %collective-permute-start.22 = (bf16[8,2,128,256]{3,2,1,0:T(8,128)(2,1)}, bf16[8,2,128,256]{3,2,1,0:T(8,128)(2,1)S(1)}, u32[]{:S(2)}, u32[]{:S(2)}) collective-permute-start(bf16[8,2,128,256]{3,2,1,0:T(8,128)(2,1)} %get-tuple-element.51), channel_id=1, source_target_pairs={{0,8},{4,12},{8,16},{12,20},{16,24},{20,28},{24,32},{28,36},{32,40... | collective-permute-start | bytes 3145736 | tf_op jit(solution)/shard_map/ppermute | solution.py:392
  167.1 45.2 %collective-permute-start.23 = (bf16[8,2,128,256]{3,2,1,0:T(8,128)(2,1)}, bf16[8,2,128,256]{3,2,1,0:T(8,128)(2,1)S(1)}, u32[]{:S(2)}, u32[]{:S(2)}) collective-permute-start(bf16[8,2,128,256]{3,2,1,0:T(8,128)(2,1)} %get-tuple-element.52), channel_id=1, source_target_pairs={{0,56},{4,60},{8,0},{12,4},{16,8},{20,12},{24,16},{28,20},{32,24},... | collective-permute-start | bytes 3145736 | tf_op jit(solution)/shard_map/ppermute | solution.py:392
  171.5 7.5 %copy-start.8 = (bf16[1024,512]{1,0:T(8,128)(2,1)S(1)}, bf16[1024,512]{1,0:T(8,128)(2,1)}, u32[]{:S(2)}) copy-start(bf16[1024,512]{1,0:T(8,128)(2,1)} %copy-done.7) | copy-start | bytes 3145732
  171.5 29.9 %collective-permute-start.27 = (bf16[128,1024]{1,0:T(8,128)(2,1)S(1)}, bf16[128,1024]{1,0:T(8,128)(2,1)S(1)}, u32[]{:S(2)}, u32[]{:S(2)}) collective-permute-start(bf16[128,1024]{1,0:T(8,128)(2,1)S(1)} %slice.73), channel_id=1, source_target_pairs={{4,0},{8,4},{12,8},{16,12},{20,16},{24,20},{28,24},{32,28},{36,32}... | collective-permute-start | bytes 786440 | tf_op jit(solution)/shard_map/ppermute | solution.py:387
  175.3 36.9 %collective-permute-start.24 = (bf16[4,2,128,256]{3,2,1,0:T(8,128)(2,1)}, bf16[4,2,128,256]{3,2,1,0:T(8,128)(2,1)S(1)}, u32[]{:S(2)}, u32[]{:S(2)}) collective-permute-start(bf16[4,2,128,256]{3,2,1,0:T(8,128)(2,1)} %get-tuple-element.53), channel_id=1, source_target_pairs={{0,16},{4,20},{8,24},{12,28},{16,32},{20,36},{24,40},{28,44},{32,4... | collective-permute-start | bytes 1572872 | tf_op jit(solution)/shard_map/ppermute | solution.py:392
  176.0 36.2 %collective-permute-start.25 = (bf16[4,2,128,256]{3,2,1,0:T(8,128)(2,1)}, bf16[4,2,128,256]{3,2,1,0:T(8,128)(2,1)S(1)}, u32[]{:S(2)}, u32[]{:S(2)}) collective-permute-start(bf16[4,2,128,256]{3,2,1,0:T(8,128)(2,1)} %get-tuple-element.54), channel_id=1, source_target_pairs={{0,48},{4,52},{8,56},{12,60},{16,0},{20,4},{24,8},{28,12},{32,16},... | collective-permute-start | bytes 1572872 | tf_op jit(solution)/shard_map/ppermute | solution.py:392
  201.8 10.5 %copy-start.3 = (bf16[8,2,128,256]{3,2,1,0:T(8,128)(2,1)S(1)}, bf16[8,2,128,256]{3,2,1,0:T(8,128)(2,1)}, u32[]{:S(2)}) copy-start(bf16[8,2,128,256]{3,2,1,0:T(8,128)(2,1)} %copy-done.2) | copy-start | bytes 3145732
  214.6 13.5 %copy-start.15 = (s32[1,2048]{1,0:T(1,128)S(1)}, s32[1,2048]{1,0:T(1,128)}, u32[]{:S(2)}) copy-start(s32[1,2048]{1,0:T(1,128)} %param.7) | copy-start | bytes 24580
  214.6 60.5 %all-to-all-start.1 = ((bf16[8,4,2,128,256]{4,3,2,1,0:T(8,128)(2,1)}), bf16[8,4,2,128,256]{4,3,2,1,0:T(8,128)(2,1)}, u32[]{:S(2)}, u32[]{:S(2)}) async-start(bf16[8,4,2,128,256]{4,3,2,1,0:T(8,128)(2,1)} %merge_copied.1), calls=%async_computation.1 | async-start | bytes 8388608 | tf_op jit(solution)/shard_map/all_to_all | solution.py:407
  287.3 1.4 copy-start.1
  288.7 57.8 %all-to-all-start.2 = ((bf16[64,128,128]{2,1,0:T(8,128)(2,1)}), bf16[64,128,128]{2,1,0:T(8,128)(2,1)S(1)}, u32[]{:S(2)}, u32[]{:S(2)}) async-start(bf16[64,128,128]{2,1,0:T(8,128)(2,1)} %copy-done.1), calls=%async_computation.2 | async-start | bytes 4194304 | tf_op jit(solution)/shard_map/all_to_all | solution.py:431
where the time goes:
time: 350 us; the launch traced here: 348 us
  waiting for transfers between devices  175 us (50%)
  starting transfers between devices  78.8 us (23%)
  Pallas kernels  43.6 us (12%)
  matrix products  29.9 us (9%)
  other arithmetic  11 us (3%)
  local copies, waits for them, and re-layouts  9.27 us (3%)
    all_to_all x1, waiting for transfers between devices, local(): back = lax.all_to_all(done, 'seq', split_axis=0, concat_axis=0, tiled=True)  51.2 us
    all_to_all x2, waiting for transfers between devices, in_plane(): lax.all_to_all(block, 'seq', split_axis=0, concat_axis=0, axis_index_grou...  46.8 us
    ppermute x9, waiting for transfers between devices, spread(): lax.ppermute(block, 'seq', [(h, h + k * stride) for h in holders])  42 us
    dot_general x14, matrix products, dot(): return jnp.dot(a, b, preferred_element_type=F32)  29.9 us
    all_to_all x2, starting transfers between devices, in_plane(): lax.all_to_all(block, 'seq', split_axis=0, concat_axis=0, axis_index_grou...  22.3 us
    ppermute x1, waiting for transfers between devices, local(): after = lax.ppermute(pair[:blk], 'seq', down)  20.7 us
    ppermute x8, starting transfers between devices, along_z(): lax.ppermute(part, 'seq', seq_pairs(lambda x, z, c: (x, z + move, c)))  15.8 us
    pallas_call x2, Pallas kernels, pack_tiles(): pl.pallas_call(kernel, out_shape=[jax.ShapeDtypeStruct((share, 2, blk, 2...  15.6 us
  transfers between devices with their start and end apart: 31, of which 9 were waited for; matrix products, arithmetic and copies ran while one was open for 13% of the time, Pallas kernels for 8%

commit v1 on v0

--- a/solution.py
+++ b/solution.py
@@ -369,14 +369,12 @@
             axis=0,
         )
 
-    copied = lax.ppermute(tokens, "seq", seq_pairs(lambda x, z, c: (x, z + NZ // 2, c)))
     from_low, from_high, far_top, far_bottom = ring(tokens)
     zero = tokens[:blk]
     zero = jnp.where(me == 0, zero, jnp.zeros_like(zero))
-    zero, own_table = lax.optimization_barrier((zero, tables[0]))
-    zero = spread(spread(zero, peers // 4), peers // 16)
-    zero, _ = lax.optimization_barrier((zero, (from_low, from_high)))
-    zero = spread(zero, peers // 64)
+    zero = spread(spread(spread(zero, peers // 4), peers // 16), peers // 64)
+    copied, zero = lax.optimization_barrier((tokens, zero))
+    copied = lax.ppermute(copied, "seq", seq_pairs(lambda x, z, c: (x, z + NZ // 2, c)))
     copied = jnp.concatenate([copied, zero], axis=0)
     copied_ring = ring(copied)
 
@@ -409,10 +407,10 @@
         )
         return got.reshape(-1, blk, 2 * hd)
 
-    own_parts = shifted(pack(own_table, pair, "pack_own"))
+    own_parts = shifted(pack(tables[0], pair, "pack_own"))
     copied_pair = keys_values(copied, *copied_ring)
     copied_parts = pack(tables[1], copied_pair, "pack_copied")
-    own_parts, copied_parts = lax.optimization_barrier((own_parts, copied_parts))
+    own_parts, _ = lax.optimization_barrier((own_parts, copied_parts))
     copied_parts = shifted(copied_parts)
     own_tiles = in_plane(merge_parts(own_parts, places, "merge_own"))
 

time: 350 us -> 349 us (level)
  starting transfers between devices: 78.8 us -> 65.3 us
  waiting for transfers between devices: 175 us -> 188 us
  local copies, waits for them, and re-layouts: 9.27 us -> 13.1 us
    ppermute x1, waiting for transfers between devices: 0.01 us -> 36.6 us  [local(): lax.ppermute(copied, 'seq', seq_pairs(lambda x, z, c: (x, z + NZ // 2, c)))]
    ppermute x9, waiting for transfers between devices: 42 us -> 13.7 us  [spread(): lax.ppermute(block, 'seq', [(h, h + k * stride) for h in holders])]
    ppermute x1, waiting for transfers between devices: 20.7 us -> 0.01 us  [local(): after = lax.ppermute(pair[:blk], 'seq', down)]
    ppermute x1, waiting for transfers between devices: 0.01 us -> 12.1 us  [local(): before = lax.ppermute(pair[-blk:], 'seq', up)]
    ppermute x8, starting transfers between devices: 15.8 us -> 9.38 us  [along_z(): lax.ppermute(part, 'seq', seq_pairs(lambda x, z, c: (x, z + move, c)))]
    ppermute x2, waiting for transfers between devices: 0.31 us -> 6.49 us  [ring(): high = lax.ppermute(part, 'head', backward)]
    ppermute x2, waiting for transfers between devices: 5.73 us -> 0.01 us  [ring(): low = lax.ppermute(part, 'head', onward)]
    ppermute x8, waiting for transfers between devices: 8.34 us -> 13.6 us  [along_z(): lax.ppermute(part, 'seq', seq_pairs(lambda x, z, c: (x, z + move, c)))]
  transfers between devices with their start and end apart: 31 -> 31, of which waited for: 9 -> 12; matrix products, arithmetic and copies ran while one was open for 13% -> 13% of each run, Pallas kernels for 8% -> 8%
where the time goes in v1:
time: 349 us; the launch traced here: 347 us
  waiting for transfers between devices  188 us (54%)
  starting transfers between devices  65.3 us (19%)
  Pallas kernels  43.5 us (12%)
  matrix products  28.8 us (8%)
  local copies, waits for them, and re-layouts  13.1 us (4%)
  other arithmetic  7.52 us (2%)
    all_to_all x1, waiting for transfers between devices, local(): back = lax.all_to_all(done, 'seq', split_axis=0, concat_axis=0, tiled=True)  51.3 us
    all_to_all x2, waiting for transfers between devices, in_plane(): lax.all_to_all(block, 'seq', split_axis=0, concat_axis=0, axis_index_grou...  51 us
    ppermute x1, waiting for transfers between devices, local(): lax.ppermute(copied, 'seq', seq_pairs(lambda x, z, c: (x, z + NZ // 2, c)))  36.6 us
    dot_general x14, matrix products, dot(): return jnp.dot(a, b, preferred_element_type=F32)  28.8 us
    all_to_all x2, starting transfers between devices, in_plane(): lax.all_to_all(block, 'seq', split_axis=0, concat_axis=0, axis_index_grou...  21.1 us
    pallas_call x2, Pallas kernels, pack_tiles(): pl.pallas_call(kernel, out_shape=[jax.ShapeDtypeStruct((share, 2, blk, 2...  15.6 us
    ppermute x9, waiting for transfers between devices, spread(): lax.ppermute(block, 'seq', [(h, h + k * stride) for h in holders])  13.7 us
    ppermute x8, waiting for transfers between devices, along_z(): lax.ppermute(part, 'seq', seq_pairs(lambda x, z, c: (x, z + move, c)))  13.6 us
  transfers between devices with their start and end apart: 31, of which 12 were waited for; matrix products, arithmetic and copies ran while one was open for 13% of the time, Pallas kernels for 8%

profile of v1, /device:TPU:1, one launch (start us, length us, event | category | flops | bytes accessed | tf_op | source)
XLA Modules:
  0.0 347.5 jit_solution(8567244428165449932)
XLA Ops:
  0.0 1.0 slice_select_fusion
  1.0 0.7 collective-permute-start.5
  1.7 0.7 collective-permute-start.6
  3.0 3.6 %collective-permute-start.2 = (bf16[1024,512]{1,0:T(8,128)(2,1)}, bf16[1024,512]{1,0:T(8,128)(2,1)}, u32[]{:S(2)}, u32[]{:S(2)}) collective-permute-start(bf16[1024,512]{1,0:T(8,128)(2,1)} %param.5), channel_id=1, source_target_pairs={{1,0},{2,1},{3,2},{0,3},{5,4},{6,5},{7,6},{4,7},{9,8},{10,9},{11,1... | collective-permute-start | bytes 3145736 | tf_op jit(solution)/shard_map/ppermute | solution.py:356
  6.7 1.1 reshape.309
  8.3 0.7 select_reduce_fusion.1
  9.0 0.9 add_add_fusion.2
  13.4 1.3 collective-permute-start.10
  15.7 13.6 %collective-permute-done.10 = bf16[128,512]{1,0:T(8,128)(2,1)S(1)} collective-permute-done((bf16[128,512]{1,0:T(8,128)(2,1)S(1)}, bf16[128,512]{1,0:T(8,128)(2,1)S(1)}, u32[]{:S(2)}, u32[]{:S(2)}) %collective-permute-start.10) | collective-permute-done | bytes 131104 | tf_op jit(solution)/shard_map/ppermute | solution.py:346
  29.3 4.8 %collective-permute-start.13 = (bf16[1024,512]{1,0:T(8,128)(2,1)S(1)}, bf16[1024,512]{1,0:T(8,128)(2,1)}, u32[]{:S(2)}, u32[]{:S(2)}) collective-permute-start(bf16[1024,512]{1,0:T(8,128)(2,1)S(1)} %copy-done.4), channel_id=1, source_target_pairs={{0,32},{4,36},{8,40},{12,44},{16,48},{20,52},{24,56},{28,60},{32,0... | collective-permute-start | bytes 3145736 | tf_op jit(solution)/shard_map/ppermute | solution.py:377
  34.3 2.6 fusion.17
  37.0 1.1 slice.65
  38.1 3.0 collective-permute-start.3
  41.3 2.6 fusion.13
  43.9 36.6 %collective-permute-done.13 = bf16[1024,512]{1,0:T(8,128)(2,1)} collective-permute-done((bf16[1024,512]{1,0:T(8,128)(2,1)S(1)}, bf16[1024,512]{1,0:T(8,128)(2,1)}, u32[]{:S(2)}, u32[]{:S(2)}) %collective-permute-start.13) | collective-permute-done | bytes 1048608 | tf_op jit(solution)/shard_map/ppermute | solution.py:377
  80.5 2.3 constant_dynamic-update-slice_fusion.1
  82.7 0.7 constant_dynamic-update-slice_fusion
  83.4 3.0 collective-permute-start.15
  86.4 2.5 add_bitcast_fusion
  88.9 0.7 fusion.3
  89.7 0.7 fusion.4
  90.4 1.5 pad_maximum_fusion.2.pair_ref
  91.9 9.2 %pack_own.1 = (bf16[8,2,128,256]{3,2,1,0:T(8,128)(2,1)S(1)}, bf16[8,2,128,256]{3,2,1,0:T(8,128)(2,1)S(1)}, bf16[8,2,128,256]{3,2,1,0:T(8,128)(2,1)S(1)}, bf16[4,...) custom-call(s32[128]{0:T(128)S(1)} %reshape.313.table_ref, s32[32]{0:T(128)S(1)} %concatenate.28.dest_ref, ...), custom_call_target="tpu_custom_call" | custom-call | tf_op jit(solution)/shard_map/pack_own/pallas_call | solution.py:54
  101.2 2.9 collective-permute-start.24
  104.1 6.5 %collective-permute-done.15 = bf16[1152,512]{1,0:T(8,128)(2,1)} collective-permute-done((bf16[1152,512]{1,0:T(8,128)(2,1)}, bf16[1152,512]{1,0:T(8,128)(2,1)}, u32[]{:S(2)}, u32[]{:S(2)}) %collective-permute-start.15) | collective-permute-done | bytes 1179680 | tf_op jit(solution)/shard_map/ppermute | solution.py:356
  110.6 1.1 slice.69
  111.7 3.5 %collective-permute-start.17 = (bf16[576,512]{1,0:T(8,128)(2,1)S(1)}, bf16[576,512]{1,0:T(8,128)(2,1)S(1)}, u32[]{:S(2)}, u32[]{:S(2)}) collective-permute-start(bf16[576,512]{1,0:T(8,128)(2,1)S(1)} %slice.69), channel_id=1, source_target_pairs={{1,0},{2,1},{3,2},{0,3},{5,4},{6,5},{7,6},{4,7},{9,8},{10,9},{11,1... | collective-permute-start | bytes 1769480 | tf_op jit(solution)/shard_map/ppermute | solution.py:358
  115.2 1.1 slice.67
  116.4 2.7 fusion.15
  119.1 2.7 fusion.11
  121.7 2.7 fusion
  124.4 1.1 collective-permute-done.17
  125.6 2.0 fusion.1
  127.6 2.3 collective-permute-done.16
  129.9 2.0 fusion.2
  131.9 1.6 pad_maximum_fusion.1.pair_ref
  133.5 6.4 %pack_copied.1 = (bf16[8,2,128,256]{3,2,1,0:T(8,128)(2,1)S(1)}, bf16[8,2,128,256]{3,2,1,0:T(8,128)(2,1)}, bf16[8,2,128,256]{3,2,1,0:T(8,128)(2,1)}, bf16[4,2,128...) custom-call(s32[128]{0:T(128)S(1)} %reshape.312.table_ref, s32[32]{0:T(128)S(1)} %concatenate.28.dest_ref, ...), custom_call_target="tpu_custom_call" | custom-call | tf_op jit(solution)/shard_map/pack_copied/pallas_call | solution.py:54
  139.9 1.0 copy-done.2
  140.9 10.5 %collective-permute-done.27.refs_4_ = bf16[4,2,128,256]{3,2,1,0:T(8,128)(2,1)S(1)} collective-permute-done((bf16[4,2,128,256]{3,2,1,0:T(8,128)(2,1)S(1)}, bf16[4,2,128,256]{3,2,1,0:T(8,128)(2,1)S(1)}, u32[]{:S(2)}, u32[]{:S(2)}) %collective-permute-start.27) | collective-permute-done | bytes 524320 | tf_op jit(solution)/shard_map/ppermute | solution.py:390
  151.5 2.3 merge_own.1
  153.8 7.2 %all-to-all-start = ((bf16[8,4,2,128,256]{4,3,2,1,0:T(8,128)(2,1)}), bf16[8,4,2,128,256]{4,3,2,1,0:T(8,128)(2,1)}, u32[]{:S(2)}, u32[]{:S(2)}) async-start(bf16[8,4,2,128,256]{4,3,2,1,0:T(8,128)(2,1)} %merge_own.1), calls=%async_computation | async-start | bytes 8388608 | tf_op jit(solution)/shard_map/all_to_all | solution.py:405
  161.1 2.1 fusion.34
  163.2 2.2 collective-permute-start.23
  165.5 2.7 collective-permute-start.19
  168.2 1.7 fusion.32
  170.0 2.9 collective-permute-start.22
  172.9 1.7 fusion.6
  174.6 1.4 collective-permute-start.20
  176.0 2.3 collective-permute-start.21
  178.3 2.1 fusion.5.q_ref
  180.4 12.1 %collective-permute-done.22 = bf16[128,1024]{1,0:T(8,128)(2,1)S(1)} collective-permute-done((bf16[128,1024]{1,0:T(8,128)(2,1)S(1)}, bf16[128,1024]{1,0:T(8,128)(2,1)S(1)}, u32[]{:S(2)}, u32[]{:S(2)}) %collective-permute-start.22) | collective-permute-done | bytes 262176 | tf_op jit(solution)/shard_map/ppermute | solution.py:384
  192.8 1.0 slice.74.first_ref
  193.8 9.4 %near_attend.1 = (f32[32,128,128]{2,1,0:T(8,128)S(1)}, f32[32,8,128]{2,1,0:T(8,128)S(1)}) custom-call(s32[2]{0:T(128)S(1)} %add_convert_fusion.edge_ref, bf16[1024,512]{1,0:T(8,128)(2,1)S(1)} %fusion.5.q_ref, bf16[1280,1024]{1,0:T(8,128)(2,1)S(1)} %pad_maximum_fusion.kv_ref, bf16[128,1024]{1,0:T(8,128)(2,1)S(1)} %slice.74.first_ref), custom_call_target="tpu_custom_call" | custom-call | tf_op jit(solution)/shard_map/near_attend/pallas_call | solution.py:155
  203.2 2.9 collective-permute-done.20.refs_3_
  206.2 2.3 merge_copied.1
  208.5 4.3 %all-to-all-done = bf16[8,4,2,128,256]{4,3,2,1,0:T(8,128)(2,1)} async-done(((bf16[8,4,2,128,256]{4,3,2,1,0:T(8,128)(2,1)}), bf16[8,4,2,128,256]{4,3,2,1,0:T(8,128)(2,1)}, u32[]{:S(2)}, u32[]{:S(2)}) %all-to-all-start) | async-done | bytes 4194336 | tf_op jit(solution)/shard_map/all_to_all | solution.py:405
  212.8 13.9 %all-to-all-start.1 = ((bf16[8,4,2,128,256]{4,3,2,1,0:T(8,128)(2,1)}), bf16[8,4,2,128,256]{4,3,2,1,0:T(8,128)(2,1)}, u32[]{:S(2)}, u32[]{:S(2)}) async-start(bf16[8,4,2,128,256]{4,3,2,1,0:T(8,128)(2,1)} %merge_copied.1), calls=%async_computation.1 | async-start | bytes 8388608 | tf_op jit(solution)/shard_map/all_to_all | solution.py:405
  227.0 1.2 copy.27
  228.9 46.8 %all-to-all-done.1 = bf16[8,4,2,128,256]{4,3,2,1,0:T(8,128)(2,1)} async-done(((bf16[8,4,2,128,256]{4,3,2,1,0:T(8,128)(2,1)}), bf16[8,4,2,128,256]{4,3,2,1,0:T(8,128)(2,1)}, u32[]{:S(2)}, u32[]{:S(2)}) %all-to-all-start.1) | async-done | bytes 4194336 | tf_op jit(solution)/shard_map/all_to_all | solution.py:405
  275.6 12.2 %rand_attend.1 = bf16[64,128,128]{2,1,0:T(8,128)(2,1)S(1)} custom-call(s32[128]{0:T(128)S(1)} %fusion.69.slot_ref, s32[32]{0:T(128)S(1)} %reshape.311.count_ref, s32[32]{0:T(128)S(1)} %select_reduce_fusion.4.target_ref, bf16[1024,512]{1,0:T(8,128)(2,1)S(1)} %fusion.5.q_ref, f32[32,128,128]{2,1,0:T(8,128)S(1)} %get-tuple-element.40.acc_ref, ...), custom_call_target="tpu_custom_call" | custom-call | tf_op jit(solution)/shard_map/rand_attend/pallas_call | solution.py:230
  287.8 1.3 copy-done.1
  289.2 5.0 %all-to-all-start.2 = ((bf16[64,128,128]{2,1,0:T(8,128)(2,1)}), bf16[64,128,128]{2,1,0:T(8,128)(2,1)S(1)}, u32[]{:S(2)}, u32[]{:S(2)}) async-start(bf16[64,128,128]{2,1,0:T(8,128)(2,1)} %copy-done.1), calls=%async_computation.2 | async-start | bytes 4194304 | tf_op jit(solution)/shard_map/all_to_all | solution.py:429
  294.3 51.3 %all-to-all-done.2.in_ref = bf16[64,128,128]{2,1,0:T(8,128)(2,1)S(1)} async-done(((bf16[64,128,128]{2,1,0:T(8,128)(2,1)}), bf16[64,128,128]{2,1,0:T(8,128)(2,1)S(1)}, u32[]{:S(2)}, u32[]{:S(2)}) %all-to-all-start.2) | async-done | bytes 2097184 | tf_op jit(solution)/shard_map/all_to_all | solution.py:429
  345.5 1.8 take_tiles.1
  (100 shorter events, 7.5 us)
Async XLA Ops:
  0.0 226.7 %copy-start = (s32[4,512]{1,0:T(4,128)S(1)}, s32[4,512]{1,0:T(4,128)}, u32[]{:S(2)}) copy-start(s32[4,512]{1,0:T(4,128)} %param.9) | copy-start | bytes 24580
  0.0 29.3 %copy-start.4 = (bf16[1024,512]{1,0:T(8,128)(2,1)S(1)}, bf16[1024,512]{1,0:T(8,128)(2,1)}, u32[]{:S(2)}) copy-start(bf16[1024,512]{1,0:T(8,128)(2,1)} %param.5) | copy-start | bytes 3145732
  1.0 8.0 %collective-permute-start.5 = (bf16[128,512]{1,0:T(8,128)(2,1)S(1)}, bf16[128,512]{1,0:T(8,128)(2,1)S(1)}, u32[]{:S(2)}, u32[]{:S(2)}) collective-permute-start(bf16[128,512]{1,0:T(8,128)(2,1)S(1)} %slice_select_fusion), channel_id=1, source_target_pairs={{0,128},{1,129},{2,130},{3,131}} | collective-permute-start | bytes 393224 | tf_op jit(solution)/shard_map/ppermute | solution.py:346
  1.7 7.3 %collective-permute-start.6 = (bf16[128,512]{1,0:T(8,128)(2,1)S(1)}, bf16[128,512]{1,0:T(8,128)(2,1)S(1)}, u32[]{:S(2)}, u32[]{:S(2)}) collective-permute-start(bf16[128,512]{1,0:T(8,128)(2,1)S(1)} %slice_select_fusion), channel_id=1, source_target_pairs={{0,192},{1,193},{2,194},{3,195}} | collective-permute-start | bytes 393224 | tf_op jit(solution)/shard_map/ppermute | solution.py:346
  2.4 6.6 %collective-permute-start.4 = (bf16[128,512]{1,0:T(8,128)(2,1)S(1)}, bf16[128,512]{1,0:T(8,128)(2,1)S(1)}, u32[]{:S(2)}, u32[]{:S(2)}) collective-permute-start(bf16[128,512]{1,0:T(8,128)(2,1)S(1)} %slice_select_fusion), channel_id=1, source_target_pairs={{0,64},{1,65},{2,66},{3,67}} | collective-permute-start | bytes 393224 | tf_op jit(solution)/shard_map/ppermute | solution.py:346
  3.0 33.9 %collective-permute-start.2 = (bf16[1024,512]{1,0:T(8,128)(2,1)}, bf16[1024,512]{1,0:T(8,128)(2,1)}, u32[]{:S(2)}, u32[]{:S(2)}) collective-permute-start(bf16[1024,512]{1,0:T(8,128)(2,1)} %param.5), channel_id=1, source_target_pairs={{1,0},{2,1},{3,2},{0,3},{5,4},{6,5},{7,6},{4,7},{9,8},{10,9},{11,1... | collective-permute-start | bytes 3145736 | tf_op jit(solution)/shard_map/ppermute | solution.py:356
  6.7 34.4 %collective-permute-start = (bf16[1024,512]{1,0:T(8,128)(2,1)}, bf16[1024,512]{1,0:T(8,128)(2,1)S(1)}, u32[]{:S(2)}, u32[]{:S(2)}) collective-permute-start(bf16[1024,512]{1,0:T(8,128)(2,1)} %param.5), channel_id=1, source_target_pairs={{0,1},{1,2},{2,3},{3,0},{4,5},{5,6},{6,7},{7,4},{8,9},{9,10},{10,1... | collective-permute-start | bytes 3145736 | tf_op jit(solution)/shard_map/ppermute | solution.py:355
  7.8 29.2 %copy-start.5 = (s32[4,64,8,4]{2,1,3,0:T(8,128)}, s32[4,64,8,4]{2,1,3,0:T(8,128)S(1)}, u32[]{:S(2)}) copy-start(s32[4,64,8,4]{2,1,3,0:T(8,128)S(1)} %reshape.309) | copy-start | bytes 98308
  9.9 2.1 collective-permute-start.9
  10.6 1.4 collective-permute-start.8
  11.3 0.7 collective-permute-start.7
  12.1 3.6 %collective-permute-start.12 = (bf16[128,512]{1,0:T(8,128)(2,1)S(1)}, bf16[128,512]{1,0:T(8,128)(2,1)S(1)}, u32[]{:S(2)}, u32[]{:S(2)}) collective-permute-start(bf16[128,512]{1,0:T(8,128)(2,1)S(1)} %add_add_fusion.1), channel_id=1, source_target_pairs={{0,12},{16,28},{32,44},{48,60},{64,76},{80,92},{96,108},{112,124},... | collective-permute-start | bytes 393224 | tf_op jit(solution)/shard_map/ppermute | solution.py:346
  12.7 2.9 collective-permute-start.11
  13.4 15.9 %collective-permute-start.10 = (bf16[128,512]{1,0:T(8,128)(2,1)S(1)}, bf16[128,512]{1,0:T(8,128)(2,1)S(1)}, u32[]{:S(2)}, u32[]{:S(2)}) collective-permute-start(bf16[128,512]{1,0:T(8,128)(2,1)S(1)} %add_add_fusion.1), channel_id=1, source_target_pairs={{0,4},{16,20},{32,36},{48,52},{64,68},{80,84},{96,100},{112,116},{... | collective-permute-start | bytes 393224 | tf_op jit(solution)/shard_map/ppermute | solution.py:346
  29.3 51.1 %collective-permute-start.13 = (bf16[1024,512]{1,0:T(8,128)(2,1)S(1)}, bf16[1024,512]{1,0:T(8,128)(2,1)}, u32[]{:S(2)}, u32[]{:S(2)}) collective-permute-start(bf16[1024,512]{1,0:T(8,128)(2,1)S(1)} %copy-done.4), channel_id=1, source_target_pairs={{0,32},{4,36},{8,40},{12,44},{16,48},{20,52},{24,56},{28,60},{32,0... | collective-permute-start | bytes 3145736 | tf_op jit(solution)/shard_map/ppermute | solution.py:377
  34.3 52.0 %slice-start = ((s8[6291456]{0:T(1024)(128)(4,1)}), s8[4194304]{0:T(1024)(128)(4,1)S(1)}, s32[]{:S(2)}) async-start(s8[6291456]{0:T(1024)(128)(4,1)} %bitcast.64), calls=%async_computation.3 | async-start | bytes 8388608
  38.1 51.6 %collective-permute-start.3 = (bf16[512,512]{1,0:T(8,128)(2,1)S(1)}, bf16[512,512]{1,0:T(8,128)(2,1)S(1)}, u32[]{:S(2)}, u32[]{:S(2)}) collective-permute-start(bf16[512,512]{1,0:T(8,128)(2,1)S(1)} %slice.65), channel_id=1, source_target_pairs={{1,0},{2,1},{3,2},{0,3},{5,4},{6,5},{7,6},{4,7},{9,8},{10,9},{11,1... | collective-permute-start | bytes 1572872 | tf_op jit(solution)/shard_map/ppermute | solution.py:358
  41.2 45.2 %slice-start.1 = ((s8[6291456]{0:T(1024)(128)(4,1)}), s8[2097152]{0:T(1024)(128)(4,1)S(1)}, s32[]{:S(2)}) async-start(s8[6291456]{0:T(1024)(128)(4,1)} %bitcast.64), calls=%async_computation.4 | async-start | bytes 4194304
  41.2 47.7 %collective-permute-start.1 = (bf16[512,512]{1,0:T(8,128)(2,1)S(1)}, bf16[512,512]{1,0:T(8,128)(2,1)S(1)}, u32[]{:S(2)}, u32[]{:S(2)}) collective-permute-start(bf16[512,512]{1,0:T(8,128)(2,1)S(1)} %slice.64), channel_id=1, source_target_pairs={{0,1},{1,2},{2,3},{3,0},{4,5},{5,6},{6,7},{7,4},{8,9},{9,10},{10,1... | collective-permute-start | bytes 1572872 | tf_op jit(solution)/shard_map/ppermute | solution.py:357
  83.4 27.2 %collective-permute-start.15 = (bf16[1152,512]{1,0:T(8,128)(2,1)}, bf16[1152,512]{1,0:T(8,128)(2,1)}, u32[]{:S(2)}, u32[]{:S(2)}) collective-permute-start(bf16[1152,512]{1,0:T(8,128)(2,1)} %constant_dynamic-update-slice_fusion), channel_id=1, source_target_pairs={{1,0},{2,1},{3,2},{0,3},{5,4},{6,5},{7,6},{4,7},{9,8},{10,9},{11,1... | collective-permute-start | bytes 3538952 | tf_op jit(solution)/shard_map/ppermute | solution.py:356
  86.4 28.8 %collective-permute-start.14 = (bf16[1152,512]{1,0:T(8,128)(2,1)}, bf16[1152,512]{1,0:T(8,128)(2,1)}, u32[]{:S(2)}, u32[]{:S(2)}) collective-permute-start(bf16[1152,512]{1,0:T(8,128)(2,1)} %constant_dynamic-update-slice_fusion), channel_id=1, source_target_pairs={{0,1},{1,2},{2,3},{3,0},{4,5},{5,6},{6,7},{7,4},{8,9},{9,10},{10,1... | collective-permute-start | bytes 3538952 | tf_op jit(solution)/shard_map/ppermute | solution.py:355
  88.9 1.5 copy-start.9
  89.6 0.8 copy-start.7
  101.1 39.8 %collective-permute-start.26 = (bf16[4,2,128,256]{3,2,1,0:T(8,128)(2,1)S(1)}, bf16[4,2,128,256]{3,2,1,0:T(8,128)(2,1)S(1)}, u32[]{:S(2)}, u32[]{:S(2)}) collective-permute-start(bf16[4,2,128,256]{3,2,1,0:T(8,128)(2,1)S(1)} %get-tuple-element.45), channel_id=1, source_target_pairs={{0,16},{4,20},{8,24},{12,28},{16,32},{20,36},{24,40},{28,44},{32,4... | collective-permute-start | bytes 1572872 | tf_op jit(solution)/shard_map/ppermute | solution.py:390
  101.2 50.2 %collective-permute-start.24 = (bf16[8,2,128,256]{3,2,1,0:T(8,128)(2,1)S(1)}, bf16[8,2,128,256]{3,2,1,0:T(8,128)(2,1)S(1)}, u32[]{:S(2)}, u32[]{:S(2)}) collective-permute-start(bf16[8,2,128,256]{3,2,1,0:T(8,128)(2,1)S(1)} %get-tuple-element.43), channel_id=1, source_target_pairs={{0,8},{4,12},{8,16},{12,20},{16,24},{20,28},{24,32},{28,36},{32,40... | collective-permute-start | bytes 3145736 | tf_op jit(solution)/shard_map/ppermute | solution.py:390
  104.1 47.3 %collective-permute-start.25 = (bf16[8,2,128,256]{3,2,1,0:T(8,128)(2,1)S(1)}, bf16[8,2,128,256]{3,2,1,0:T(8,128)(2,1)S(1)}, u32[]{:S(2)}, u32[]{:S(2)}) collective-permute-start(bf16[8,2,128,256]{3,2,1,0:T(8,128)(2,1)S(1)} %get-tuple-element.44), channel_id=1, source_target_pairs={{0,56},{4,60},{8,0},{12,4},{16,8},{20,12},{24,16},{28,20},{32,24},... | collective-permute-start | bytes 3145736 | tf_op jit(solution)/shard_map/ppermute | solution.py:390
  111.7 13.8 %collective-permute-start.17 = (bf16[576,512]{1,0:T(8,128)(2,1)S(1)}, bf16[576,512]{1,0:T(8,128)(2,1)S(1)}, u32[]{:S(2)}, u32[]{:S(2)}) collective-permute-start(bf16[576,512]{1,0:T(8,128)(2,1)S(1)} %slice.69), channel_id=1, source_target_pairs={{1,0},{2,1},{3,2},{0,3},{5,4},{6,5},{7,6},{4,7},{9,8},{10,9},{11,1... | collective-permute-start | bytes 1769480 | tf_op jit(solution)/shard_map/ppermute | solution.py:358
  116.3 13.6 %collective-permute-start.16 = (bf16[576,512]{1,0:T(8,128)(2,1)S(1)}, bf16[576,512]{1,0:T(8,128)(2,1)S(1)}, u32[]{:S(2)}, u32[]{:S(2)}) collective-permute-start(bf16[576,512]{1,0:T(8,128)(2,1)S(1)} %slice.67), channel_id=1, source_target_pairs={{0,1},{1,2},{2,3},{3,0},{4,5},{5,6},{6,7},{7,4},{8,9},{9,10},{10,1... | collective-permute-start | bytes 1769480 | tf_op jit(solution)/shard_map/ppermute | solution.py:357
  125.6 25.9 %collective-permute-start.27 = (bf16[4,2,128,256]{3,2,1,0:T(8,128)(2,1)S(1)}, bf16[4,2,128,256]{3,2,1,0:T(8,128)(2,1)S(1)}, u32[]{:S(2)}, u32[]{:S(2)}) collective-permute-start(bf16[4,2,128,256]{3,2,1,0:T(8,128)(2,1)S(1)} %get-tuple-element.46), channel_id=1, source_target_pairs={{0,48},{4,52},{8,56},{12,60},{16,0},{20,4},{24,8},{28,12},{32,16},... | collective-permute-start | bytes 1572872 | tf_op jit(solution)/shard_map/ppermute | solution.py:390
  127.6 4.3 %copy-start.6 = (bf16[576,1024]{1,0:T(8,128)(2,1)}, bf16[576,1024]{1,0:T(8,128)(2,1)S(1)}, u32[]{:S(2)}) copy-start(bf16[576,1024]{1,0:T(8,128)(2,1)S(1)} %fusion.1) | copy-start | bytes 3538948
  139.9 1.0 copy-start.2
  153.8 59.0 %all-to-all-start = ((bf16[8,4,2,128,256]{4,3,2,1,0:T(8,128)(2,1)}), bf16[8,4,2,128,256]{4,3,2,1,0:T(8,128)(2,1)}, u32[]{:S(2)}, u32[]{:S(2)}) async-start(bf16[8,4,2,128,256]{4,3,2,1,0:T(8,128)(2,1)} %merge_own.1), calls=%async_computation | async-start | bytes 8388608 | tf_op jit(solution)/shard_map/all_to_all | solution.py:405
  163.2 9.6 %copy-start.8 = (bf16[512,512]{1,0:T(8,128)(2,1)S(1)}, bf16[512,512]{1,0:T(8,128)(2,1)}, u32[]{:S(2)}) copy-start(bf16[512,512]{1,0:T(8,128)(2,1)} %copy-done.7) | copy-start | bytes 1572868
  163.2 9.6 %copy-start.10 = (bf16[512,512]{1,0:T(8,128)(2,1)S(1)}, bf16[512,512]{1,0:T(8,128)(2,1)}, u32[]{:S(2)}) copy-start(bf16[512,512]{1,0:T(8,128)(2,1)} %copy-done.9) | copy-start | bytes 1572868
  163.2 12.7 %collective-permute-start.23 = (bf16[128,1024]{1,0:T(8,128)(2,1)S(1)}, bf16[128,1024]{1,0:T(8,128)(2,1)S(1)}, u32[]{:S(2)}, u32[]{:S(2)}) collective-permute-start(bf16[128,1024]{1,0:T(8,128)(2,1)S(1)} %slice.73), channel_id=1, source_target_pairs={{4,0},{8,4},{12,8},{16,12},{20,16},{24,20},{28,24},{32,28},{36,32}... | collective-permute-start | bytes 786440 | tf_op jit(solution)/shard_map/ppermute | solution.py:385
  165.4 40.8 %collective-permute-start.18 = (bf16[8,2,128,256]{3,2,1,0:T(8,128)(2,1)}, bf16[8,2,128,256]{3,2,1,0:T(8,128)(2,1)S(1)}, u32[]{:S(2)}, u32[]{:S(2)}) collective-permute-start(bf16[8,2,128,256]{3,2,1,0:T(8,128)(2,1)} %get-tuple-element.34), channel_id=1, source_target_pairs={{0,8},{4,12},{8,16},{12,20},{16,24},{20,28},{24,32},{28,36},{32,40... | collective-permute-start | bytes 3145736 | tf_op jit(solution)/shard_map/ppermute | solution.py:390
  165.5 40.7 %collective-permute-start.19 = (bf16[8,2,128,256]{3,2,1,0:T(8,128)(2,1)}, bf16[8,2,128,256]{3,2,1,0:T(8,128)(2,1)S(1)}, u32[]{:S(2)}, u32[]{:S(2)}) collective-permute-start(bf16[8,2,128,256]{3,2,1,0:T(8,128)(2,1)} %get-tuple-element.35), channel_id=1, source_target_pairs={{0,56},{4,60},{8,0},{12,4},{16,8},{20,12},{24,16},{28,20},{32,24},... | collective-permute-start | bytes 3145736 | tf_op jit(solution)/shard_map/ppermute | solution.py:390
  170.0 22.6 %collective-permute-start.22 = (bf16[128,1024]{1,0:T(8,128)(2,1)S(1)}, bf16[128,1024]{1,0:T(8,128)(2,1)S(1)}, u32[]{:S(2)}, u32[]{:S(2)}) collective-permute-start(bf16[128,1024]{1,0:T(8,128)(2,1)S(1)} %slice.71), channel_id=1, source_target_pairs={{0,4},{4,8},{8,12},{12,16},{16,20},{20,24},{24,28},{28,32},{32,36}... | collective-permute-start | bytes 786440 | tf_op jit(solution)/shard_map/ppermute | solution.py:384
  174.6 31.5 %collective-permute-start.20 = (bf16[4,2,128,256]{3,2,1,0:T(8,128)(2,1)}, bf16[4,2,128,256]{3,2,1,0:T(8,128)(2,1)S(1)}, u32[]{:S(2)}, u32[]{:S(2)}) collective-permute-start(bf16[4,2,128,256]{3,2,1,0:T(8,128)(2,1)} %get-tuple-element.36), channel_id=1, source_target_pairs={{0,16},{4,20},{8,24},{12,28},{16,32},{20,36},{24,40},{28,44},{32,4... | collective-permute-start | bytes 1572872 | tf_op jit(solution)/shard_map/ppermute | solution.py:390
  176.0 30.2 %collective-permute-start.21 = (bf16[4,2,128,256]{3,2,1,0:T(8,128)(2,1)}, bf16[4,2,128,256]{3,2,1,0:T(8,128)(2,1)S(1)}, u32[]{:S(2)}, u32[]{:S(2)}) collective-permute-start(bf16[4,2,128,256]{3,2,1,0:T(8,128)(2,1)} %get-tuple-element.37), channel_id=1, source_target_pairs={{0,48},{4,52},{8,56},{12,60},{16,0},{20,4},{24,8},{28,12},{32,16},... | collective-permute-start | bytes 1572872 | tf_op jit(solution)/shard_map/ppermute | solution.py:390
  180.4 25.8 %copy-start.3 = (bf16[8,2,128,256]{3,2,1,0:T(8,128)(2,1)S(1)}, bf16[8,2,128,256]{3,2,1,0:T(8,128)(2,1)}, u32[]{:S(2)}) copy-start(bf16[8,2,128,256]{3,2,1,0:T(8,128)(2,1)} %copy-done.2) | copy-start | bytes 3145732
  208.5 20.1 %copy-start.11 = (s32[1,2048]{1,0:T(1,128)S(1)}, s32[1,2048]{1,0:T(1,128)}, u32[]{:S(2)}) copy-start(s32[1,2048]{1,0:T(1,128)} %param.7) | copy-start | bytes 24580
  212.8 62.8 %all-to-all-start.1 = ((bf16[8,4,2,128,256]{4,3,2,1,0:T(8,128)(2,1)}), bf16[8,4,2,128,256]{4,3,2,1,0:T(8,128)(2,1)}, u32[]{:S(2)}, u32[]{:S(2)}) async-start(bf16[8,4,2,128,256]{4,3,2,1,0:T(8,128)(2,1)} %merge_copied.1), calls=%async_computation.1 | async-start | bytes 8388608 | tf_op jit(solution)/shard_map/all_to_all | solution.py:405
  287.8 1.3 copy-start.1
  289.2 56.4 %all-to-all-start.2 = ((bf16[64,128,128]{2,1,0:T(8,128)(2,1)}), bf16[64,128,128]{2,1,0:T(8,128)(2,1)S(1)}, u32[]{:S(2)}, u32[]{:S(2)}) async-start(bf16[64,128,128]{2,1,0:T(8,128)(2,1)} %copy-done.1), calls=%async_computation.2 | async-start | bytes 4194304 | tf_op jit(solution)/shard_map/all_to_all | solution.py:429

commit v2 on v1

--- a/solution.py
+++ b/solution.py
@@ -340,11 +340,8 @@
     def w_query(shift):
         return weight(shift, 0, width)
 
-    def spread(block, stride):
-        holders = range(0, peers, 4 * stride)
-        got = [
-            lax.ppermute(block, "seq", [(h, h + k * stride) for h in holders]) for k in (1, 2, 3)
-        ]
+    def spread(block, holders, stride):
+        got = [lax.ppermute(block, "seq", [(h, h + k * stride) for h in holders]) for k in (1, 2, 3)]
         return block + got[0] + got[1] + got[2]
 
     onward = [(i, (i + 1) % groups) for i in range(groups)]
@@ -372,11 +369,10 @@
     from_low, from_high, far_top, far_bottom = ring(tokens)
     zero = tokens[:blk]
     zero = jnp.where(me == 0, zero, jnp.zeros_like(zero))
-    zero = spread(spread(spread(zero, peers // 4), peers // 16), peers // 64)
+    zero = spread(spread(zero, [0], 4), range(0, 16, 4), 1)
     copied, zero = lax.optimization_barrier((tokens, zero))
     copied = lax.ppermute(copied, "seq", seq_pairs(lambda x, z, c: (x, z + NZ // 2, c)))
-    copied = jnp.concatenate([copied, zero], axis=0)
-    copied_ring = ring(copied)
+    zero = spread(zero, range(16), 16)
 
     pair = keys_values(tokens, from_low, from_high, far_top, far_bottom)
     up = [(i, i + 1) for i in range(peers - 1)]
@@ -407,7 +403,11 @@
         )
         return got.reshape(-1, blk, 2 * hd)
 
-    own_parts = shifted(pack(tables[0], pair, "pack_own"))
+    own_parts = pack(tables[0], pair, "pack_own")
+    copied, zero, _ = lax.optimization_barrier((copied, zero, own_parts))
+    own_parts = shifted(own_parts)
+    copied = jnp.concatenate([copied, zero], axis=0)
+    copied_ring = ring(copied)
     copied_pair = keys_values(copied, *copied_ring)
     copied_parts = pack(tables[1], copied_pair, "pack_copied")
     own_parts, _ = lax.optimization_barrier((own_parts, copied_parts))

time: 349 us -> 352 us (level)
  starting transfers between devices: 65.3 us -> 60 us
  waiting for transfers between devices: 188 us -> 192 us
  matrix products: 28.8 us -> 32.5 us
    ppermute x1, waiting for transfers between devices: 36.6 us -> 13.2 us  [local(): lax.ppermute(copied, 'seq', seq_pairs(lambda x, z, c: (x, z + NZ // 2, c)))]
    ppermute x1, waiting for transfers between devices: 0.01 us -> 19.3 us  [local(): after = lax.ppermute(pair[:blk], 'seq', down)]
    ppermute x2, waiting for transfers between devices: 6.49 us -> 22 us  [ring(): high = lax.ppermute(part, 'head', backward)]
    ppermute x1, waiting for transfers between devices: 12.1 us -> 0.01 us  [local(): before = lax.ppermute(pair[-blk:], 'seq', up)]
    all_to_all x2, starting transfers between devices: 21.1 us -> 16.1 us  [in_plane(): lax.all_to_all(block, 'seq', split_axis=0, concat_axis=0, axis_index_grou...]
    ppermute x1, starting transfers between devices: 4.8 us -> 0.04 us  [local(): lax.ppermute(copied, 'seq', seq_pairs(lambda x, z, c: (x, z + NZ // 2, c)))]
    ppermute x2, waiting for transfers between devices: 1.15 us -> 5.63 us  [ring(): bottom = lax.ppermute(high[middle:], 'head', backward)]
    all_to_all x2, waiting for transfers between devices: 51 us -> 46.8 us  [in_plane(): lax.all_to_all(block, 'seq', split_axis=0, concat_axis=0, axis_index_grou...]
  transfers between devices with their start and end apart: 31 -> 31, of which waited for: 12 -> 14; matrix products, arithmetic and copies ran while one was open for 13% -> 13% of each run, Pallas kernels for 8% -> 8%
where the time goes in v2:
time: 352 us; the launch traced here: 351 us
  waiting for transfers between devices  192 us (55%)
  starting transfers between devices  60 us (17%)
  Pallas kernels  43.5 us (12%)
  matrix products  32.5 us (9%)
  local copies, waits for them, and re-layouts  14.9 us (4%)
  other arithmetic  7.46 us (2%)
    all_to_all x1, waiting for transfers between devices, local(): back = lax.all_to_all(done, 'seq', split_axis=0, concat_axis=0, tiled=True)  51.2 us
    all_to_all x2, waiting for transfers between devices, in_plane(): lax.all_to_all(block, 'seq', split_axis=0, concat_axis=0, axis_index_grou...  46.8 us
    dot_general x14, matrix products, dot(): return jnp.dot(a, b, preferred_element_type=F32)  32.5 us
    ppermute x2, waiting for transfers between devices, ring(): high = lax.ppermute(part, 'head', backward)  22 us
    ppermute x1, waiting for transfers between devices, local(): after = lax.ppermute(pair[:blk], 'seq', down)  19.3 us
    all_to_all x2, starting transfers between devices, in_plane(): lax.all_to_all(block, 'seq', split_axis=0, concat_axis=0, axis_index_grou...  16.1 us
    ppermute x9, waiting for transfers between devices, spread(): lax.ppermute(block, 'seq', [(h, h + k * stride) for h in holders])  16 us
    pallas_call x2, Pallas kernels, pack_tiles(): pl.pallas_call(kernel, out_shape=[jax.ShapeDtypeStruct((share, 2, blk, 2...  15.6 us
  transfers between devices with their start and end apart: 31, of which 14 were waited for; matrix products, arithmetic and copies ran while one was open for 13% of the time, Pallas kernels for 8%

profile of v2, /device:TPU:1, one launch (start us, length us, event | category | flops | bytes accessed | tf_op | source)
XLA Modules:
  0.0 351.2 jit_solution(16828355097286161070)
XLA Ops:
  0.0 0.9 slice_select_fusion
  3.0 3.6 %collective-permute-start.2 = (bf16[1024,512]{1,0:T(8,128)(2,1)}, bf16[1024,512]{1,0:T(8,128)(2,1)S(1)}, u32[]{:S(2)}, u32[]{:S(2)}) collective-permute-start(bf16[1024,512]{1,0:T(8,128)(2,1)} %param.5), channel_id=1, source_target_pairs={{1,0},{2,1},{3,2},{0,3},{5,4},{6,5},{7,6},{4,7},{9,8},{10,9},{11,1... | collective-permute-start | bytes 3145736 | tf_op jit(solution)/shard_map/ppermute | solution.py:353
  6.7 1.1 reshape.309
  8.2 4.8 %fusion.16 = f32[1024,1024]{0,1:T(8,128)} fusion(bf16[1024,512]{1,0:T(8,128)(2,1)} %param.5, bf16[2048,1536]{1,0:T(8,128)(2,1)} %param.6, s32[]{:T(128)S(6)} %select_n.427), kind=kOutput, calls=%fused_computation.29 | convolution fusion | flops 1073741824 | bytes 6291460 | tf_op jit(solution)/shard_map/dot_general | solution.py:17
  13.7 0.9 add_add_fusion.2
  16.0 1.3 collective-permute-start.7
  17.4 12.6 %collective-permute-done.7 = bf16[128,512]{1,0:T(8,128)(2,1)S(1)} collective-permute-done((bf16[128,512]{1,0:T(8,128)(2,1)S(1)}, bf16[128,512]{1,0:T(8,128)(2,1)S(1)}, u32[]{:S(2)}, u32[]{:S(2)}) %collective-permute-start.7) | collective-permute-done | bytes 131104 | tf_op jit(solution)/shard_map/ppermute | solution.py:344
  30.1 1.3 collective-permute-start.13
  31.4 1.3 collective-permute-start.12
  32.7 1.3 collective-permute-start.11
  35.4 2.8 collective-permute-done.11
  38.3 3.0 collective-permute-start.3
  41.5 2.7 fusion.13
  44.3 2.6 add_bitcast_fusion
  46.8 4.8 %collective-permute-done.3 = bf16[512,512]{1,0:T(8,128)(2,1)S(1)} collective-permute-done((bf16[512,512]{1,0:T(8,128)(2,1)S(1)}, bf16[512,512]{1,0:T(8,128)(2,1)S(1)}, u32[]{:S(2)}, u32[]{:S(2)}) %collective-permute-start.3) | collective-permute-done | bytes 524320 | tf_op jit(solution)/shard_map/ppermute | solution.py:355
  51.6 2.2 fusion.2
  53.8 1.1 collective-permute-done.1
  54.9 2.2 fusion.3
  57.1 1.0 copy-done.16
  58.1 1.5 pad_maximum_fusion.2.pair_ref
  59.6 9.2 %pack_own.1 = (bf16[8,2,128,256]{3,2,1,0:T(8,128)(2,1)S(1)}, bf16[8,2,128,256]{3,2,1,0:T(8,128)(2,1)S(1)}, bf16[8,2,128,256]{3,2,1,0:T(8,128)(2,1)S(1)}, bf16[4,...) custom-call(s32[128]{0:T(128)S(1)} %reshape.313.table_ref, s32[32]{0:T(128)S(1)} %concatenate.28.dest_ref, ...), custom_call_target="tpu_custom_call" | custom-call | tf_op jit(solution)/shard_map/pack_own/pallas_call | solution.py:54
  68.8 0.8 copy-done.6
  69.6 0.8 copy-done.10
  70.4 13.2 %collective-permute-done.10 = bf16[1024,512]{1,0:T(8,128)(2,1)S(1)} collective-permute-done((bf16[1024,512]{1,0:T(8,128)(2,1)}, bf16[1024,512]{1,0:T(8,128)(2,1)S(1)}, u32[]{:S(2)}, u32[]{:S(2)}) %collective-permute-start.10) | collective-permute-done | bytes 1048608 | tf_op jit(solution)/shard_map/ppermute | solution.py:374
  83.6 1.1 constant_dynamic-update-slice_fusion.1
  85.3 3.0 collective-permute-start.15
  88.7 2.7 collective-permute-start.25
  91.3 22.0 %collective-permute-done.15 = bf16[1152,512]{1,0:T(8,128)(2,1)} collective-permute-done((bf16[1152,512]{1,0:T(8,128)(2,1)}, bf16[1152,512]{1,0:T(8,128)(2,1)}, u32[]{:S(2)}, u32[]{:S(2)}) %collective-permute-start.15) | collective-permute-done | bytes 1179680 | tf_op jit(solution)/shard_map/ppermute | solution.py:353
  113.4 1.1 slice.71
  114.5 3.5 collective-permute-start.17
  118.0 1.1 slice.69
  119.2 3.1 fusion.11
  122.3 3.2 convolution_add_fusion.1
  125.6 2.8 convolution_add_fusion
  128.4 0.9 collective-permute-done.17
  130.1 3.5 collective-permute-done.16
  134.4 1.6 pad_maximum_fusion.1.pair_ref
  136.0 6.4 %pack_copied.1 = (bf16[8,2,128,256]{3,2,1,0:T(8,128)(2,1)S(1)}, bf16[8,2,128,256]{3,2,1,0:T(8,128)(2,1)}, bf16[8,2,128,256]{3,2,1,0:T(8,128)(2,1)}, bf16[4,2,128...) custom-call(s32[128]{0:T(128)S(1)} %reshape.312.table_ref, s32[32]{0:T(128)S(1)} %concatenate.28.dest_ref, ...), custom_call_target="tpu_custom_call" | custom-call | tf_op jit(solution)/shard_map/pack_copied/pallas_call | solution.py:54
  142.4 1.0 copy-done.2
  143.4 0.8 copy-done.4
  145.0 8.3 %collective-permute-done.27.refs_4_ = bf16[4,2,128,256]{3,2,1,0:T(8,128)(2,1)S(1)} collective-permute-done((bf16[4,2,128,256]{3,2,1,0:T(8,128)(2,1)S(1)}, bf16[4,2,128,256]{3,2,1,0:T(8,128)(2,1)S(1)}, u32[]{:S(2)}, u32[]{:S(2)}) %collective-permute-start.27) | collective-permute-done | bytes 524320 | tf_op jit(solution)/shard_map/ppermute | solution.py:386
  153.3 2.3 merge_own.1
  155.7 6.2 %all-to-all-start = ((bf16[8,4,2,128,256]{4,3,2,1,0:T(8,128)(2,1)}), bf16[8,4,2,128,256]{4,3,2,1,0:T(8,128)(2,1)}, u32[]{:S(2)}, u32[]{:S(2)}) async-start(bf16[8,4,2,128,256]{4,3,2,1,0:T(8,128)(2,1)} %merge_own.1), calls=%async_computation | async-start | bytes 8388608 | tf_op jit(solution)/shard_map/all_to_all | solution.py:401
  161.9 2.2 fusion.32
  164.2 2.2 collective-permute-start.22
  166.9 3.7 %collective-permute-start.19 = (bf16[8,2,128,256]{3,2,1,0:T(8,128)(2,1)}, bf16[8,2,128,256]{3,2,1,0:T(8,128)(2,1)S(1)}, u32[]{:S(2)}, u32[]{:S(2)}) collective-permute-start(bf16[8,2,128,256]{3,2,1,0:T(8,128)(2,1)} %get-tuple-element.44), channel_id=1, source_target_pairs={{0,56},{4,60},{8,0},{12,4},{16,8},{20,12},{24,16},{28,20},{32,24},... | collective-permute-start | bytes 3145736 | tf_op jit(solution)/shard_map/ppermute | solution.py:386
  170.6 1.7 fusion.30
  172.4 1.9 collective-permute-start.23
  174.3 1.8 fusion.5
  176.2 3.5 %collective-permute-start.21 = (bf16[4,2,128,256]{3,2,1,0:T(8,128)(2,1)S(1)}, bf16[4,2,128,256]{3,2,1,0:T(8,128)(2,1)S(1)}, u32[]{:S(2)}, u32[]{:S(2)}) collective-permute-start(bf16[4,2,128,256]{3,2,1,0:T(8,128)(2,1)S(1)} %copy-done.5), channel_id=1, source_target_pairs={{0,48},{4,52},{8,56},{12,60},{16,0},{20,4},{24,8},{28,12},{32,16},... | collective-permute-start | bytes 1572872 | tf_op jit(solution)/shard_map/ppermute | solution.py:386
  179.7 1.8 fusion.4.q_ref
  181.5 19.3 %collective-permute-done.23 = bf16[128,1024]{1,0:T(8,128)(2,1)S(1)} collective-permute-done((bf16[128,1024]{1,0:T(8,128)(2,1)S(1)}, bf16[128,1024]{1,0:T(8,128)(2,1)S(1)}, u32[]{:S(2)}, u32[]{:S(2)}) %collective-permute-start.23) | collective-permute-done | bytes 262176 | tf_op jit(solution)/shard_map/ppermute | solution.py:381
  201.1 1.0 slice.74.first_ref
  202.1 9.4 %near_attend.1 = (f32[32,128,128]{2,1,0:T(8,128)S(1)}, f32[32,8,128]{2,1,0:T(8,128)S(1)}) custom-call(s32[2]{0:T(128)S(1)} %add_convert_fusion.edge_ref, bf16[1024,512]{1,0:T(8,128)(2,1)S(1)} %fusion.4.q_ref, bf16[1280,1024]{1,0:T(8,128)(2,1)S(1)} %pad_maximum_fusion.kv_ref, bf16[128,1024]{1,0:T(8,128)(2,1)S(1)} %slice.74.first_ref), custom_call_target="tpu_custom_call" | custom-call | tf_op jit(solution)/shard_map/near_attend/pallas_call | solution.py:155
  211.5 4.6 %collective-permute-done.21.refs_4_ = bf16[4,2,128,256]{3,2,1,0:T(8,128)(2,1)S(1)} collective-permute-done((bf16[4,2,128,256]{3,2,1,0:T(8,128)(2,1)S(1)}, bf16[4,2,128,256]{3,2,1,0:T(8,128)(2,1)S(1)}, u32[]{:S(2)}, u32[]{:S(2)}) %collective-permute-start.21) | collective-permute-done | bytes 524320 | tf_op jit(solution)/shard_map/ppermute | solution.py:386
  216.1 2.2 merge_copied.1
  218.4 9.9 %all-to-all-start.1 = ((bf16[8,4,2,128,256]{4,3,2,1,0:T(8,128)(2,1)}), bf16[8,4,2,128,256]{4,3,2,1,0:T(8,128)(2,1)}, u32[]{:S(2)}, u32[]{:S(2)}) async-start(bf16[8,4,2,128,256]{4,3,2,1,0:T(8,128)(2,1)} %merge_copied.1), calls=%async_computation.1 | async-start | bytes 8388608 | tf_op jit(solution)/shard_map/all_to_all | solution.py:401
  228.5 1.2 copy.27
  230.5 46.8 %all-to-all-done.1 = bf16[8,4,2,128,256]{4,3,2,1,0:T(8,128)(2,1)} async-done(((bf16[8,4,2,128,256]{4,3,2,1,0:T(8,128)(2,1)}), bf16[8,4,2,128,256]{4,3,2,1,0:T(8,128)(2,1)}, u32[]{:S(2)}, u32[]{:S(2)}) %all-to-all-start.1) | async-done | bytes 4194336 | tf_op jit(solution)/shard_map/all_to_all | solution.py:401
  277.2 12.2 %rand_attend.1 = bf16[64,128,128]{2,1,0:T(8,128)(2,1)S(1)} custom-call(s32[128]{0:T(128)S(1)} %fusion.67.slot_ref, s32[32]{0:T(128)S(1)} %reshape.311.count_ref, s32[32]{0:T(128)S(1)} %select_reduce_fusion.4.target_ref, bf16[1024,512]{1,0:T(8,128)(2,1)S(1)} %fusion.4.q_ref, f32[32,128,128]{2,1,0:T(8,128)S(1)} %get-tuple-element.49.acc_ref, ...), custom_call_target="tpu_custom_call" | custom-call | tf_op jit(solution)/shard_map/rand_attend/pallas_call | solution.py:230
  289.4 1.3 copy-done.1
  290.7 7.2 %all-to-all-start.2 = ((bf16[64,128,128]{2,1,0:T(8,128)(2,1)}), bf16[64,128,128]{2,1,0:T(8,128)(2,1)S(1)}, u32[]{:S(2)}, u32[]{:S(2)}) async-start(bf16[64,128,128]{2,1,0:T(8,128)(2,1)} %copy-done.1), calls=%async_computation.2 | async-start | bytes 4194304 | tf_op jit(solution)/shard_map/all_to_all | solution.py:429
  298.1 51.2 %all-to-all-done.2.in_ref = bf16[64,128,128]{2,1,0:T(8,128)(2,1)S(1)} async-done(((bf16[64,128,128]{2,1,0:T(8,128)(2,1)}), bf16[64,128,128]{2,1,0:T(8,128)(2,1)S(1)}, u32[]{:S(2)}, u32[]{:S(2)}) %all-to-all-start.2) | async-done | bytes 2097184 | tf_op jit(solution)/shard_map/all_to_all | solution.py:429
  349.2 1.8 take_tiles.1
  (130 shorter events, 11.6 us)
Async XLA Ops:
  0.0 228.3 %copy-start = (s32[4,512]{1,0:T(4,128)S(1)}, s32[4,512]{1,0:T(4,128)}, u32[]{:S(2)}) copy-start(s32[4,512]{1,0:T(4,128)} %param.9) | copy-start | bytes 24580
  0.9 12.8 %collective-permute-start.5 = (bf16[128,512]{1,0:T(8,128)(2,1)S(1)}, bf16[128,512]{1,0:T(8,128)(2,1)S(1)}, u32[]{:S(2)}, u32[]{:S(2)}) collective-permute-start(bf16[128,512]{1,0:T(8,128)(2,1)S(1)} %slice_select_fusion), channel_id=1, source_target_pairs={{0,32},{1,33},{2,34},{3,35}} | collective-permute-start | bytes 393224 | tf_op jit(solution)/shard_map/ppermute | solution.py:344
  1.6 12.1 %collective-permute-start.6 = (bf16[128,512]{1,0:T(8,128)(2,1)S(1)}, bf16[128,512]{1,0:T(8,128)(2,1)S(1)}, u32[]{:S(2)}, u32[]{:S(2)}) collective-permute-start(bf16[128,512]{1,0:T(8,128)(2,1)S(1)} %slice_select_fusion), channel_id=1, source_target_pairs={{0,48},{1,49},{2,50},{3,51}} | collective-permute-start | bytes 393224 | tf_op jit(solution)/shard_map/ppermute | solution.py:344
  2.3 11.4 %collective-permute-start.4 = (bf16[128,512]{1,0:T(8,128)(2,1)S(1)}, bf16[128,512]{1,0:T(8,128)(2,1)S(1)}, u32[]{:S(2)}, u32[]{:S(2)}) collective-permute-start(bf16[128,512]{1,0:T(8,128)(2,1)S(1)} %slice_select_fusion), channel_id=1, source_target_pairs={{0,16},{1,17},{2,18},{3,19}} | collective-permute-start | bytes 393224 | tf_op jit(solution)/shard_map/ppermute | solution.py:344
  3.0 35.3 %collective-permute-start.2 = (bf16[1024,512]{1,0:T(8,128)(2,1)}, bf16[1024,512]{1,0:T(8,128)(2,1)S(1)}, u32[]{:S(2)}, u32[]{:S(2)}) collective-permute-start(bf16[1024,512]{1,0:T(8,128)(2,1)} %param.5), channel_id=1, source_target_pairs={{1,0},{2,1},{3,2},{0,3},{5,4},{6,5},{7,6},{4,7},{9,8},{10,9},{11,1... | collective-permute-start | bytes 3145736 | tf_op jit(solution)/shard_map/ppermute | solution.py:353
  6.6 34.7 %collective-permute-start = (bf16[1024,512]{1,0:T(8,128)(2,1)}, bf16[1024,512]{1,0:T(8,128)(2,1)S(1)}, u32[]{:S(2)}, u32[]{:S(2)}) collective-permute-start(bf16[1024,512]{1,0:T(8,128)(2,1)} %param.5), channel_id=1, source_target_pairs={{0,1},{1,2},{2,3},{3,0},{4,5},{5,6},{6,7},{7,4},{8,9},{9,10},{10,1... | collective-permute-start | bytes 3145736 | tf_op jit(solution)/shard_map/ppermute | solution.py:352
  7.8 6.9 %copy-start.18 = (s32[4,64,8,4]{2,1,3,0:T(8,128)}, s32[4,64,8,4]{2,1,3,0:T(8,128)S(1)}, u32[]{:S(2)}) copy-start(s32[4,64,8,4]{2,1,3,0:T(8,128)S(1)} %reshape.309) | copy-start | bytes 98308
  14.7 2.7 collective-permute-start.9
  15.4 2.0 collective-permute-start.8
  16.0 14.0 %collective-permute-start.7 = (bf16[128,512]{1,0:T(8,128)(2,1)S(1)}, bf16[128,512]{1,0:T(8,128)(2,1)S(1)}, u32[]{:S(2)}, u32[]{:S(2)}) collective-permute-start(bf16[128,512]{1,0:T(8,128)(2,1)S(1)} %add_add_fusion.2), channel_id=1, source_target_pairs={{0,4},{16,20},{32,36},{48,52},{1,5},{17,21},{33,37},{49,53},{2,6},... | collective-permute-start | bytes 393224 | tf_op jit(solution)/shard_map/ppermute | solution.py:344
  30.1 4.7 %collective-permute-start.13 = (bf16[128,512]{1,0:T(8,128)(2,1)S(1)}, bf16[128,512]{1,0:T(8,128)(2,1)S(1)}, u32[]{:S(2)}, u32[]{:S(2)}) collective-permute-start(bf16[128,512]{1,0:T(8,128)(2,1)S(1)} %add_add_fusion.1), channel_id=1, source_target_pairs={{0,192},{4,196},{8,200},{12,204},{16,208},{20,212},{24,216},{28,22... | collective-permute-start | bytes 393224 | tf_op jit(solution)/shard_map/ppermute | solution.py:344
  31.4 4.0 %collective-permute-start.12 = (bf16[128,512]{1,0:T(8,128)(2,1)S(1)}, bf16[128,512]{1,0:T(8,128)(2,1)S(1)}, u32[]{:S(2)}, u32[]{:S(2)}) collective-permute-start(bf16[128,512]{1,0:T(8,128)(2,1)S(1)} %add_add_fusion.1), channel_id=1, source_target_pairs={{0,128},{4,132},{8,136},{12,140},{16,144},{20,148},{24,152},{28,15... | collective-permute-start | bytes 393224 | tf_op jit(solution)/shard_map/ppermute | solution.py:344
  32.7 5.5 %collective-permute-start.11 = (bf16[128,512]{1,0:T(8,128)(2,1)S(1)}, bf16[128,512]{1,0:T(8,128)(2,1)S(1)}, u32[]{:S(2)}, u32[]{:S(2)}) collective-permute-start(bf16[128,512]{1,0:T(8,128)(2,1)S(1)} %add_add_fusion.1), channel_id=1, source_target_pairs={{0,64},{4,68},{8,72},{12,76},{16,80},{20,84},{24,88},{28,92},{32,9... | collective-permute-start | bytes 393224 | tf_op jit(solution)/shard_map/ppermute | solution.py:344
  34.8 48.8 %collective-permute-start.10 = (bf16[1024,512]{1,0:T(8,128)(2,1)}, bf16[1024,512]{1,0:T(8,128)(2,1)S(1)}, u32[]{:S(2)}, u32[]{:S(2)}) collective-permute-start(bf16[1024,512]{1,0:T(8,128)(2,1)} %param.5), channel_id=1, source_target_pairs={{0,32},{4,36},{8,40},{12,44},{16,48},{20,52},{24,56},{28,60},{32,0... | collective-permute-start | bytes 3145736 | tf_op jit(solution)/shard_map/ppermute | solution.py:374
  38.2 6.0 %copy-start.11 = (f32[1024,1024]{0,1:T(8,128)S(1)}, f32[1024,1024]{0,1:T(8,128)}, u32[]{:S(2)}) copy-start(f32[1024,1024]{0,1:T(8,128)} %fusion.16) | copy-start | bytes 12582916
  38.3 6.0 %copy-start.19 = (bf16[1024,512]{1,0:T(8,128)(2,1)}, bf16[1024,512]{1,0:T(8,128)(2,1)S(1)}, u32[]{:S(2)}) copy-start(bf16[1024,512]{1,0:T(8,128)(2,1)S(1)} %collective-permute-done.2) | copy-start | bytes 3145732
  38.3 13.3 %collective-permute-start.3 = (bf16[512,512]{1,0:T(8,128)(2,1)S(1)}, bf16[512,512]{1,0:T(8,128)(2,1)S(1)}, u32[]{:S(2)}, u32[]{:S(2)}) collective-permute-start(bf16[512,512]{1,0:T(8,128)(2,1)S(1)} %slice.65), channel_id=1, source_target_pairs={{1,0},{2,1},{3,2},{0,3},{5,4},{6,5},{7,6},{4,7},{9,8},{10,9},{11,1... | collective-permute-start | bytes 1572872 | tf_op jit(solution)/shard_map/ppermute | solution.py:355
  41.4 5.5 %copy-start.12 = (bf16[1024,512]{1,0:T(8,128)(2,1)}, bf16[1024,512]{1,0:T(8,128)(2,1)S(1)}, u32[]{:S(2)}) copy-start(bf16[1024,512]{1,0:T(8,128)(2,1)S(1)} %collective-permute-done) | copy-start | bytes 3145732
  41.4 13.5 %collective-permute-start.1 = (bf16[512,512]{1,0:T(8,128)(2,1)S(1)}, bf16[512,512]{1,0:T(8,128)(2,1)S(1)}, u32[]{:S(2)}, u32[]{:S(2)}) collective-permute-start(bf16[512,512]{1,0:T(8,128)(2,1)S(1)} %slice.64), channel_id=1, source_target_pairs={{0,1},{1,2},{2,3},{3,0},{4,5},{5,6},{6,7},{7,4},{8,9},{9,10},{10,1... | collective-permute-start | bytes 1572872 | tf_op jit(solution)/shard_map/ppermute | solution.py:354
  51.6 2.2 copy-start.22
  53.8 3.2 copy-start.14
  54.9 2.2 copy-start.24
  57.1 1.0 copy-start.16
  68.8 0.8 copy-start.6
  69.6 0.8 copy-start.10
  85.3 28.1 %collective-permute-start.15 = (bf16[1152,512]{1,0:T(8,128)(2,1)}, bf16[1152,512]{1,0:T(8,128)(2,1)}, u32[]{:S(2)}, u32[]{:S(2)}) collective-permute-start(bf16[1152,512]{1,0:T(8,128)(2,1)} %constant_dynamic-update-slice_fusion), channel_id=1, source_target_pairs={{1,0},{2,1},{3,2},{0,3},{5,4},{6,5},{7,6},{4,7},{9,8},{10,9},{11,1... | collective-permute-start | bytes 3538952 | tf_op jit(solution)/shard_map/ppermute | solution.py:353
  88.2 29.7 %collective-permute-start.14 = (bf16[1152,512]{1,0:T(8,128)(2,1)}, bf16[1152,512]{1,0:T(8,128)(2,1)}, u32[]{:S(2)}, u32[]{:S(2)}) collective-permute-start(bf16[1152,512]{1,0:T(8,128)(2,1)} %constant_dynamic-update-slice_fusion), channel_id=1, source_target_pairs={{0,1},{1,2},{2,3},{3,0},{4,5},{5,6},{6,7},{7,4},{8,9},{9,10},{10,1... | collective-permute-start | bytes 3538952 | tf_op jit(solution)/shard_map/ppermute | solution.py:352
  88.5 56.5 %collective-permute-start.26 = (bf16[4,2,128,256]{3,2,1,0:T(8,128)(2,1)}, bf16[4,2,128,256]{3,2,1,0:T(8,128)(2,1)S(1)}, u32[]{:S(2)}, u32[]{:S(2)}) collective-permute-start(bf16[4,2,128,256]{3,2,1,0:T(8,128)(2,1)} %copy-done.10), channel_id=1, source_target_pairs={{0,16},{4,20},{8,24},{12,28},{16,32},{20,36},{24,40},{28,44},{32,4... | collective-permute-start | bytes 1572872 | tf_op jit(solution)/shard_map/ppermute | solution.py:386
  88.6 64.7 %collective-permute-start.24 = (bf16[8,2,128,256]{3,2,1,0:T(8,128)(2,1)S(1)}, bf16[8,2,128,256]{3,2,1,0:T(8,128)(2,1)S(1)}, u32[]{:S(2)}, u32[]{:S(2)}) collective-permute-start(bf16[8,2,128,256]{3,2,1,0:T(8,128)(2,1)S(1)} %get-tuple-element.36), channel_id=1, source_target_pairs={{0,8},{4,12},{8,16},{12,20},{16,24},{20,28},{24,32},{28,36},{32,40... | collective-permute-start | bytes 3145736 | tf_op jit(solution)/shard_map/ppermute | solution.py:386
  88.7 64.6 %collective-permute-start.25 = (bf16[8,2,128,256]{3,2,1,0:T(8,128)(2,1)S(1)}, bf16[8,2,128,256]{3,2,1,0:T(8,128)(2,1)S(1)}, u32[]{:S(2)}, u32[]{:S(2)}) collective-permute-start(bf16[8,2,128,256]{3,2,1,0:T(8,128)(2,1)S(1)} %get-tuple-element.37), channel_id=1, source_target_pairs={{0,56},{4,60},{8,0},{12,4},{16,8},{20,12},{24,16},{28,20},{32,24},... | collective-permute-start | bytes 3145736 | tf_op jit(solution)/shard_map/ppermute | solution.py:386
  114.5 14.8 %collective-permute-start.17 = (bf16[576,512]{1,0:T(8,128)(2,1)S(1)}, bf16[576,512]{1,0:T(8,128)(2,1)S(1)}, u32[]{:S(2)}, u32[]{:S(2)}) collective-permute-start(bf16[576,512]{1,0:T(8,128)(2,1)S(1)} %slice.71), channel_id=1, source_target_pairs={{1,0},{2,1},{3,2},{0,3},{5,4},{6,5},{7,6},{4,7},{9,8},{10,9},{11,1... | collective-permute-start | bytes 1769480 | tf_op jit(solution)/shard_map/ppermute | solution.py:355
  119.1 14.5 %collective-permute-start.16 = (bf16[576,512]{1,0:T(8,128)(2,1)S(1)}, bf16[576,512]{1,0:T(8,128)(2,1)S(1)}, u32[]{:S(2)}, u32[]{:S(2)}) collective-permute-start(bf16[576,512]{1,0:T(8,128)(2,1)S(1)} %slice.69), channel_id=1, source_target_pairs={{0,1},{1,2},{2,3},{3,0},{4,5},{5,6},{6,7},{7,4},{8,9},{9,10},{10,1... | collective-permute-start | bytes 1769480 | tf_op jit(solution)/shard_map/ppermute | solution.py:354
  119.2 6.4 %slice-start = ((s8[6291456]{0:T(1024)(128)(4,1)}), s8[4194304]{0:T(1024)(128)(4,1)S(1)}, s32[]{:S(2)}) async-start(s8[6291456]{0:T(1024)(128)(4,1)} %bitcast.64), calls=%async_computation.3 | async-start | bytes 8388608
  122.3 3.2 slice-start.1
  125.6 3.7 %copy-start.7 = (bf16[4,2,128,256]{3,2,1,0:T(8,128)(2,1)S(1)}, bf16[4,2,128,256]{3,2,1,0:T(8,128)(2,1)}, u32[]{:S(2)}) copy-start(bf16[4,2,128,256]{3,2,1,0:T(8,128)(2,1)} %copy-done.6) | copy-start | bytes 1572868
  129.2 24.1 %collective-permute-start.27 = (bf16[4,2,128,256]{3,2,1,0:T(8,128)(2,1)S(1)}, bf16[4,2,128,256]{3,2,1,0:T(8,128)(2,1)S(1)}, u32[]{:S(2)}, u32[]{:S(2)}) collective-permute-start(bf16[4,2,128,256]{3,2,1,0:T(8,128)(2,1)S(1)} %copy-done.7), channel_id=1, source_target_pairs={{0,48},{4,52},{8,56},{12,60},{16,0},{20,4},{24,8},{28,12},{32,16},... | collective-permute-start | bytes 1572872 | tf_op jit(solution)/shard_map/ppermute | solution.py:386
  130.0 5.9 %copy-start.21 = (bf16[576,1024]{1,0:T(8,128)(2,1)}, bf16[576,1024]{1,0:T(8,128)(2,1)S(1)}, u32[]{:S(2)}) copy-start(bf16[576,1024]{1,0:T(8,128)(2,1)S(1)} %fusion) | copy-start | bytes 3538948
  142.4 1.0 copy-start.2
  143.4 0.8 copy-start.4
  144.2 0.8 copy-start.8
  155.7 62.7 %all-to-all-start = ((bf16[8,4,2,128,256]{4,3,2,1,0:T(8,128)(2,1)}), bf16[8,4,2,128,256]{4,3,2,1,0:T(8,128)(2,1)}, u32[]{:S(2)}, u32[]{:S(2)}) async-start(bf16[8,4,2,128,256]{4,3,2,1,0:T(8,128)(2,1)} %merge_own.1), calls=%async_computation | async-start | bytes 8388608 | tf_op jit(solution)/shard_map/all_to_all | solution.py:401
  161.8 2.3 copy-start.15
  161.8 8.7 %copy-start.13 = (bf16[1024,512]{1,0:T(8,128)(2,1)S(1)}, bf16[1024,512]{1,0:T(8,128)(2,1)}, u32[]{:S(2)}) copy-start(bf16[1024,512]{1,0:T(8,128)(2,1)} %copy-done.12) | copy-start | bytes 3145732
  164.1 8.2 %copy-start.17 = (bf16[512,1024]{1,0:T(8,128)(2,1)S(1)}, bf16[512,1024]{1,0:T(8,128)(2,1)}, u32[]{:S(2)}) copy-start(bf16[512,1024]{1,0:T(8,128)(2,1)} %copy-done.16) | copy-start | bytes 3145732
  164.1 10.2 %copy-start.23 = (bf16[512,512]{1,0:T(8,128)(2,1)S(1)}, bf16[512,512]{1,0:T(8,128)(2,1)}, u32[]{:S(2)}) copy-start(bf16[512,512]{1,0:T(8,128)(2,1)} %copy-done.22) | copy-start | bytes 1572868
  164.1 10.2 %copy-start.25 = (bf16[512,512]{1,0:T(8,128)(2,1)S(1)}, bf16[512,512]{1,0:T(8,128)(2,1)}, u32[]{:S(2)}) copy-start(bf16[512,512]{1,0:T(8,128)(2,1)} %copy-done.24) | copy-start | bytes 1572868
  164.2 11.9 %copy-start.9 = (bf16[4,2,128,256]{3,2,1,0:T(8,128)(2,1)S(1)}, bf16[4,2,128,256]{3,2,1,0:T(8,128)(2,1)}, u32[]{:S(2)}) copy-start(bf16[4,2,128,256]{3,2,1,0:T(8,128)(2,1)} %copy-done.8) | copy-start | bytes 1572868
  164.2 12.0 %copy-start.5 = (bf16[4,2,128,256]{3,2,1,0:T(8,128)(2,1)S(1)}, bf16[4,2,128,256]{3,2,1,0:T(8,128)(2,1)}, u32[]{:S(2)}) copy-start(bf16[4,2,128,256]{3,2,1,0:T(8,128)(2,1)} %copy-done.4) | copy-start | bytes 1572868
  164.2 15.5 %copy-start.20 = (bf16[1024,512]{1,0:T(8,128)(2,1)S(1)}, bf16[1024,512]{1,0:T(8,128)(2,1)}, u32[]{:S(2)}) copy-start(bf16[1024,512]{1,0:T(8,128)(2,1)} %copy-done.19) | copy-start | bytes 3145732
  164.2 12.0 %collective-permute-start.22 = (bf16[128,1024]{1,0:T(8,128)(2,1)S(1)}, bf16[128,1024]{1,0:T(8,128)(2,1)S(1)}, u32[]{:S(2)}, u32[]{:S(2)}) collective-permute-start(bf16[128,1024]{1,0:T(8,128)(2,1)S(1)} %slice.72), channel_id=1, source_target_pairs={{0,4},{4,8},{8,12},{12,16},{16,20},{20,24},{24,28},{28,32},{32,36}... | collective-permute-start | bytes 786440 | tf_op jit(solution)/shard_map/ppermute | solution.py:380
  166.4 49.7 %collective-permute-start.18 = (bf16[8,2,128,256]{3,2,1,0:T(8,128)(2,1)}, bf16[8,2,128,256]{3,2,1,0:T(8,128)(2,1)S(1)}, u32[]{:S(2)}, u32[]{:S(2)}) collective-permute-start(bf16[8,2,128,256]{3,2,1,0:T(8,128)(2,1)} %get-tuple-element.43), channel_id=1, source_target_pairs={{0,8},{4,12},{8,16},{12,20},{16,24},{20,28},{24,32},{28,36},{32,40... | collective-permute-start | bytes 3145736 | tf_op jit(solution)/shard_map/ppermute | solution.py:386
  166.9 49.2 %collective-permute-start.19 = (bf16[8,2,128,256]{3,2,1,0:T(8,128)(2,1)}, bf16[8,2,128,256]{3,2,1,0:T(8,128)(2,1)S(1)}, u32[]{:S(2)}, u32[]{:S(2)}) collective-permute-start(bf16[8,2,128,256]{3,2,1,0:T(8,128)(2,1)} %get-tuple-element.44), channel_id=1, source_target_pairs={{0,56},{4,60},{8,0},{12,4},{16,8},{20,12},{24,16},{28,20},{32,24},... | collective-permute-start | bytes 3145736 | tf_op jit(solution)/shard_map/ppermute | solution.py:386
  172.4 28.5 %collective-permute-start.23 = (bf16[128,1024]{1,0:T(8,128)(2,1)S(1)}, bf16[128,1024]{1,0:T(8,128)(2,1)S(1)}, u32[]{:S(2)}, u32[]{:S(2)}) collective-permute-start(bf16[128,1024]{1,0:T(8,128)(2,1)S(1)} %slice.73), channel_id=1, source_target_pairs={{4,0},{8,4},{12,8},{16,12},{20,16},{24,20},{28,24},{32,28},{36,32}... | collective-permute-start | bytes 786440 | tf_op jit(solution)/shard_map/ppermute | solution.py:381
  176.1 35.4 %collective-permute-start.20 = (bf16[4,2,128,256]{3,2,1,0:T(8,128)(2,1)S(1)}, bf16[4,2,128,256]{3,2,1,0:T(8,128)(2,1)S(1)}, u32[]{:S(2)}, u32[]{:S(2)}) collective-permute-start(bf16[4,2,128,256]{3,2,1,0:T(8,128)(2,1)S(1)} %copy-done.9), channel_id=1, source_target_pairs={{0,16},{4,20},{8,24},{12,28},{16,32},{20,36},{24,40},{28,44},{32,4... | collective-permute-start | bytes 1572872 | tf_op jit(solution)/shard_map/ppermute | solution.py:386
  176.2 39.9 %collective-permute-start.21 = (bf16[4,2,128,256]{3,2,1,0:T(8,128)(2,1)S(1)}, bf16[4,2,128,256]{3,2,1,0:T(8,128)(2,1)S(1)}, u32[]{:S(2)}, u32[]{:S(2)}) collective-permute-start(bf16[4,2,128,256]{3,2,1,0:T(8,128)(2,1)S(1)} %copy-done.5), channel_id=1, source_target_pairs={{0,48},{4,52},{8,56},{12,60},{16,0},{20,4},{24,8},{28,12},{32,16},... | collective-permute-start | bytes 1572872 | tf_op jit(solution)/shard_map/ppermute | solution.py:386
  181.5 34.6 %copy-start.3 = (bf16[8,2,128,256]{3,2,1,0:T(8,128)(2,1)S(1)}, bf16[8,2,128,256]{3,2,1,0:T(8,128)(2,1)}, u32[]{:S(2)}) copy-start(bf16[8,2,128,256]{3,2,1,0:T(8,128)(2,1)} %copy-done.2) | copy-start | bytes 3145732
  218.3 11.9 %copy-start.26 = (s32[1,2048]{1,0:T(1,128)S(1)}, s32[1,2048]{1,0:T(1,128)}, u32[]{:S(2)}) copy-start(s32[1,2048]{1,0:T(1,128)} %param.7) | copy-start | bytes 24580
  218.4 58.9 %all-to-all-start.1 = ((bf16[8,4,2,128,256]{4,3,2,1,0:T(8,128)(2,1)}), bf16[8,4,2,128,256]{4,3,2,1,0:T(8,128)(2,1)}, u32[]{:S(2)}, u32[]{:S(2)}) async-start(bf16[8,4,2,128,256]{4,3,2,1,0:T(8,128)(2,1)} %merge_copied.1), calls=%async_computation.1 | async-start | bytes 8388608 | tf_op jit(solution)/shard_map/all_to_all | solution.py:401
  289.4 1.3 copy-start.1
  290.7 58.5 %all-to-all-start.2 = ((bf16[64,128,128]{2,1,0:T(8,128)(2,1)}), bf16[64,128,128]{2,1,0:T(8,128)(2,1)S(1)}, u32[]{:S(2)}, u32[]{:S(2)}) async-start(bf16[64,128,128]{2,1,0:T(8,128)(2,1)} %copy-done.1), calls=%async_computation.2 | async-start | bytes 4194304 | tf_op jit(solution)/shard_map/all_to_all | solution.py:429

commit v3 on v2

--- a/solution.py
+++ b/solution.py
@@ -290,13 +290,9 @@
 
     far_z = device(my_x, my_z + NZ // 2, my_core)
     tables = (held_for(me), held_for(far_z))
-    plane = NX * NC
-    spot = jnp.arange(plane, dtype=jnp.int32)
-    even = jnp.concatenate([spot[0:2], spot[4:6]])
-    odd = jnp.concatenate([spot[2:4], spot[6:8]])
-    moves = [(0, spot), (1, spot), (-1, spot), (2, even), (-2, odd)]
+    spot = jnp.arange(NX * NC, dtype=jnp.int32)
     dests = jnp.concatenate(
-        [device(at // NC, my_z + move, at % NC) for move, at in moves]
+        [device(spot // NC, my_z + step, spot % NC) for step in (0, 1, -1, 2 - 4 * my_core)]
     ).astype(jnp.int32)
 
     wanted = lax.dynamic_index_in_dim(asked, me, 0, keepdims=False)
@@ -307,11 +303,11 @@
     )
     step = (my_z - source // NC) % NZ
     source_spot = source // (NZ * NC) * NC + source % NC
-    my_two = (2 - 4 * (my_x % 2)) % NZ
+    source_two = (2 - 4 * (source % NC)) % NZ
 
     def route_kind(step):
         return jnp.where(
-            step == 0, 0, jnp.where(step == 1, 1, jnp.where(step == NZ - 1, 2, jnp.where(step == my_two, 3, -1)))
+            step == 0, 0, jnp.where(step == 1, 1, jnp.where(step == NZ - 1, 2, jnp.where(step == source_two, 3, -1)))
         )
 
     near_kind = route_kind(step)
@@ -382,20 +378,19 @@
 
     planes = [[device(x, z, c) for x in range(NX) for c in range(NC)] for z in range(NZ)]
 
-    def along_z(part, move):
-        return lax.ppermute(part, "seq", seq_pairs(lambda x, z, c: (x, z + move, c))) if move else part
-
-    shares = [at.shape[0] for _, at in moves]
-    steps = [move for move, _ in moves]
-    whole = list(range(NX * NC))
-    spots = [whole, whole, whole, [0, 1, 4, 5], [2, 3, 6, 7]]
-    places = [[(g, min(k, 3)) for g in at] for k, at in enumerate(spots)]
-
     def pack(table, pair, name):
-        return pack_tiles(table, dests, pair, shares, rows, heads, blk, hd, name)
+        return pack_tiles(table, dests, pair, [NX * NC] * 4, rows, heads, blk, hd, name)
 
     def shifted(parts):
-        return [along_z(part, move) for part, move in zip(parts, steps)]
+        goals = [
+            lambda x, z, c: (x, z + 1, c),
+            lambda x, z, c: (x, z - 1, c),
+            lambda x, z, c: (x, z + 2 - 4 * c, c),
+        ]
+        moved = [lax.ppermute(part, "seq", seq_pairs(goal)) for part, goal in zip(parts[1:], goals)]
+        return [parts[0], *moved]
+
+    places = [[(g, a) for g in range(NX * NC)] for a in range(4)]
 
     def in_plane(block):
         got = lax.all_to_all(
@@ -404,7 +399,13 @@
         return got.reshape(-1, blk, 2 * hd)
 
     own_parts = pack(tables[0], pair, "pack_own")
-    copied, zero, _ = lax.optimization_barrier((copied, zero, own_parts))
+    own_parts, far_top, far_bottom = lax.optimization_barrier((own_parts, far_top, far_bottom))
+    far = jnp.concatenate([far_top, far_bottom], axis=0)
+    query = dot(far, w_query(2)) + dot(tokens, w_query(0))
+    query = (query + dot(from_low, w_query(3)) + dot(from_high, w_query(1))).astype(BF)
+    copied, zero, before, after, query = lax.optimization_barrier(
+        (copied, zero, before, after, query)
+    )
     own_parts = shifted(own_parts)
     copied = jnp.concatenate([copied, zero], axis=0)
     copied_ring = ring(copied)
@@ -415,9 +416,6 @@
     own_tiles = in_plane(merge_parts(own_parts, places, "merge_own"))
 
     around = jnp.concatenate([before, pair, after], axis=0)
-    far = jnp.concatenate([far_top, far_bottom], axis=0)
-    query = dot(far, w_query(2)) + dot(tokens, w_query(0))
-    query = (query + dot(from_low, w_query(3)) + dot(from_high, w_query(1))).astype(BF)
     first = copied_pair[count:]
     acc, stat = near_attend(edges, query, around, first, rows, heads, blk, hd, factor)
     copied_parts, acc, stat = lax.optimization_barrier((copied_parts, acc, stat))

time: 352 us -> 338 us (0.960)
  starting transfers between devices: 60 us -> 52.9 us
  waiting for transfers between devices: 192 us -> 186 us
    ppermute x8 -> x6, waiting for transfers between devices: 12.9 us -> 33.3 us  [shifted(): lax.ppermute(part, 'seq', seq_pairs(goal))]
    ppermute x1, waiting for transfers between devices: 19.3 us -> 0.01 us  [local(): after = lax.ppermute(pair[:blk], 'seq', down)]
    ppermute x1, waiting for transfers between devices: 13.2 us -> 9.23 us  [local(): lax.ppermute(copied, 'seq', seq_pairs(lambda x, z, c: (x, z + NZ // 2, c)))]
    ppermute x8 -> x6, starting transfers between devices: 10.6 us -> 7.05 us  [shifted(): lax.ppermute(part, 'seq', seq_pairs(goal))]
    ppermute x2, starting transfers between devices: 6.59 us -> 3.05 us  [ring(): high = lax.ppermute(part, 'head', backward)]
    unnamed x59 -> x47, local copies, waits for them, and re-layouts: 7.69 us -> 4.68 us
  transfers between devices with their start and end apart: 31 -> 29, of which waited for: 14 -> 12; matrix products, arithmetic and copies ran while one was open for 13% -> 13% of each run, Pallas kernels for 8% -> 9%
where the time goes in v3:
time: 338 us; the launch traced here: 337 us
  waiting for transfers between devices  186 us (55%)
  starting transfers between devices  52.9 us (16%)
  Pallas kernels  45.4 us (13%)
  matrix products  30.3 us (9%)
  local copies, waits for them, and re-layouts  12.4 us (4%)
  other arithmetic  8.98 us (3%)
    all_to_all x1, waiting for transfers between devices, local(): back = lax.all_to_all(done, 'seq', split_axis=0, concat_axis=0, tiled=True)  51.2 us
    all_to_all x2, waiting for transfers between devices, in_plane(): lax.all_to_all(block, 'seq', split_axis=0, concat_axis=0, axis_index_grou...  46.8 us
    ppermute x6, waiting for transfers between devices, shifted(): lax.ppermute(part, 'seq', seq_pairs(goal))  33.3 us
    dot_general x14, matrix products, dot(): return jnp.dot(a, b, preferred_element_type=F32)  30.3 us
    ppermute x2, waiting for transfers between devices, ring(): high = lax.ppermute(part, 'head', backward)  21.8 us
    ppermute x9, waiting for transfers between devices, spread(): lax.ppermute(block, 'seq', [(h, h + k * stride) for h in holders])  16.5 us
    pallas_call x2, Pallas kernels, pack_tiles(): pl.pallas_call(kernel, out_shape=[jax.ShapeDtypeStruct((share, 2, blk, 2...  15.6 us
    all_to_all x2, starting transfers between devices, in_plane(): lax.all_to_all(block, 'seq', split_axis=0, concat_axis=0, axis_index_grou...  13.2 us
  transfers between devices with their start and end apart: 29, of which 12 were waited for; matrix products, arithmetic and copies ran while one was open for 13% of the time, Pallas kernels for 9%

profile of v3, /device:TPU:1, one launch (start us, length us, event | category | flops | bytes accessed | tf_op | source)
XLA Modules:
  0.0 336.6 jit_solution(16637764470757049947)
XLA Ops:
  0.0 0.9 slice_select_fusion
  3.0 2.2 collective-permute-start.10
  5.2 1.5 collective-permute-start.11
  6.7 3.4 %fusion.32 = f32[512,1024]{0,1:T(8,128)} fusion(bf16[1024,512]{1,0:T(8,128)(2,1)} %param.5, bf16[2048,1536]{1,0:T(8,128)(2,1)} %param.6, s32[]{:T(128)S(6)} %select_n.404), kind=kOutput, calls=%fused_computation.48 | convolution fusion | flops 536870912 | bytes 3670020 | tf_op jit(solution)/shard_map/dot_general | solution.py:17
  10.2 4.8 %fusion.16 = f32[1024,1024]{0,1:T(8,128)} fusion(bf16[1024,512]{1,0:T(8,128)(2,1)} %param.5, bf16[2048,1536]{1,0:T(8,128)(2,1)} %param.6, s32[]{:T(128)S(6)} %select_n.404), kind=kOutput, calls=%fused_computation.29 | convolution fusion | flops 1073741824 | bytes 6291460 | tf_op jit(solution)/shard_map/dot_general | solution.py:17
  15.8 1.2 select_reduce_fusion.1
  17.0 1.0 add_add_fusion.2
  19.3 1.3 collective-permute-start.3
  20.7 12.8 %collective-permute-done.3 = bf16[128,512]{1,0:T(8,128)(2,1)S(1)} collective-permute-done((bf16[128,512]{1,0:T(8,128)(2,1)S(1)}, bf16[128,512]{1,0:T(8,128)(2,1)S(1)}, u32[]{:S(2)}, u32[]{:S(2)}) %collective-permute-start.3) | collective-permute-done | bytes 131104 | tf_op jit(solution)/shard_map/ppermute | solution.py:340
  33.4 1.3 collective-permute-start.9
  34.8 1.3 collective-permute-start.8
  36.1 1.3 collective-permute-start.7
  37.8 1.0 collective-permute-done.8
  38.8 2.8 collective-permute-done.7
  41.9 2.7 collective-permute-start.12
  44.6 2.6 fusion.13
  47.2 2.7 add_bitcast_fusion
  50.0 2.1 fusion.30
  52.1 2.5 collective-permute-done.12
  54.5 0.7 fusion.3
  55.3 0.8 slice.50
  56.8 0.8 slice.53
  57.5 4.3 %collective-permute-start.15 = (bf16[128,1024]{1,0:T(8,128)(2,1)}, bf16[128,1024]{1,0:T(8,128)(2,1)S(1)}, u32[]{:S(2)}, u32[]{:S(2)}) collective-permute-start(bf16[128,1024]{1,0:T(8,128)(2,1)} %slice.53), channel_id=1, source_target_pairs={{4,0},{8,4},{12,8},{16,12},{20,16},{24,20},{28,24},{32,28},{36,32}... | collective-permute-start | bytes 786440 | tf_op jit(solution)/shard_map/ppermute | solution.py:377
  61.9 2.1 collective-permute-start.13
  64.0 1.5 pad_maximum_fusion.2.pair_ref
  65.5 9.2 %pack_own.1 = (bf16[8,2,128,256]{3,2,1,0:T(8,128)(2,1)S(1)}, bf16[8,2,128,256]{3,2,1,0:T(8,128)(2,1)S(1)}, bf16[8,2,128,256]{3,2,1,0:T(8,128)(2,1)S(1)}, bf16[8,2,128,256]{3,2,1,0:T(8,128)(2,1)S(1)}) custom-call(s32[128]{0:T(128)S(1)} %reshape.312.table_ref, s32[32]{0:T(128)S(1)} %pad_add_fusion.2.dest_ref, bf16[1024,1024]{1,0:T(8,128)(2,1)} %pad_maximum_fusion.2.pair_ref), custom_call_target="tpu_custom_call" | custom-call | tf_op jit(solution)/shard_map/pack_own/pallas_call | solution.py:54
  74.7 0.7 fusion.5
  75.5 2.0 fusion.4.q_ref
  77.5 9.2 %collective-permute-done.6 = bf16[1024,512]{1,0:T(8,128)(2,1)} collective-permute-done((bf16[1024,512]{1,0:T(8,128)(2,1)}, bf16[1024,512]{1,0:T(8,128)(2,1)}, u32[]{:S(2)}, u32[]{:S(2)}) %collective-permute-start.6) | collective-permute-done | bytes 1048608 | tf_op jit(solution)/shard_map/ppermute | solution.py:370
  86.8 2.3 constant_dynamic-update-slice_fusion.1
  89.7 1.5 collective-permute-start.17
  91.8 2.4 collective-permute-start.24
  94.3 0.8 collective-permute-start.25
  95.1 21.8 %collective-permute-done.17 = bf16[1152,512]{1,0:T(8,128)(2,1)} collective-permute-done((bf16[1152,512]{1,0:T(8,128)(2,1)}, bf16[1152,512]{1,0:T(8,128)(2,1)}, u32[]{:S(2)}, u32[]{:S(2)}) %collective-permute-start.17) | collective-permute-done | bytes 1179680 | tf_op jit(solution)/shard_map/ppermute | solution.py:349
  116.9 1.1 slice.57
  118.0 2.8 collective-permute-start.19
  120.8 1.1 slice.55
  122.2 3.1 fusion.11
  125.4 3.1 convolution_add_fusion.1
  128.5 2.7 convolution_add_fusion
  131.9 0.8 fusion
  132.7 3.7 %collective-permute-done.18 = bf16[576,512]{1,0:T(8,128)(2,1)S(1)} collective-permute-done((bf16[576,512]{1,0:T(8,128)(2,1)S(1)}, bf16[576,512]{1,0:T(8,128)(2,1)S(1)}, u32[]{:S(2)}, u32[]{:S(2)}) %collective-permute-start.18) | collective-permute-done | bytes 589856 | tf_op jit(solution)/shard_map/ppermute | solution.py:350
  136.4 0.8 fusion.1
  137.2 1.6 pad_maximum_fusion.1.pair_ref
  138.9 6.4 %pack_copied.1 = (bf16[8,2,128,256]{3,2,1,0:T(8,128)(2,1)S(1)}, bf16[8,2,128,256]{3,2,1,0:T(8,128)(2,1)}, bf16[8,2,128,256]{3,2,1,0:T(8,128)(2,1)}, bf16[8,2,128,256]{3,2,1,0:T(8,128)(2,1)}) custom-call(s32[128]{0:T(128)S(1)} %reshape.313.table_ref, s32[32]{0:T(128)S(1)} %pad_add_fusion.2.dest_ref, bf16[1152,1024]{1,0:T(8,128)(2,1)} %pad_maximum_fusion.1.pair_ref), custom_call_target="tpu_custom_call" | custom-call | tf_op jit(solution)/shard_map/pack_copied/pallas_call | solution.py:54
  145.2 1.0 copy-done.2
  146.2 2.3 merge_own.1
  148.5 7.6 %all-to-all-start = ((bf16[8,4,2,128,256]{4,3,2,1,0:T(8,128)(2,1)}), bf16[8,4,2,128,256]{4,3,2,1,0:T(8,128)(2,1)}, u32[]{:S(2)}, u32[]{:S(2)}) async-start(bf16[8,4,2,128,256]{4,3,2,1,0:T(8,128)(2,1)} %merge_own.1), calls=%async_computation | async-start | bytes 8388608 | tf_op jit(solution)/shard_map/all_to_all | solution.py:396
  156.5 2.2 collective-permute-start.21
  158.8 0.8 collective-permute-start.22
  159.6 1.3 pad_maximum_fusion.kv_ref
  160.9 1.0 slice.58.first_ref
  161.9 9.4 %near_attend.1 = (f32[32,128,128]{2,1,0:T(8,128)S(1)}, f32[32,8,128]{2,1,0:T(8,128)S(1)}) custom-call(s32[2]{0:T(128)S(1)} %add_convert_fusion.edge_ref, bf16[1024,512]{1,0:T(8,128)(2,1)S(1)} %fusion.4.q_ref, bf16[1280,1024]{1,0:T(8,128)(2,1)S(1)} %pad_maximum_fusion.kv_ref, bf16[128,1024]{1,0:T(8,128)(2,1)S(1)} %slice.58.first_ref), custom_call_target="tpu_custom_call" | custom-call | tf_op jit(solution)/shard_map/near_attend/pallas_call | solution.py:155
  171.3 11.1 %collective-permute-done.20.refs_1_ = bf16[8,2,128,256]{3,2,1,0:T(8,128)(2,1)} collective-permute-done((bf16[8,2,128,256]{3,2,1,0:T(8,128)(2,1)}, bf16[8,2,128,256]{3,2,1,0:T(8,128)(2,1)}, u32[]{:S(2)}, u32[]{:S(2)}) %collective-permute-start.20) | collective-permute-done | bytes 1048608 | tf_op jit(solution)/shard_map/ppermute | solution.py:390
  182.4 22.2 %collective-permute-done.22.refs_3_ = bf16[8,2,128,256]{3,2,1,0:T(8,128)(2,1)} collective-permute-done((bf16[8,2,128,256]{3,2,1,0:T(8,128)(2,1)}, bf16[8,2,128,256]{3,2,1,0:T(8,128)(2,1)}, u32[]{:S(2)}, u32[]{:S(2)}) %collective-permute-start.22) | collective-permute-done | bytes 1048608 | tf_op jit(solution)/shard_map/ppermute | solution.py:390
  204.6 4.2 %merge_copied.1 = bf16[8,4,2,128,256]{4,3,2,1,0:T(8,128)(2,1)} custom-call(bf16[8,2,128,256]{3,2,1,0:T(8,128)(2,1)S(1)} %copy-done.3, bf16[8,2,128,256]{3,2,1,0:T(8,128)(2,1)} %collective-permute-done.20.refs_1_, bf16[8,2,128,256]{3,2,1,0:T(8,128)(2,1)} %collective-permute-done.21.refs_2_, bf16[8,2,128,256]{3,2,1,0:T(8,128)(2,1)} %collective-permute-done.22.refs_3_), custom_call_target="tpu_custom_call" | custom-call | tf_op jit(solution)/shard_map/merge_copied/pallas_call | solution.py:89
  208.8 5.6 %all-to-all-start.1 = ((bf16[8,4,2,128,256]{4,3,2,1,0:T(8,128)(2,1)}), bf16[8,4,2,128,256]{4,3,2,1,0:T(8,128)(2,1)}, u32[]{:S(2)}, u32[]{:S(2)}) async-start(bf16[8,4,2,128,256]{4,3,2,1,0:T(8,128)(2,1)} %merge_copied.1), calls=%async_computation.1 | async-start | bytes 8388608 | tf_op jit(solution)/shard_map/all_to_all | solution.py:396
  214.6 1.2 copy.27
  216.5 46.8 %all-to-all-done.1 = bf16[8,4,2,128,256]{4,3,2,1,0:T(8,128)(2,1)} async-done(((bf16[8,4,2,128,256]{4,3,2,1,0:T(8,128)(2,1)}), bf16[8,4,2,128,256]{4,3,2,1,0:T(8,128)(2,1)}, u32[]{:S(2)}, u32[]{:S(2)}) %all-to-all-start.1) | async-done | bytes 4194336 | tf_op jit(solution)/shard_map/all_to_all | solution.py:396
  263.3 12.2 %rand_attend.1 = bf16[64,128,128]{2,1,0:T(8,128)(2,1)S(1)} custom-call(s32[128]{0:T(128)S(1)} %fusion.64.slot_ref, s32[32]{0:T(128)S(1)} %reshape.311.count_ref, s32[32]{0:T(128)S(1)} %select_reduce_fusion.4.target_ref, bf16[1024,512]{1,0:T(8,128)(2,1)S(1)} %fusion.4.q_ref, f32[32,128,128]{2,1,0:T(8,128)S(1)} %get-tuple-element.57.acc_ref, ...), custom_call_target="tpu_custom_call" | custom-call | tf_op jit(solution)/shard_map/rand_attend/pallas_call | solution.py:230
  275.5 1.3 copy-done.1
  276.8 6.5 %all-to-all-start.2 = ((bf16[64,128,128]{2,1,0:T(8,128)(2,1)}), bf16[64,128,128]{2,1,0:T(8,128)(2,1)S(1)}, u32[]{:S(2)}, u32[]{:S(2)}) async-start(bf16[64,128,128]{2,1,0:T(8,128)(2,1)} %copy-done.1), calls=%async_computation.2 | async-start | bytes 4194304 | tf_op jit(solution)/shard_map/all_to_all | solution.py:427
  283.5 51.2 %all-to-all-done.2.in_ref = bf16[64,128,128]{2,1,0:T(8,128)(2,1)S(1)} async-done(((bf16[64,128,128]{2,1,0:T(8,128)(2,1)}), bf16[64,128,128]{2,1,0:T(8,128)(2,1)S(1)}, u32[]{:S(2)}, u32[]{:S(2)}) %all-to-all-start.2) | async-done | bytes 2097184 | tf_op jit(solution)/shard_map/all_to_all | solution.py:427
  334.6 1.8 take_tiles.1
  (107 shorter events, 9.3 us)
Async XLA Ops:
  0.0 214.4 %copy-start = (s32[4,512]{1,0:T(4,128)S(1)}, s32[4,512]{1,0:T(4,128)}, u32[]{:S(2)}) copy-start(s32[4,512]{1,0:T(4,128)} %param.9) | copy-start | bytes 24580
  0.9 16.0 %collective-permute-start.1 = (bf16[128,512]{1,0:T(8,128)(2,1)S(1)}, bf16[128,512]{1,0:T(8,128)(2,1)S(1)}, u32[]{:S(2)}, u32[]{:S(2)}) collective-permute-start(bf16[128,512]{1,0:T(8,128)(2,1)S(1)} %slice_select_fusion), channel_id=1, source_target_pairs={{0,32},{1,33},{2,34},{3,35}} | collective-permute-start | bytes 393224 | tf_op jit(solution)/shard_map/ppermute | solution.py:340
  1.6 15.3 %collective-permute-start.2 = (bf16[128,512]{1,0:T(8,128)(2,1)S(1)}, bf16[128,512]{1,0:T(8,128)(2,1)S(1)}, u32[]{:S(2)}, u32[]{:S(2)}) collective-permute-start(bf16[128,512]{1,0:T(8,128)(2,1)S(1)} %slice_select_fusion), channel_id=1, source_target_pairs={{0,48},{1,49},{2,50},{3,51}} | collective-permute-start | bytes 393224 | tf_op jit(solution)/shard_map/ppermute | solution.py:340
  2.3 14.7 %collective-permute-start = (bf16[128,512]{1,0:T(8,128)(2,1)S(1)}, bf16[128,512]{1,0:T(8,128)(2,1)S(1)}, u32[]{:S(2)}, u32[]{:S(2)}) collective-permute-start(bf16[128,512]{1,0:T(8,128)(2,1)S(1)} %slice_select_fusion), channel_id=1, source_target_pairs={{0,16},{1,17},{2,18},{3,19}} | collective-permute-start | bytes 393224 | tf_op jit(solution)/shard_map/ppermute | solution.py:340
  3.0 38.7 %collective-permute-start.10 = (bf16[1024,512]{1,0:T(8,128)(2,1)}, bf16[1024,512]{1,0:T(8,128)(2,1)S(1)}, u32[]{:S(2)}, u32[]{:S(2)}) collective-permute-start(bf16[1024,512]{1,0:T(8,128)(2,1)} %param.5), channel_id=1, source_target_pairs={{0,1},{1,2},{2,3},{3,0},{4,5},{5,6},{6,7},{7,4},{8,9},{9,10},{10,1... | collective-permute-start | bytes 3145736 | tf_op jit(solution)/shard_map/ppermute | solution.py:348
  5.2 36.7 %collective-permute-start.11 = (bf16[1024,512]{1,0:T(8,128)(2,1)}, bf16[1024,512]{1,0:T(8,128)(2,1)S(1)}, u32[]{:S(2)}, u32[]{:S(2)}) collective-permute-start(bf16[1024,512]{1,0:T(8,128)(2,1)} %param.5), channel_id=1, source_target_pairs={{1,0},{2,1},{3,2},{0,3},{5,4},{6,5},{7,6},{4,7},{9,8},{10,9},{11,1... | collective-permute-start | bytes 3145736 | tf_op jit(solution)/shard_map/ppermute | solution.py:349
  10.2 4.8 %copy-start.16 = (s32[4,512,4]{1,2,0:T(4,128)S(1)}, s32[4,512,4]{1,2,0:T(4,128)}, u32[]{:S(2)}) copy-start(s32[4,512,4]{1,2,0:T(4,128)} %param.8) | copy-start | bytes 98308
  15.3 22.2 %copy-start.13 = (s32[4,64,8,4]{2,1,3,0:T(8,128)}, s32[4,64,8,4]{2,1,3,0:T(8,128)S(1)}, u32[]{:S(2)}) copy-start(s32[4,64,8,4]{2,1,3,0:T(8,128)S(1)} %reshape.309) | copy-start | bytes 98308
  17.9 2.7 collective-permute-start.5
  18.6 2.1 collective-permute-start.4
  19.3 14.1 %collective-permute-start.3 = (bf16[128,512]{1,0:T(8,128)(2,1)S(1)}, bf16[128,512]{1,0:T(8,128)(2,1)S(1)}, u32[]{:S(2)}, u32[]{:S(2)}) collective-permute-start(bf16[128,512]{1,0:T(8,128)(2,1)S(1)} %add_add_fusion.2), channel_id=1, source_target_pairs={{0,4},{16,20},{32,36},{48,52},{1,5},{17,21},{33,37},{49,53},{2,6},... | collective-permute-start | bytes 393224 | tf_op jit(solution)/shard_map/ppermute | solution.py:340
  33.4 4.3 %collective-permute-start.9 = (bf16[128,512]{1,0:T(8,128)(2,1)S(1)}, bf16[128,512]{1,0:T(8,128)(2,1)S(1)}, u32[]{:S(2)}, u32[]{:S(2)}) collective-permute-start(bf16[128,512]{1,0:T(8,128)(2,1)S(1)} %add_add_fusion.1), channel_id=1, source_target_pairs={{0,192},{4,196},{8,200},{12,204},{16,208},{20,212},{24,216},{28,22... | collective-permute-start | bytes 393224 | tf_op jit(solution)/shard_map/ppermute | solution.py:340
  34.8 4.0 %collective-permute-start.8 = (bf16[128,512]{1,0:T(8,128)(2,1)S(1)}, bf16[128,512]{1,0:T(8,128)(2,1)S(1)}, u32[]{:S(2)}, u32[]{:S(2)}) collective-permute-start(bf16[128,512]{1,0:T(8,128)(2,1)S(1)} %add_add_fusion.1), channel_id=1, source_target_pairs={{0,128},{4,132},{8,136},{12,140},{16,144},{20,148},{24,152},{28,15... | collective-permute-start | bytes 393224 | tf_op jit(solution)/shard_map/ppermute | solution.py:340
  36.1 5.5 %collective-permute-start.7 = (bf16[128,512]{1,0:T(8,128)(2,1)S(1)}, bf16[128,512]{1,0:T(8,128)(2,1)S(1)}, u32[]{:S(2)}, u32[]{:S(2)}) collective-permute-start(bf16[128,512]{1,0:T(8,128)(2,1)S(1)} %add_add_fusion.1), channel_id=1, source_target_pairs={{0,64},{4,68},{8,72},{12,76},{16,80},{20,84},{24,88},{28,92},{32,9... | collective-permute-start | bytes 393224 | tf_op jit(solution)/shard_map/ppermute | solution.py:340
  37.8 49.0 %collective-permute-start.6 = (bf16[1024,512]{1,0:T(8,128)(2,1)}, bf16[1024,512]{1,0:T(8,128)(2,1)}, u32[]{:S(2)}, u32[]{:S(2)}) collective-permute-start(bf16[1024,512]{1,0:T(8,128)(2,1)} %param.5), channel_id=1, source_target_pairs={{0,32},{4,36},{8,40},{12,44},{16,48},{20,52},{24,56},{28,60},{32,0... | collective-permute-start | bytes 3145736 | tf_op jit(solution)/shard_map/ppermute | solution.py:370
  41.6 5.6 %copy-start.6 = (f32[1024,1024]{0,1:T(8,128)S(1)}, f32[1024,1024]{0,1:T(8,128)}, u32[]{:S(2)}) copy-start(f32[1024,1024]{0,1:T(8,128)} %fusion.16) | copy-start | bytes 12582916
  41.7 14.3 %collective-permute-start.14 = (bf16[512,512]{1,0:T(8,128)(2,1)S(1)}, bf16[512,512]{1,0:T(8,128)(2,1)S(1)}, u32[]{:S(2)}, u32[]{:S(2)}) collective-permute-start(bf16[512,512]{1,0:T(8,128)(2,1)S(1)} %slice.52), channel_id=1, source_target_pairs={{0,1},{1,2},{2,3},{3,0},{4,5},{5,6},{6,7},{7,4},{8,9},{9,10},{10,1... | collective-permute-start | bytes 1572872 | tf_op jit(solution)/shard_map/ppermute | solution.py:350
  41.8 8.1 %copy-start.14 = (bf16[1024,512]{1,0:T(8,128)(2,1)}, bf16[1024,512]{1,0:T(8,128)(2,1)S(1)}, u32[]{:S(2)}) copy-start(bf16[1024,512]{1,0:T(8,128)(2,1)S(1)} %collective-permute-done.11) | copy-start | bytes 3145732
  41.9 12.6 %collective-permute-start.12 = (bf16[512,512]{1,0:T(8,128)(2,1)S(1)}, bf16[512,512]{1,0:T(8,128)(2,1)S(1)}, u32[]{:S(2)}, u32[]{:S(2)}) collective-permute-start(bf16[512,512]{1,0:T(8,128)(2,1)S(1)} %slice.49), channel_id=1, source_target_pairs={{1,0},{2,1},{3,2},{0,3},{5,4},{6,5},{7,6},{4,7},{9,8},{10,9},{11,1... | collective-permute-start | bytes 1572872 | tf_op jit(solution)/shard_map/ppermute | solution.py:351
  44.6 5.4 %slice-start = ((s8[6291456]{0:T(1024)(128)(4,1)}), s8[4194304]{0:T(1024)(128)(4,1)S(1)}, s32[]{:S(2)}) async-start(s8[6291456]{0:T(1024)(128)(4,1)} %bitcast.63), calls=%async_computation.3 | async-start | bytes 8388608
  47.2 2.8 slice-start.1
  55.2 8.7 %copy-start.9 = (bf16[512,1024]{1,0:T(8,128)(2,1)}, bf16[512,1024]{1,0:T(8,128)(2,1)S(1)}, u32[]{:S(2)}) copy-start(bf16[512,1024]{1,0:T(8,128)(2,1)S(1)} %fusion.3) | copy-start | bytes 3145732
  56.7 7.3 %copy-start.11 = (bf16[512,1024]{1,0:T(8,128)(2,1)}, bf16[512,1024]{1,0:T(8,128)(2,1)S(1)}, u32[]{:S(2)}) copy-start(bf16[512,1024]{1,0:T(8,128)(2,1)S(1)} %fusion.2) | copy-start | bytes 3145732
  57.5 17.9 %copy-start.7 = (f32[512,1024]{0,1:T(8,128)S(1)}, f32[512,1024]{0,1:T(8,128)}, u32[]{:S(2)}) copy-start(f32[512,1024]{0,1:T(8,128)} %fusion.32) | copy-start | bytes 6291460
  57.5 17.9 %copy-start.8 = (f32[512,1024]{0,1:T(8,128)S(1)}, f32[512,1024]{0,1:T(8,128)}, u32[]{:S(2)}) copy-start(f32[512,1024]{0,1:T(8,128)} %fusion.30) | copy-start | bytes 6291460
  57.5 29.2 %collective-permute-start.15 = (bf16[128,1024]{1,0:T(8,128)(2,1)}, bf16[128,1024]{1,0:T(8,128)(2,1)S(1)}, u32[]{:S(2)}, u32[]{:S(2)}) collective-permute-start(bf16[128,1024]{1,0:T(8,128)(2,1)} %slice.53), channel_id=1, source_target_pairs={{4,0},{8,4},{12,8},{16,12},{20,16},{24,20},{28,24},{32,28},{36,32}... | collective-permute-start | bytes 786440 | tf_op jit(solution)/shard_map/ppermute | solution.py:377
  61.9 24.9 %collective-permute-start.13 = (bf16[128,1024]{1,0:T(8,128)(2,1)}, bf16[128,1024]{1,0:T(8,128)(2,1)}, u32[]{:S(2)}, u32[]{:S(2)}) collective-permute-start(bf16[128,1024]{1,0:T(8,128)(2,1)} %slice.50), channel_id=1, source_target_pairs={{0,4},{4,8},{8,12},{12,16},{16,20},{20,24},{24,28},{28,32},{32,36}... | collective-permute-start | bytes 786440 | tf_op jit(solution)/shard_map/ppermute | solution.py:376
  74.7 2.8 copy-start.4
  74.7 2.8 copy-start.5
  75.5 15.8 %copy-start.18 = (s32[64]{0:T(128)S(1)}, s32[64]{0:T(128)}, u32[]{:S(2)}) copy-start(s32[64]{0:T(128)} %get-tuple-element.72) | copy-start | bytes 772
  89.7 27.2 %collective-permute-start.17 = (bf16[1152,512]{1,0:T(8,128)(2,1)}, bf16[1152,512]{1,0:T(8,128)(2,1)}, u32[]{:S(2)}, u32[]{:S(2)}) collective-permute-start(bf16[1152,512]{1,0:T(8,128)(2,1)} %constant_dynamic-update-slice_fusion), channel_id=1, source_target_pairs={{1,0},{2,1},{3,2},{0,3},{5,4},{6,5},{7,6},{4,7},{9,8},{10,9},{11,1... | collective-permute-start | bytes 3538952 | tf_op jit(solution)/shard_map/ppermute | solution.py:349
  91.2 29.6 %collective-permute-start.16 = (bf16[1152,512]{1,0:T(8,128)(2,1)}, bf16[1152,512]{1,0:T(8,128)(2,1)}, u32[]{:S(2)}, u32[]{:S(2)}) collective-permute-start(bf16[1152,512]{1,0:T(8,128)(2,1)} %constant_dynamic-update-slice_fusion), channel_id=1, source_target_pairs={{0,1},{1,2},{2,3},{3,0},{4,5},{5,6},{6,7},{7,4},{8,9},{9,10},{10,1... | collective-permute-start | bytes 3538952 | tf_op jit(solution)/shard_map/ppermute | solution.py:348
  91.5 54.7 %collective-permute-start.23 = (bf16[8,2,128,256]{3,2,1,0:T(8,128)(2,1)}, bf16[8,2,128,256]{3,2,1,0:T(8,128)(2,1)S(1)}, u32[]{:S(2)}, u32[]{:S(2)}) collective-permute-start(bf16[8,2,128,256]{3,2,1,0:T(8,128)(2,1)} %copy-done.5), channel_id=1, source_target_pairs={{0,8},{4,12},{8,16},{12,20},{16,24},{20,28},{24,32},{28,36},{32,40... | collective-permute-start | bytes 3145736 | tf_op jit(solution)/shard_map/ppermute | solution.py:390
  91.8 54.4 %collective-permute-start.24 = (bf16[8,2,128,256]{3,2,1,0:T(8,128)(2,1)}, bf16[8,2,128,256]{3,2,1,0:T(8,128)(2,1)S(1)}, u32[]{:S(2)}, u32[]{:S(2)}) collective-permute-start(bf16[8,2,128,256]{3,2,1,0:T(8,128)(2,1)} %copy-done.4), channel_id=1, source_target_pairs={{0,56},{4,60},{8,0},{12,4},{16,8},{20,12},{24,16},{28,20},{32,24},... | collective-permute-start | bytes 3145736 | tf_op jit(solution)/shard_map/ppermute | solution.py:390
  94.3 51.9 %collective-permute-start.25 = (bf16[8,2,128,256]{3,2,1,0:T(8,128)(2,1)S(1)}, bf16[8,2,128,256]{3,2,1,0:T(8,128)(2,1)S(1)}, u32[]{:S(2)}, u32[]{:S(2)}) collective-permute-start(bf16[8,2,128,256]{3,2,1,0:T(8,128)(2,1)S(1)} %get-tuple-element.62), channel_id=1, source_target_pairs={{0,16},{4,52},{8,24},{12,60},{16,32},{20,4},{24,40},{28,12},{32,48... | collective-permute-start | bytes 3145736 | tf_op jit(solution)/shard_map/ppermute | solution.py:390
  118.0 13.9 %collective-permute-start.19 = (bf16[576,512]{1,0:T(8,128)(2,1)S(1)}, bf16[576,512]{1,0:T(8,128)(2,1)S(1)}, u32[]{:S(2)}, u32[]{:S(2)}) collective-permute-start(bf16[576,512]{1,0:T(8,128)(2,1)S(1)} %slice.57), channel_id=1, source_target_pairs={{1,0},{2,1},{3,2},{0,3},{5,4},{6,5},{7,6},{4,7},{9,8},{10,9},{11,1... | collective-permute-start | bytes 1769480 | tf_op jit(solution)/shard_map/ppermute | solution.py:351
  121.9 14.5 %collective-permute-start.18 = (bf16[576,512]{1,0:T(8,128)(2,1)S(1)}, bf16[576,512]{1,0:T(8,128)(2,1)S(1)}, u32[]{:S(2)}, u32[]{:S(2)}) collective-permute-start(bf16[576,512]{1,0:T(8,128)(2,1)S(1)} %slice.55), channel_id=1, source_target_pairs={{0,1},{1,2},{2,3},{3,0},{4,5},{5,6},{6,7},{7,4},{8,9},{9,10},{10,1... | collective-permute-start | bytes 1769480 | tf_op jit(solution)/shard_map/ppermute | solution.py:350
  122.2 6.3 %slice-start.2 = ((s8[6291456]{0:T(1024)(128)(4,1)}), s8[4194304]{0:T(1024)(128)(4,1)S(1)}, s32[]{:S(2)}) async-start(s8[6291456]{0:T(1024)(128)(4,1)} %bitcast.65), calls=%async_computation.5 | async-start | bytes 8388608
  125.3 3.2 slice-start.3
  132.7 6.2 %copy-start.15 = (bf16[576,1024]{1,0:T(8,128)(2,1)}, bf16[576,1024]{1,0:T(8,128)(2,1)S(1)}, u32[]{:S(2)}) copy-start(bf16[576,1024]{1,0:T(8,128)(2,1)S(1)} %fusion) | copy-start | bytes 3538948
  145.2 1.0 copy-start.2
  148.5 11.1 %copy-start.10 = (bf16[512,1024]{1,0:T(8,128)(2,1)S(1)}, bf16[512,1024]{1,0:T(8,128)(2,1)}, u32[]{:S(2)}) copy-start(bf16[512,1024]{1,0:T(8,128)(2,1)} %copy-done.9) | copy-start | bytes 3145732
  148.5 11.1 %copy-start.12 = (bf16[512,1024]{1,0:T(8,128)(2,1)S(1)}, bf16[512,1024]{1,0:T(8,128)(2,1)}, u32[]{:S(2)}) copy-start(bf16[512,1024]{1,0:T(8,128)(2,1)} %copy-done.11) | copy-start | bytes 3145732
  148.5 60.3 %all-to-all-start = ((bf16[8,4,2,128,256]{4,3,2,1,0:T(8,128)(2,1)}), bf16[8,4,2,128,256]{4,3,2,1,0:T(8,128)(2,1)}, u32[]{:S(2)}, u32[]{:S(2)}) async-start(bf16[8,4,2,128,256]{4,3,2,1,0:T(8,128)(2,1)} %merge_own.1), calls=%async_computation | async-start | bytes 8388608 | tf_op jit(solution)/shard_map/all_to_all | solution.py:396
  156.1 26.3 %collective-permute-start.20 = (bf16[8,2,128,256]{3,2,1,0:T(8,128)(2,1)}, bf16[8,2,128,256]{3,2,1,0:T(8,128)(2,1)}, u32[]{:S(2)}, u32[]{:S(2)}) collective-permute-start(bf16[8,2,128,256]{3,2,1,0:T(8,128)(2,1)} %get-tuple-element.50), channel_id=1, source_target_pairs={{0,8},{4,12},{8,16},{12,20},{16,24},{20,28},{24,32},{28,36},{32,40... | collective-permute-start | bytes 3145736 | tf_op jit(solution)/shard_map/ppermute | solution.py:390
  156.5 25.9 %collective-permute-start.21 = (bf16[8,2,128,256]{3,2,1,0:T(8,128)(2,1)}, bf16[8,2,128,256]{3,2,1,0:T(8,128)(2,1)}, u32[]{:S(2)}, u32[]{:S(2)}) collective-permute-start(bf16[8,2,128,256]{3,2,1,0:T(8,128)(2,1)} %get-tuple-element.51), channel_id=1, source_target_pairs={{0,56},{4,60},{8,0},{12,4},{16,8},{20,12},{24,16},{28,20},{32,24},... | collective-permute-start | bytes 3145736 | tf_op jit(solution)/shard_map/ppermute | solution.py:390
  158.8 45.8 %collective-permute-start.22 = (bf16[8,2,128,256]{3,2,1,0:T(8,128)(2,1)}, bf16[8,2,128,256]{3,2,1,0:T(8,128)(2,1)}, u32[]{:S(2)}, u32[]{:S(2)}) collective-permute-start(bf16[8,2,128,256]{3,2,1,0:T(8,128)(2,1)} %get-tuple-element.52), channel_id=1, source_target_pairs={{0,16},{4,52},{8,24},{12,60},{16,32},{20,4},{24,40},{28,12},{32,48... | collective-permute-start | bytes 3145736 | tf_op jit(solution)/shard_map/ppermute | solution.py:390
  159.6 45.0 %copy-start.3 = (bf16[8,2,128,256]{3,2,1,0:T(8,128)(2,1)S(1)}, bf16[8,2,128,256]{3,2,1,0:T(8,128)(2,1)}, u32[]{:S(2)}) copy-start(bf16[8,2,128,256]{3,2,1,0:T(8,128)(2,1)} %copy-done.2) | copy-start | bytes 3145732
  208.8 7.5 %copy-start.17 = (s32[1,2048]{1,0:T(1,128)S(1)}, s32[1,2048]{1,0:T(1,128)}, u32[]{:S(2)}) copy-start(s32[1,2048]{1,0:T(1,128)} %param.7) | copy-start | bytes 24580
  208.8 54.5 %all-to-all-start.1 = ((bf16[8,4,2,128,256]{4,3,2,1,0:T(8,128)(2,1)}), bf16[8,4,2,128,256]{4,3,2,1,0:T(8,128)(2,1)}, u32[]{:S(2)}, u32[]{:S(2)}) async-start(bf16[8,4,2,128,256]{4,3,2,1,0:T(8,128)(2,1)} %merge_copied.1), calls=%async_computation.1 | async-start | bytes 8388608 | tf_op jit(solution)/shard_map/all_to_all | solution.py:396
  275.5 1.4 copy-start.1
  276.8 57.8 %all-to-all-start.2 = ((bf16[64,128,128]{2,1,0:T(8,128)(2,1)}), bf16[64,128,128]{2,1,0:T(8,128)(2,1)S(1)}, u32[]{:S(2)}, u32[]{:S(2)}) async-start(bf16[64,128,128]{2,1,0:T(8,128)(2,1)} %copy-done.1), calls=%async_computation.2 | async-start | bytes 4194304 | tf_op jit(solution)/shard_map/all_to_all | solution.py:427

commit v4 on v3

--- a/solution.py
+++ b/solution.py
@@ -67,34 +67,6 @@
         compiler_params=params(),
         name=name,
     )(table, dests, pair)
-
-
-def merge_parts(parts, places, name):
-    count = sum(len(at) for at in places)
-    rest = parts[0].shape[1:]
-
-    def kernel(*refs):
-        out_ref, sems = refs[len(parts) :]
-        copies = []
-        for ref, at in zip(refs, places):
-            for i, (g, a) in enumerate(at):
-                copies.append(
-                    pltpu.make_async_copy(ref.at[i], out_ref.at[g, a], sems.at[len(copies)])
-                )
-        for copy in copies:
-            copy.start()
-        for copy in copies:
-            copy.wait()
-
-    return pl.pallas_call(
-        kernel,
-        out_shape=jax.ShapeDtypeStruct((count // 4, 4, *rest), parts[0].dtype),
-        in_specs=[pl.BlockSpec(memory_space=pltpu.VMEM)] * len(parts),
-        out_specs=pl.BlockSpec(memory_space=pltpu.HBM),
-        scratch_shapes=[pltpu.SemaphoreType.DMA((count,))],
-        compiler_params=params(),
-        name=name,
-    )(*parts)
 
 
 def take_tiles(index, tiles):
@@ -180,12 +152,19 @@
     items = rows * heads
     slots = items * rand
     share = slots // len(tiles)
+    spots = share // 2
 
     def kernel(slot_ref, count_ref, target_ref, q_ref, acc_ref, stat_ref, *refs):
         out_ref, buffer, done, in_sems, out_sems = refs[len(tiles) :]
+        pairs = []
+        for n in range(len(tiles)):
+            if n % 4:
+                pairs.append((refs[n], buffer.at[n]))
+            else:
+                pairs += [(refs[n].at[g, 0], buffer.at[n, pl.ds(2 * g, 2)]) for g in range(spots)]
         copies = [
-            pltpu.make_async_copy(refs[n], buffer.at[pl.ds(n * share, share)], in_sems.at[n])
-            for n in range(len(tiles))
+            pltpu.make_async_copy(source, place, in_sems.at[n])
+            for n, (source, place) in enumerate(pairs)
         ]
 
         def deliver(i):
@@ -200,7 +179,8 @@
             at = pl.ds(pl.multiple_of(r * blk, blk), blk)
             each = range(heads)
             places = [[slot_ref[(first + e) * rand + j] for j in range(rand)] for e in each]
-            keys = [jnp.concatenate([buffer[p, :, :hd] for p in places[e]], axis=0) for e in each]
+            places = [[(p // share, p % share) for p in at_e] for at_e in places]
+            keys = [jnp.concatenate([buffer[n, i, :, :hd] for n, i in places[e]], axis=0) for e in each]
             scores = [dot_t(keys[e], q_ref[at, e * hd : (e + 1) * hd]) for e in each]
             scores = [
                 jnp.where(key < count_ref[first + e] * blk, scores[e] * factor, NEG) for e in each
@@ -211,7 +191,7 @@
             keep = [jnp.exp2(top0[e] - top[e]) for e in each]
             expo = [jnp.exp2(scores[e] - top[e]) for e in each]
             total = [total0[e] * keep[e] + jnp.sum(expo[e], axis=0, keepdims=True) for e in each]
-            values = [jnp.concatenate([buffer[p, :, hd:] for p in places[e]], axis=1) for e in each]
+            values = [jnp.concatenate([buffer[n, i, :, hd:] for n, i in places[e]], axis=1) for e in each]
             summed = [acc_ref[first + e] * keep[e] + dot(values[e], expo[e].astype(BF)) for e in each]
             for e in each:
                 done[first + e] = (summed[e] / total[e]).T.astype(BF)
@@ -236,9 +216,9 @@
             in_specs=[vmem, vmem, vmem, *[anywhere] * len(tiles)],
             out_specs=pl.BlockSpec(memory_space=pltpu.HBM),
             scratch_shapes=[
-                pltpu.VMEM((slots, blk, 2 * hd), BF),
+                pltpu.VMEM((len(tiles), share, blk, 2 * hd), BF),
                 pltpu.VMEM((items, blk, hd), BF),
-                pltpu.SemaphoreType.DMA((len(tiles),)),
+                pltpu.SemaphoreType.DMA((len(tiles) * 3 // 4 + 2 * spots,)),
                 pltpu.SemaphoreType.DMA((items,)),
             ],
         ),
@@ -290,10 +270,11 @@
 
     far_z = device(my_x, my_z + NZ // 2, my_core)
     tables = (held_for(me), held_for(far_z))
-    spot = jnp.arange(NX * NC, dtype=jnp.int32)
-    dests = jnp.concatenate(
-        [device(spot // NC, my_z + step, spot % NC) for step in (0, 1, -1, 2 - 4 * my_core)]
-    ).astype(jnp.int32)
+    goal = jnp.arange(4 * NX * NC, dtype=jnp.int32)
+    spot, kind = goal // 4, goal % 4
+    two = 2 - 4 * (spot % NC)
+    z_move = jnp.where(kind == 3, two, jnp.where(kind == 2, -1, kind))
+    dests = device(spot // NC, my_z + z_move, spot % NC).astype(jnp.int32)
 
     wanted = lax.dynamic_index_in_dim(asked, me, 0, keepdims=False)
     source = wanted // rows
@@ -303,18 +284,17 @@
     )
     step = (my_z - source // NC) % NZ
     source_spot = source // (NZ * NC) * NC + source % NC
-    source_two = (2 - 4 * (source % NC)) % NZ
+    my_two = (2 - 4 * my_core) % NZ
 
     def route_kind(step):
         return jnp.where(
-            step == 0, 0, jnp.where(step == 1, 1, jnp.where(step == NZ - 1, 2, jnp.where(step == source_two, 3, -1)))
+            step == 0, 0, jnp.where(step == 1, 1, jnp.where(step == NZ - 1, 2, jnp.where(step == my_two, 3, -1)))
         )
 
     near_kind = route_kind(step)
     other_kind = route_kind((step + NZ // 2) % NZ)
     half = (near_kind < 0).astype(jnp.int32)
-    slot = source_spot * 4 + jnp.where(half == 1, other_kind, near_kind)
-    slot = half * (items * rand // 2) + slot * 2 + rank
+    slot = jnp.where(half == 1, 4 + other_kind, near_kind) * (2 * NX * NC) + source_spot * 2 + rank
 
     my_used = lax.dynamic_slice_in_dim(rand_used, me * rows, rows, axis=1).T.reshape(-1)
     number = jnp.arange(items, dtype=jnp.int32)
@@ -379,49 +359,46 @@
     planes = [[device(x, z, c) for x in range(NX) for c in range(NC)] for z in range(NZ)]
 
     def pack(table, pair, name):
-        return pack_tiles(table, dests, pair, [NX * NC] * 4, rows, heads, blk, hd, name)
-
-    def shifted(parts):
+        (packed,) = pack_tiles(table, dests, pair, [4 * NX * NC], rows, heads, blk, hd, name)
+        return packed.reshape(NX * NC, 4, 2, blk, 2 * hd)
+
+    def in_plane(block):
+        return lax.all_to_all(
+            block, "seq", split_axis=0, concat_axis=0, axis_index_groups=planes, tiled=True
+        )
+
+    def along_z(got):
         goals = [
             lambda x, z, c: (x, z + 1, c),
             lambda x, z, c: (x, z - 1, c),
             lambda x, z, c: (x, z + 2 - 4 * c, c),
         ]
-        moved = [lax.ppermute(part, "seq", seq_pairs(goal)) for part, goal in zip(parts[1:], goals)]
-        return [parts[0], *moved]
-
-    places = [[(g, a) for g in range(NX * NC)] for a in range(4)]
-
-    def in_plane(block):
-        got = lax.all_to_all(
-            block, "seq", split_axis=0, concat_axis=0, axis_index_groups=planes, tiled=True
-        )
-        return got.reshape(-1, blk, 2 * hd)
-
-    own_parts = pack(tables[0], pair, "pack_own")
-    own_parts, far_top, far_bottom = lax.optimization_barrier((own_parts, far_top, far_bottom))
+        moved = [
+            lax.ppermute(got[:, k].reshape(-1, blk, 2 * hd), "seq", seq_pairs(goal))
+            for k, goal in enumerate(goals, 1)
+        ]
+        return [got, *moved]
+
+    own_block = pack(tables[0], pair, "pack_own")
+    own_block, far_top, far_bottom = lax.optimization_barrier((own_block, far_top, far_bottom))
     far = jnp.concatenate([far_top, far_bottom], axis=0)
     query = dot(far, w_query(2)) + dot(tokens, w_query(0))
     query = (query + dot(from_low, w_query(3)) + dot(from_high, w_query(1))).astype(BF)
     copied, zero, before, after, query = lax.optimization_barrier(
         (copied, zero, before, after, query)
     )
-    own_parts = shifted(own_parts)
+    own_parts = along_z(in_plane(own_block))
     copied = jnp.concatenate([copied, zero], axis=0)
     copied_ring = ring(copied)
     copied_pair = keys_values(copied, *copied_ring)
-    copied_parts = pack(tables[1], copied_pair, "pack_copied")
-    own_parts, _ = lax.optimization_barrier((own_parts, copied_parts))
-    copied_parts = shifted(copied_parts)
-    own_tiles = in_plane(merge_parts(own_parts, places, "merge_own"))
-
+    copied_block = pack(tables[1], copied_pair, "pack_copied")
     around = jnp.concatenate([before, pair, after], axis=0)
     first = copied_pair[count:]
     acc, stat = near_attend(edges, query, around, first, rows, heads, blk, hd, factor)
-    copied_parts, acc, stat = lax.optimization_barrier((copied_parts, acc, stat))
-    copied_tiles = in_plane(merge_parts(copied_parts, places, "merge_copied"))
+    copied_got, acc, stat = lax.optimization_barrier((in_plane(copied_block), acc, stat))
+    copied_parts = along_z(copied_got)
     done = rand_attend(
-        slot, my_used, target, query, (own_tiles, copied_tiles), acc, stat,
+        slot, my_used, target, query, (*own_parts, *copied_parts), acc, stat,
         rows, heads, blk, hd, rand, peers, factor,
     )
     back = lax.all_to_all(done, "seq", split_axis=0, concat_axis=0, tiled=True)

time: 338 us -> 362 us (1.071)
  starting transfers between devices: 52.9 us -> 80.7 us
  Pallas kernels: 45.4 us -> 31 us
  local copies, waits for them, and re-layouts: 12.4 us -> 20.8 us
    ppermute x6, waiting for transfers between devices: 33.3 us -> 52.9 us  [along_z(): lax.ppermute(got[:, k].reshape(-1, blk, 2 * hd), 'seq', seq_pairs(goal))]
    ppermute x1, starting transfers between devices: 4.33 us -> 22.1 us  [local(): after = lax.ppermute(pair[:blk], 'seq', down)]
    all_to_all x2, waiting for transfers between devices: 46.8 us -> 29.3 us  [in_plane(): lax.all_to_all(block, 'seq', split_axis=0, concat_axis=0, axis_index_grou...]
    ppermute x1, waiting for transfers between devices: 9.23 us -> 0.01 us  [local(): lax.ppermute(copied, 'seq', seq_pairs(lambda x, z, c: (x, z + NZ // 2, c)))]
    pallas_call x2, Pallas kernels: 15.6 us -> 7.2 us  [pack_tiles(): pl.pallas_call(kernel, out_shape=[jax.ShapeDtypeStruct((share, 2, blk, 2...]
    slice x0 -> x2, local copies, waits for them, and re-layouts: none -> 7.37 us  [along_z(): got[:, k].reshape(-1, blk, 2 * hd)]
    pallas_call x2 -> x0, Pallas kernels: 6.48 us -> none  [merge_parts(): pl.pallas_call(kernel, out_shape=jax.ShapeDtypeStruct((count // 4, 4, *re...]
    ppermute x1, starting transfers between devices: 2.1 us -> 8.08 us  [local(): before = lax.ppermute(pair[-blk:], 'seq', up)]
  transfers between devices with their start and end apart: 29 -> 29, of which waited for: 12 -> 12; matrix products, arithmetic and copies ran while one was open for 13% -> 18% of each run, Pallas kernels for 9% -> 5%
where the time goes in v4:
time: 362 us; the launch traced here: 360 us
  waiting for transfers between devices  183 us (51%)
  starting transfers between devices  80.7 us (22%)
  matrix products  33.9 us (9%)
  Pallas kernels  31 us (9%)
  local copies, waits for them, and re-layouts  20.8 us (6%)
  other arithmetic  10.3 us (3%)
    ppermute x6, waiting for transfers between devices, along_z(): lax.ppermute(got[:, k].reshape(-1, blk, 2 * hd), 'seq', seq_pairs(goal))  52.9 us
    all_to_all x1, waiting for transfers between devices, local(): back = lax.all_to_all(done, 'seq', split_axis=0, concat_axis=0, tiled=True)  51.2 us
    dot_general x14, matrix products, dot(): return jnp.dot(a, b, preferred_element_type=F32)  33.9 us
    all_to_all x2, waiting for transfers between devices, in_plane(): lax.all_to_all(block, 'seq', split_axis=0, concat_axis=0, axis_index_grou...  29.3 us
    ppermute x2, waiting for transfers between devices, ring(): high = lax.ppermute(part, 'head', backward)  25.8 us
    ppermute x1, starting transfers between devices, local(): after = lax.ppermute(pair[:blk], 'seq', down)  22.1 us
    all_to_all x2, starting transfers between devices, in_plane(): lax.all_to_all(block, 'seq', split_axis=0, concat_axis=0, axis_index_grou...  15.7 us
    pallas_call x1, Pallas kernels, rand_attend(): pl.pallas_call(kernel, out_shape=jax.ShapeDtypeStruct((peers, blk, hd), B...  12.7 us
  transfers between devices with their start and end apart: 29, of which 12 were waited for; matrix products, arithmetic and copies ran while one was open for 18% of the time, Pallas kernels for 5%

profile of v4, /device:TPU:1, one launch (start us, length us, event | category | flops | bytes accessed | tf_op | source)
XLA Modules:
  0.0 360.5 jit_solution(1882344783413025828)
XLA Ops:
  0.0 2.1 collective-permute-start.10
  2.1 1.5 collective-permute-start.11
  3.7 0.9 slice_select_fusion
  6.0 1.3 collective-permute-start.2
  7.9 4.8 %fusion.16 = f32[1024,1024]{0,1:T(8,128)} fusion(bf16[1024,512]{1,0:T(8,128)(2,1)} %param.5, bf16[2048,1536]{1,0:T(8,128)(2,1)} %param.6, s32[]{:T(128)S(6)} %select_n.376), kind=kOutput, calls=%fused_computation.29 | convolution fusion | flops 1073741824 | bytes 6291460 | tf_op jit(solution)/shard_map/dot_general | solution.py:17
  12.7 1.7 fusion.32
  14.4 1.9 reshape.309
  16.3 1.5 broadcast_compare_fusion.1
  17.8 2.2 select_reduce_fusion.1
  20.0 1.0 add_add_fusion.2
  21.0 1.3 collective-permute-start.3
  23.7 9.6 %collective-permute-done.3 = bf16[128,512]{1,0:T(8,128)(2,1)S(1)} collective-permute-done((bf16[128,512]{1,0:T(8,128)(2,1)S(1)}, bf16[128,512]{1,0:T(8,128)(2,1)S(1)}, u32[]{:S(2)}, u32[]{:S(2)}) %collective-permute-start.3) | collective-permute-done | bytes 131104 | tf_op jit(solution)/shard_map/ppermute | solution.py:320
  33.3 1.3 collective-permute-start.7
  34.6 1.3 collective-permute-start.8
  35.9 1.3 collective-permute-start.9
  37.9 1.2 collective-permute-done.9
  39.2 1.2 slice.76
  40.6 1.1 slice.73
  41.7 2.7 collective-permute-start.12
  44.3 2.8 fusion.13
  47.1 2.8 add_bitcast_fusion
  50.0 3.4 fusion.30
  53.4 2.1 fusion.3
  56.3 3.0 fusion.2
  59.3 1.7 slice.77
  60.9 1.5 pad_maximum_fusion.2.pair_ref
  62.4 3.6 %pack_own.1 = bf16[32,2,128,256]{3,2,1,0:T(8,128)(2,1)} custom-call(s32[128]{0:T(128)S(1)} %reshape.312.table_ref, s32[32]{0:T(128)S(1)} %multiply_add_fusion.1.dest_ref, bf16[1024,1024]{1,0:T(8,128)(2,1)S(1)} %pad_maximum_fusion.2.pair_ref), custom_call_target="tpu_custom_call" | custom-call | tf_op jit(solution)/shard_map/pack_own/pallas_call | solution.py:54
  66.1 8.1 %collective-permute-start.13 = (bf16[128,1024]{1,0:T(8,128)(2,1)}, bf16[128,1024]{1,0:T(8,128)(2,1)S(1)}, u32[]{:S(2)}, u32[]{:S(2)}) collective-permute-start(bf16[128,1024]{1,0:T(8,128)(2,1)} %slice.74), channel_id=1, source_target_pairs={{0,4},{4,8},{8,12},{12,16},{16,20},{20,24},{24,28},{28,32},{32,36}... | collective-permute-start | bytes 786440 | tf_op jit(solution)/shard_map/ppermute | solution.py:356
  74.1 22.1 %collective-permute-start.15 = (bf16[128,1024]{1,0:T(8,128)(2,1)}, bf16[128,1024]{1,0:T(8,128)(2,1)}, u32[]{:S(2)}, u32[]{:S(2)}) collective-permute-start(bf16[128,1024]{1,0:T(8,128)(2,1)} %slice.77), channel_id=1, source_target_pairs={{4,0},{8,4},{12,8},{16,12},{20,16},{24,20},{28,24},{32,28},{36,32}... | collective-permute-start | bytes 786440 | tf_op jit(solution)/shard_map/ppermute | solution.py:357
  96.2 9.4 %all-to-all-start.1 = ((bf16[8,4,2,128,256]{4,3,2,1,0:T(8,128)(2,1)}), bf16[8,4,2,128,256]{4,3,2,1,0:T(8,128)(2,1)}, u32[]{:S(2)}, u32[]{:S(2)}) async-start(bf16[8,4,2,128,256]{4,3,2,1,0:T(8,128)(2,1)} %bitcast.71), calls=%async_computation.1 | async-start | bytes 8388608 | tf_op jit(solution)/shard_map/all_to_all | solution.py:366
  105.6 2.1 fusion.5
  107.7 2.2 fusion.4.q_ref
  110.0 1.4 constant_dynamic-update-slice_fusion.1
  111.4 1.7 collective-permute-start.17
  113.4 25.8 %collective-permute-done.17 = bf16[1152,512]{1,0:T(8,128)(2,1)S(1)} collective-permute-done((bf16[1152,512]{1,0:T(8,128)(2,1)S(1)}, bf16[1152,512]{1,0:T(8,128)(2,1)S(1)}, u32[]{:S(2)}, u32[]{:S(2)}) %collective-permute-start.17) | collective-permute-done | bytes 1179680 | tf_op jit(solution)/shard_map/ppermute | solution.py:329
  139.2 2.9 collective-permute-start.19
  142.1 3.1 fusion.11
  145.3 2.9 convolution_add_fusion.1
  148.2 1.1 slice.79
  149.4 1.4 convolution_add_fusion
  150.8 3.3 collective-permute-done.19
  154.1 0.8 fusion
  154.9 9.5 %collective-permute-done.18 = bf16[576,512]{1,0:T(8,128)(2,1)S(1)} collective-permute-done((bf16[576,512]{1,0:T(8,128)(2,1)S(1)}, bf16[576,512]{1,0:T(8,128)(2,1)S(1)}, u32[]{:S(2)}, u32[]{:S(2)}) %collective-permute-start.18) | collective-permute-done | bytes 589856 | tf_op jit(solution)/shard_map/ppermute | solution.py:330
  164.4 0.8 fusion.1
  165.4 3.6 pack_copied.1
  169.0 6.3 %all-to-all-start = ((bf16[8,4,2,128,256]{4,3,2,1,0:T(8,128)(2,1)}), bf16[8,4,2,128,256]{4,3,2,1,0:T(8,128)(2,1)}, u32[]{:S(2)}, u32[]{:S(2)}) async-start(bf16[8,4,2,128,256]{4,3,2,1,0:T(8,128)(2,1)} %bitcast.72), calls=%async_computation | async-start | bytes 8388608 | tf_op jit(solution)/shard_map/all_to_all | solution.py:366
  175.4 3.7 %fusion.79 = (bf16[8,1,2,128,256]{4,3,2,1,0:T(8,128)(2,1)}, bf16[8,1,2,128,256]{4,3,2,1,0:T(8,128)(2,1)}, bf16[8,1,2,128,256]{4,3,2,1,0:T(8,128)(2,1)}) fusion(bf16[8,4,2,128,256]{4,3,2,1,0:T(8,128)(2,1)} %all-to-all-done.1.refs_0_), kind=kLoop, calls=%fused_computation.199 | loop fusion | bytes 6291456 | tf_op jit(solution)/shard_map/slice | solution.py:377
  179.2 1.5 pad_maximum_fusion.kv_ref
  180.7 1.0 slice.82.first_ref
  181.6 9.4 %near_attend.1 = (f32[32,128,128]{2,1,0:T(8,128)S(1)}, f32[32,8,128]{2,1,0:T(8,128)S(1)}) custom-call(s32[2]{0:T(128)S(1)} %add_convert_fusion.edge_ref, bf16[1024,512]{1,0:T(8,128)(2,1)S(1)} %fusion.4.q_ref, bf16[1280,1024]{1,0:T(8,128)(2,1)S(1)} %pad_maximum_fusion.kv_ref, bf16[128,1024]{1,0:T(8,128)(2,1)S(1)} %slice.82.first_ref), custom_call_target="tpu_custom_call" | custom-call | tf_op jit(solution)/shard_map/near_attend/pallas_call | solution.py:127
  191.0 1.3 copy-done.1
  192.3 2.7 collective-permute-start.21
  195.0 29.3 %all-to-all-done.refs_4_ = bf16[8,4,2,128,256]{4,3,2,1,0:T(8,128)(2,1)} async-done(((bf16[8,4,2,128,256]{4,3,2,1,0:T(8,128)(2,1)}), bf16[8,4,2,128,256]{4,3,2,1,0:T(8,128)(2,1)}, u32[]{:S(2)}, u32[]{:S(2)}) %all-to-all-start) | async-done | bytes 4194336 | tf_op jit(solution)/shard_map/all_to_all | solution.py:366
  224.3 3.7 %fusion.78 = (bf16[8,1,2,128,256]{4,3,2,1,0:T(8,128)(2,1)}, bf16[8,1,2,128,256]{4,3,2,1,0:T(8,128)(2,1)}, bf16[8,1,2,128,256]{4,3,2,1,0:T(8,128)(2,1)}) fusion(bf16[8,4,2,128,256]{4,3,2,1,0:T(8,128)(2,1)} %all-to-all-done.refs_4_), kind=kLoop, calls=%fused_computation.198 | loop fusion | bytes 6291456 | tf_op jit(solution)/shard_map/slice | solution.py:377
  228.0 2.7 collective-permute-start.24
  230.6 1.2 copy.27
  232.8 13.8 %collective-permute-done.22.refs_3_ = bf16[16,128,256]{2,1,0:T(8,128)(2,1)} collective-permute-done((bf16[16,128,256]{2,1,0:T(8,128)(2,1)}, bf16[16,128,256]{2,1,0:T(8,128)(2,1)}, u32[]{:S(2)}, u32[]{:S(2)}) %collective-permute-start.22) | collective-permute-done | bytes 1048608 | tf_op jit(solution)/shard_map/ppermute | solution.py:377
  246.6 6.9 %collective-permute-done.23.refs_5_ = bf16[16,128,256]{2,1,0:T(8,128)(2,1)} collective-permute-done((bf16[16,128,256]{2,1,0:T(8,128)(2,1)}, bf16[16,128,256]{2,1,0:T(8,128)(2,1)}, u32[]{:S(2)}, u32[]{:S(2)}) %collective-permute-start.23) | collective-permute-done | bytes 1048608 | tf_op jit(solution)/shard_map/ppermute | solution.py:377
  253.6 11.4 %collective-permute-done.24.refs_6_ = bf16[16,128,256]{2,1,0:T(8,128)(2,1)} collective-permute-done((bf16[16,128,256]{2,1,0:T(8,128)(2,1)}, bf16[16,128,256]{2,1,0:T(8,128)(2,1)}, u32[]{:S(2)}, u32[]{:S(2)}) %collective-permute-start.24) | collective-permute-done | bytes 1048608 | tf_op jit(solution)/shard_map/ppermute | solution.py:377
  265.0 20.8 %collective-permute-done.25.refs_7_ = bf16[16,128,256]{2,1,0:T(8,128)(2,1)} collective-permute-done((bf16[16,128,256]{2,1,0:T(8,128)(2,1)}, bf16[16,128,256]{2,1,0:T(8,128)(2,1)}, u32[]{:S(2)}, u32[]{:S(2)}) %collective-permute-start.25) | collective-permute-done | bytes 1048608 | tf_op jit(solution)/shard_map/ppermute | solution.py:377
  285.7 12.7 %rand_attend.1 = bf16[64,128,128]{2,1,0:T(8,128)(2,1)} custom-call(s32[128]{0:T(128)S(1)} %add_add_fusion.4.slot_ref, s32[32]{0:T(128)S(1)} %reshape.311.count_ref, s32[32]{0:T(128)S(1)} %select_reduce_fusion.4.target_ref, bf16[1024,512]{1,0:T(8,128)(2,1)S(1)} %fusion.4.q_ref, f32[32,128,128]{2,1,0:T(8,128)} %copy-done.1, ...), custom_call_target="tpu_custom_call" | custom-call | tf_op jit(solution)/shard_map/rand_attend/pallas_call | solution.py:210
  298.4 8.9 %all-to-all-start.2 = ((bf16[64,128,128]{2,1,0:T(8,128)(2,1)}), bf16[64,128,128]{2,1,0:T(8,128)(2,1)S(1)}, u32[]{:S(2)}, u32[]{:S(2)}) async-start(bf16[64,128,128]{2,1,0:T(8,128)(2,1)} %rand_attend.1), calls=%async_computation.2 | async-start | bytes 4194304 | tf_op jit(solution)/shard_map/all_to_all | solution.py:404
  307.4 51.2 %all-to-all-done.2.in_ref = bf16[64,128,128]{2,1,0:T(8,128)(2,1)S(1)} async-done(((bf16[64,128,128]{2,1,0:T(8,128)(2,1)}), bf16[64,128,128]{2,1,0:T(8,128)(2,1)S(1)}, u32[]{:S(2)}, u32[]{:S(2)}) %all-to-all-start.2) | async-done | bytes 2097184 | tf_op jit(solution)/shard_map/all_to_all | solution.py:404
  358.5 1.8 take_tiles.1
  (88 shorter events, 6.6 us)
Async XLA Ops:
  0.0 231.9 %copy-start = (s32[4,512]{1,0:T(4,128)S(1)}, s32[4,512]{1,0:T(4,128)}, u32[]{:S(2)}) copy-start(s32[4,512]{1,0:T(4,128)} %param.9) | copy-start | bytes 24580
  0.0 12.7 %copy-start.6 = (bf16[1024,512]{1,0:T(8,128)(2,1)S(1)}, bf16[1024,512]{1,0:T(8,128)(2,1)}, u32[]{:S(2)}) copy-start(bf16[1024,512]{1,0:T(8,128)(2,1)} %param.5) | copy-start | bytes 3145732
  0.0 39.2 %collective-permute-start.10 = (bf16[1024,512]{1,0:T(8,128)(2,1)}, bf16[1024,512]{1,0:T(8,128)(2,1)}, u32[]{:S(2)}, u32[]{:S(2)}) collective-permute-start(bf16[1024,512]{1,0:T(8,128)(2,1)} %param.5), channel_id=1, source_target_pairs={{0,1},{1,2},{2,3},{3,0},{4,5},{5,6},{6,7},{7,4},{8,9},{9,10},{10,1... | collective-permute-start | bytes 3145736 | tf_op jit(solution)/shard_map/ppermute | solution.py:328
  2.1 38.5 %collective-permute-start.11 = (bf16[1024,512]{1,0:T(8,128)(2,1)}, bf16[1024,512]{1,0:T(8,128)(2,1)}, u32[]{:S(2)}, u32[]{:S(2)}) collective-permute-start(bf16[1024,512]{1,0:T(8,128)(2,1)} %param.5), channel_id=1, source_target_pairs={{1,0},{2,1},{3,2},{0,3},{5,4},{6,5},{7,6},{4,7},{9,8},{10,9},{11,1... | collective-permute-start | bytes 3145736 | tf_op jit(solution)/shard_map/ppermute | solution.py:329
  4.6 15.4 %collective-permute-start = (bf16[128,512]{1,0:T(8,128)(2,1)S(1)}, bf16[128,512]{1,0:T(8,128)(2,1)S(1)}, u32[]{:S(2)}, u32[]{:S(2)}) collective-permute-start(bf16[128,512]{1,0:T(8,128)(2,1)S(1)} %slice_select_fusion), channel_id=1, source_target_pairs={{0,16},{1,17},{2,18},{3,19}} | collective-permute-start | bytes 393224 | tf_op jit(solution)/shard_map/ppermute | solution.py:320
  5.3 14.7 %collective-permute-start.1 = (bf16[128,512]{1,0:T(8,128)(2,1)S(1)}, bf16[128,512]{1,0:T(8,128)(2,1)S(1)}, u32[]{:S(2)}, u32[]{:S(2)}) collective-permute-start(bf16[128,512]{1,0:T(8,128)(2,1)S(1)} %slice_select_fusion), channel_id=1, source_target_pairs={{0,32},{1,33},{2,34},{3,35}} | collective-permute-start | bytes 393224 | tf_op jit(solution)/shard_map/ppermute | solution.py:320
  6.0 14.1 %collective-permute-start.2 = (bf16[128,512]{1,0:T(8,128)(2,1)S(1)}, bf16[128,512]{1,0:T(8,128)(2,1)}, u32[]{:S(2)}, u32[]{:S(2)}) collective-permute-start(bf16[128,512]{1,0:T(8,128)(2,1)S(1)} %slice_select_fusion), channel_id=1, source_target_pairs={{0,48},{1,49},{2,50},{3,51}} | collective-permute-start | bytes 393224 | tf_op jit(solution)/shard_map/ppermute | solution.py:320
  21.0 12.3 %collective-permute-start.3 = (bf16[128,512]{1,0:T(8,128)(2,1)S(1)}, bf16[128,512]{1,0:T(8,128)(2,1)S(1)}, u32[]{:S(2)}, u32[]{:S(2)}) collective-permute-start(bf16[128,512]{1,0:T(8,128)(2,1)S(1)} %add_add_fusion.2), channel_id=1, source_target_pairs={{0,4},{16,20},{32,36},{48,52},{1,5},{17,21},{33,37},{49,53},{2,6},... | collective-permute-start | bytes 393224 | tf_op jit(solution)/shard_map/ppermute | solution.py:320
  22.3 11.0 %collective-permute-start.4 = (bf16[128,512]{1,0:T(8,128)(2,1)S(1)}, bf16[128,512]{1,0:T(8,128)(2,1)S(1)}, u32[]{:S(2)}, u32[]{:S(2)}) collective-permute-start(bf16[128,512]{1,0:T(8,128)(2,1)S(1)} %add_add_fusion.2), channel_id=1, source_target_pairs={{0,8},{16,24},{32,40},{48,56},{1,9},{17,25},{33,41},{49,57},{2,10}... | collective-permute-start | bytes 393224 | tf_op jit(solution)/shard_map/ppermute | solution.py:320
  23.0 10.3 %collective-permute-start.5 = (bf16[128,512]{1,0:T(8,128)(2,1)S(1)}, bf16[128,512]{1,0:T(8,128)(2,1)S(1)}, u32[]{:S(2)}, u32[]{:S(2)}) collective-permute-start(bf16[128,512]{1,0:T(8,128)(2,1)S(1)} %add_add_fusion.2), channel_id=1, source_target_pairs={{0,12},{16,28},{32,44},{48,60},{1,13},{17,29},{33,45},{49,61},{2,1... | collective-permute-start | bytes 393224 | tf_op jit(solution)/shard_map/ppermute | solution.py:320
  33.3 4.3 %collective-permute-start.7 = (bf16[128,512]{1,0:T(8,128)(2,1)S(1)}, bf16[128,512]{1,0:T(8,128)(2,1)S(1)}, u32[]{:S(2)}, u32[]{:S(2)}) collective-permute-start(bf16[128,512]{1,0:T(8,128)(2,1)S(1)} %add_add_fusion.1), channel_id=1, source_target_pairs={{0,64},{4,68},{8,72},{12,76},{16,80},{20,84},{24,88},{28,92},{32,9... | collective-permute-start | bytes 393224 | tf_op jit(solution)/shard_map/ppermute | solution.py:320
  34.6 3.3 collective-permute-start.8
  35.9 3.2 collective-permute-start.9
  37.6 72.4 %collective-permute-start.6 = (bf16[1024,512]{1,0:T(8,128)(2,1)}, bf16[1024,512]{1,0:T(8,128)(2,1)}, u32[]{:S(2)}, u32[]{:S(2)}) collective-permute-start(bf16[1024,512]{1,0:T(8,128)(2,1)} %param.5), channel_id=1, source_target_pairs={{0,32},{4,36},{8,40},{12,44},{16,48},{20,52},{24,56},{28,60},{32,0... | collective-permute-start | bytes 3145736 | tf_op jit(solution)/shard_map/ppermute | solution.py:350
  39.2 8.0 %copy-start.2 = (f32[1024,1024]{0,1:T(8,128)S(1)}, f32[1024,1024]{0,1:T(8,128)}, u32[]{:S(2)}) copy-start(f32[1024,1024]{0,1:T(8,128)} %fusion.16) | copy-start | bytes 12582916
  40.4 15.9 %collective-permute-start.14 = (bf16[512,512]{1,0:T(8,128)(2,1)S(1)}, bf16[512,512]{1,0:T(8,128)(2,1)S(1)}, u32[]{:S(2)}, u32[]{:S(2)}) collective-permute-start(bf16[512,512]{1,0:T(8,128)(2,1)S(1)} %slice.76), channel_id=1, source_target_pairs={{0,1},{1,2},{2,3},{3,0},{4,5},{5,6},{6,7},{7,4},{8,9},{9,10},{10,1... | collective-permute-start | bytes 1572872 | tf_op jit(solution)/shard_map/ppermute | solution.py:330
  41.7 11.7 %collective-permute-start.12 = (bf16[512,512]{1,0:T(8,128)(2,1)S(1)}, bf16[512,512]{1,0:T(8,128)(2,1)S(1)}, u32[]{:S(2)}, u32[]{:S(2)}) collective-permute-start(bf16[512,512]{1,0:T(8,128)(2,1)S(1)} %slice.73), channel_id=1, source_target_pairs={{1,0},{2,1},{3,2},{0,3},{5,4},{6,5},{7,6},{4,7},{9,8},{10,9},{11,1... | collective-permute-start | bytes 1572872 | tf_op jit(solution)/shard_map/ppermute | solution.py:331
  53.4 5.9 %copy-start.8 = (bf16[512,512]{1,0:T(8,128)(2,1)}, bf16[512,512]{1,0:T(8,128)(2,1)S(1)}, u32[]{:S(2)}) copy-start(bf16[512,512]{1,0:T(8,128)(2,1)S(1)} %collective-permute-done.12) | copy-start | bytes 1572868
  55.5 5.4 %copy-start.4 = (bf16[512,1024]{1,0:T(8,128)(2,1)}, bf16[512,1024]{1,0:T(8,128)(2,1)S(1)}, u32[]{:S(2)}) copy-start(bf16[512,1024]{1,0:T(8,128)(2,1)S(1)} %fusion.3) | copy-start | bytes 3145732
  66.1 43.9 %collective-permute-start.13 = (bf16[128,1024]{1,0:T(8,128)(2,1)}, bf16[128,1024]{1,0:T(8,128)(2,1)S(1)}, u32[]{:S(2)}, u32[]{:S(2)}) collective-permute-start(bf16[128,1024]{1,0:T(8,128)(2,1)} %slice.74), channel_id=1, source_target_pairs={{0,4},{4,8},{8,12},{12,16},{16,20},{20,24},{24,28},{28,32},{32,36}... | collective-permute-start | bytes 786440 | tf_op jit(solution)/shard_map/ppermute | solution.py:356
  74.1 35.8 %collective-permute-start.15 = (bf16[128,1024]{1,0:T(8,128)(2,1)}, bf16[128,1024]{1,0:T(8,128)(2,1)}, u32[]{:S(2)}, u32[]{:S(2)}) collective-permute-start(bf16[128,1024]{1,0:T(8,128)(2,1)} %slice.77), channel_id=1, source_target_pairs={{4,0},{8,4},{12,8},{16,12},{20,16},{24,20},{28,24},{32,28},{36,32}... | collective-permute-start | bytes 786440 | tf_op jit(solution)/shard_map/ppermute | solution.py:357
  96.2 72.8 %all-to-all-start.1 = ((bf16[8,4,2,128,256]{4,3,2,1,0:T(8,128)(2,1)}), bf16[8,4,2,128,256]{4,3,2,1,0:T(8,128)(2,1)}, u32[]{:S(2)}, u32[]{:S(2)}) async-start(bf16[8,4,2,128,256]{4,3,2,1,0:T(8,128)(2,1)} %bitcast.71), calls=%async_computation.1 | async-start | bytes 8388608 | tf_op jit(solution)/shard_map/all_to_all | solution.py:366
  105.6 2.1 copy-start.3
  107.7 5.4 %copy-start.12 = (s32[64]{0:T(128)S(1)}, s32[64]{0:T(128)}, u32[]{:S(2)}) copy-start(s32[64]{0:T(128)} %get-tuple-element.36) | copy-start | bytes 772
  109.9 1.4 copy-start.9
  111.4 27.8 %collective-permute-start.17 = (bf16[1152,512]{1,0:T(8,128)(2,1)S(1)}, bf16[1152,512]{1,0:T(8,128)(2,1)S(1)}, u32[]{:S(2)}, u32[]{:S(2)}) collective-permute-start(bf16[1152,512]{1,0:T(8,128)(2,1)S(1)} %constant_dynamic-update-slice_fusion), channel_id=1, source_target_pairs={{1,0},{2,1},{3,2},{0,3},{5,4},{6,5},{7,6},{4,7},{9,8},{10,9},{11,1... | collective-permute-start | bytes 3538952 | tf_op jit(solution)/shard_map/ppermute | solution.py:329
  113.1 29.0 %collective-permute-start.16 = (bf16[1152,512]{1,0:T(8,128)(2,1)S(1)}, bf16[1152,512]{1,0:T(8,128)(2,1)}, u32[]{:S(2)}, u32[]{:S(2)}) collective-permute-start(bf16[1152,512]{1,0:T(8,128)(2,1)S(1)} %constant_dynamic-update-slice_fusion), channel_id=1, source_target_pairs={{0,1},{1,2},{2,3},{3,0},{4,5},{5,6},{6,7},{7,4},{8,9},{9,10},{10,1... | collective-permute-start | bytes 3538952 | tf_op jit(solution)/shard_map/ppermute | solution.py:328
  139.2 14.9 %collective-permute-start.19 = (bf16[576,512]{1,0:T(8,128)(2,1)S(1)}, bf16[576,512]{1,0:T(8,128)(2,1)S(1)}, u32[]{:S(2)}, u32[]{:S(2)}) collective-permute-start(bf16[576,512]{1,0:T(8,128)(2,1)S(1)} %slice.81), channel_id=1, source_target_pairs={{1,0},{2,1},{3,2},{0,3},{5,4},{6,5},{7,6},{4,7},{9,8},{10,9},{11,1... | collective-permute-start | bytes 1769480 | tf_op jit(solution)/shard_map/ppermute | solution.py:331
  142.1 7.2 %slice-start = ((s8[6291456]{0:T(1024)(128)(4,1)}), s8[4194304]{0:T(1024)(128)(4,1)S(1)}, s32[]{:S(2)}) async-start(s8[6291456]{0:T(1024)(128)(4,1)} %bitcast.69), calls=%async_computation.3 | async-start | bytes 8388608
  145.3 4.1 %slice-start.1 = ((s8[6291456]{0:T(1024)(128)(4,1)}), s8[2097152]{0:T(1024)(128)(4,1)S(1)}, s32[]{:S(2)}) async-start(s8[6291456]{0:T(1024)(128)(4,1)} %bitcast.69), calls=%async_computation.4 | async-start | bytes 4194304
  149.3 15.2 %collective-permute-start.18 = (bf16[576,512]{1,0:T(8,128)(2,1)S(1)}, bf16[576,512]{1,0:T(8,128)(2,1)S(1)}, u32[]{:S(2)}, u32[]{:S(2)}) collective-permute-start(bf16[576,512]{1,0:T(8,128)(2,1)S(1)} %slice.79), channel_id=1, source_target_pairs={{0,1},{1,2},{2,3},{3,0},{4,5},{5,6},{6,7},{7,4},{8,9},{9,10},{10,1... | collective-permute-start | bytes 1769480 | tf_op jit(solution)/shard_map/ppermute | solution.py:330
  154.9 10.5 %copy-start.7 = (bf16[576,1024]{1,0:T(8,128)(2,1)}, bf16[576,1024]{1,0:T(8,128)(2,1)S(1)}, u32[]{:S(2)}) copy-start(bf16[576,1024]{1,0:T(8,128)(2,1)S(1)} %fusion) | copy-start | bytes 3538948
  169.0 55.3 %all-to-all-start = ((bf16[8,4,2,128,256]{4,3,2,1,0:T(8,128)(2,1)}), bf16[8,4,2,128,256]{4,3,2,1,0:T(8,128)(2,1)}, u32[]{:S(2)}, u32[]{:S(2)}) async-start(bf16[8,4,2,128,256]{4,3,2,1,0:T(8,128)(2,1)} %bitcast.72), calls=%async_computation | async-start | bytes 8388608 | tf_op jit(solution)/shard_map/all_to_all | solution.py:366
  175.4 3.8 %copy-start.5 = (bf16[512,1024]{1,0:T(8,128)(2,1)S(1)}, bf16[512,1024]{1,0:T(8,128)(2,1)}, u32[]{:S(2)}) copy-start(bf16[512,1024]{1,0:T(8,128)(2,1)} %copy-done.4) | copy-start | bytes 3145732
  175.4 3.8 %copy-start.10 = (bf16[128,1024]{1,0:T(8,128)(2,1)S(1)}, bf16[128,1024]{1,0:T(8,128)(2,1)}, u32[]{:S(2)}) copy-start(bf16[128,1024]{1,0:T(8,128)(2,1)} %copy-done.9) | copy-start | bytes 786436
  179.1 51.6 %collective-permute-start.20 = (bf16[16,128,256]{2,1,0:T(8,128)(2,1)}, bf16[16,128,256]{2,1,0:T(8,128)(2,1)S(1)}, u32[]{:S(2)}, u32[]{:S(2)}) collective-permute-start(bf16[16,128,256]{2,1,0:T(8,128)(2,1)} %bitcast.19), channel_id=1, source_target_pairs={{0,8},{4,12},{8,16},{12,20},{16,24},{20,28},{24,32},{28,36},{32,40... | collective-permute-start | bytes 3145736 | tf_op jit(solution)/shard_map/ppermute | solution.py:377
  191.0 1.3 copy-start.1
  192.3 40.2 %copy-start.11 = (s32[1,2048]{1,0:T(1,128)S(1)}, s32[1,2048]{1,0:T(1,128)}, u32[]{:S(2)}) copy-start(s32[1,2048]{1,0:T(1,128)} %param.7) | copy-start | bytes 24580
  192.3 40.5 %collective-permute-start.21 = (bf16[16,128,256]{2,1,0:T(8,128)(2,1)}, bf16[16,128,256]{2,1,0:T(8,128)(2,1)S(1)}, u32[]{:S(2)}, u32[]{:S(2)}) collective-permute-start(bf16[16,128,256]{2,1,0:T(8,128)(2,1)} %bitcast.20), channel_id=1, source_target_pairs={{0,56},{4,60},{8,0},{12,4},{16,8},{20,12},{24,16},{28,20},{32,24},... | collective-permute-start | bytes 3145736 | tf_op jit(solution)/shard_map/ppermute | solution.py:377
  195.0 51.6 %collective-permute-start.22 = (bf16[16,128,256]{2,1,0:T(8,128)(2,1)}, bf16[16,128,256]{2,1,0:T(8,128)(2,1)}, u32[]{:S(2)}, u32[]{:S(2)}) collective-permute-start(bf16[16,128,256]{2,1,0:T(8,128)(2,1)} %bitcast.21), channel_id=1, source_target_pairs={{0,16},{4,52},{8,24},{12,60},{16,32},{20,4},{24,40},{28,12},{32,48... | collective-permute-start | bytes 3145736 | tf_op jit(solution)/shard_map/ppermute | solution.py:377
  228.0 25.6 %collective-permute-start.23 = (bf16[16,128,256]{2,1,0:T(8,128)(2,1)}, bf16[16,128,256]{2,1,0:T(8,128)(2,1)}, u32[]{:S(2)}, u32[]{:S(2)}) collective-permute-start(bf16[16,128,256]{2,1,0:T(8,128)(2,1)} %bitcast.22), channel_id=1, source_target_pairs={{0,8},{4,12},{8,16},{12,20},{16,24},{20,28},{24,32},{28,36},{32,40... | collective-permute-start | bytes 3145736 | tf_op jit(solution)/shard_map/ppermute | solution.py:377
  228.0 37.0 %collective-permute-start.24 = (bf16[16,128,256]{2,1,0:T(8,128)(2,1)}, bf16[16,128,256]{2,1,0:T(8,128)(2,1)}, u32[]{:S(2)}, u32[]{:S(2)}) collective-permute-start(bf16[16,128,256]{2,1,0:T(8,128)(2,1)} %bitcast.23), channel_id=1, source_target_pairs={{0,56},{4,60},{8,0},{12,4},{16,8},{20,12},{24,16},{28,20},{32,24},... | collective-permute-start | bytes 3145736 | tf_op jit(solution)/shard_map/ppermute | solution.py:377
  230.6 55.1 %collective-permute-start.25 = (bf16[16,128,256]{2,1,0:T(8,128)(2,1)}, bf16[16,128,256]{2,1,0:T(8,128)(2,1)}, u32[]{:S(2)}, u32[]{:S(2)}) collective-permute-start(bf16[16,128,256]{2,1,0:T(8,128)(2,1)} %bitcast.24), channel_id=1, source_target_pairs={{0,16},{4,52},{8,24},{12,60},{16,32},{20,4},{24,40},{28,12},{32,48... | collective-permute-start | bytes 3145736 | tf_op jit(solution)/shard_map/ppermute | solution.py:377
  298.4 60.1 %all-to-all-start.2 = ((bf16[64,128,128]{2,1,0:T(8,128)(2,1)}), bf16[64,128,128]{2,1,0:T(8,128)(2,1)S(1)}, u32[]{:S(2)}, u32[]{:S(2)}) async-start(bf16[64,128,128]{2,1,0:T(8,128)(2,1)} %rand_attend.1), calls=%async_computation.2 | async-start | bytes 4194304 | tf_op jit(solution)/shard_map/all_to_all | solution.py:404
